TPU v7x, 32 devices: a whole 2x2x4 slice. The times are simulated.
32 devices in a mesh: shard: 2 (over y), ctx: 4 (over x, core), tp: 4 (over z).
Axes of the slice: x: 2, y: 2, z: 4, core: 2. Of those that a mesh axis runs over, the one named last changes fastest.
Arguments:
- layer_input: bfloat16 [12, 1024, 768], P('shard', 'ctx'), may hold values from -6 to 6
- segment_ids: int32 [12, 1024], P('shard'), may hold values from 0 to 15, never falling along the last dimension, each value on 1 to 512 neighbouring positions
- query_proj: bfloat16 [768, 768], P('shard', 'tp'), may hold values from -0.21875 to 0.21875
- query_bias: bfloat16 [768], P('tp'), may hold values from -4 to 4
- key_proj: bfloat16 [768, 768], P('shard', 'tp'), may hold values from -0.21875 to 0.21875
- value_proj: bfloat16 [768, 768], P('shard', 'tp'), may hold values from -0.21875 to 0.21875
- value_bias: bfloat16 [768], P('tp'), may hold values from -3 to 3
- out_proj: bfloat16 [768, 768], P('tp', 'shard'), may hold values from -1.5 to 1.5
- out_bias: bfloat16 [768], replicated, may hold values from -3 to 3
- attn_gain: bfloat16 [768], replicated, may hold values from 0.099609375 to 1.8984375
- attn_shift: bfloat16 [768], replicated, may hold values from -3 to 3
- up_proj: bfloat16 [768, 3072], P('shard', 'tp'), may hold values from -0.21875 to 0.21875
- up_bias: bfloat16 [3072], P('tp'), may hold values from -3 to 3
- down_proj: bfloat16 [3072, 768], P('tp', 'shard'), may hold values from -0.109375 to 0.109375
- down_bias: bfloat16 [768], replicated, may hold values from -3 to 3
- ffn_gain: bfloat16 [768], replicated, may hold values from 0.099609375 to 1.8984375
- ffn_shift: bfloat16 [768], replicated, may hold values from -3 to 3
- out_cotangent: bfloat16 [12, 1024, 768], P('shard', 'ctx'), may hold values from -6 to 6
Outputs:
- layer_output: bfloat16 [12, 1024, 768], P('shard', 'ctx')
- input_grad: float32 [12, 1024, 768], P('shard', 'ctx')
- query_proj_grad: float32 [768, 768], P('shard', 'tp')
- query_bias_grad: float32 [768], P('tp')
- key_proj_grad: float32 [768, 768], P('shard', 'tp')
- value_proj_grad: float32 [768, 768], P('shard', 'tp')
- value_bias_grad: float32 [768], P('tp')
- out_proj_grad: float32 [768, 768], P('tp', 'shard')
- out_bias_grad: float32 [768], replicated
- attn_gain_grad: float32 [768], replicated
- attn_shift_grad: float32 [768], replicated
- up_proj_grad: float32 [768, 3072], P('shard', 'tp')
- up_bias_grad: float32 [3072], P('tp')
- down_proj_grad: float32 [3072, 768], P('tp', 'shard')
- down_bias_grad: float32 [768], replicated
- ffn_gain_grad: float32 [768], replicated
- ffn_shift_grad: float32 [768], replicated
Inputs may be any that keep to these rules, and one draw needn't show every extreme that they name: `segment_ids`: within a sequence the ids never fall; each of the 16 documents has 1 to 512 tokens, and one has exactly 512.
All inputs are finite; a program needn't handle non-finite values.
Results may differ from a plain program's by a relative error of at most 0.04.
Values may be sent and summed in bfloat16 or wider, within the bound.
No kernel may reach another device: no remote copies, remote signals or barrier semaphores. Data moves between devices by JAX's collectives and lax.ppermute only.
A program may use at most 192 MiB of HBM per device.

v0:
```python
from functools import partial
import math

import jax
import jax.numpy as jnp
from jax import lax
from jax.sharding import PartitionSpec as P

HEAD_DIM = 64


eps_norm = 1e-12
far_below = -1e30


def contract_rows(left, right):
    return lax.dot_general(
        left, right, (((0,), (0,)), ((), ())), preferred_element_type=jnp.float32
    )


def contract_last(left, right):
    return lax.dot_general(
        left, right, (((1,), (1,)), ((), ())), preferred_element_type=jnp.float32
    )


def norm_forward(resid, norm_gain, norm_shift):
    center = resid - jnp.mean(resid, axis=-1, keepdims=True)
    inv_std = lax.rsqrt(jnp.mean(center * center, axis=-1, keepdims=True) + eps_norm)
    normed = center * inv_std
    return (normed * norm_gain + norm_shift, normed, inv_std)


def norm_backward(grad_out, normed, inv_std, norm_gain):
    grad_normed = grad_out * norm_gain
    grad_in = inv_std * (
        grad_normed
        - jnp.mean(grad_normed, axis=-1, keepdims=True)
        - normed * jnp.mean(grad_normed * normed, axis=-1, keepdims=True)
    )
    return (grad_in, jnp.sum(grad_out * normed, axis=0), jnp.sum(grad_out, axis=0))


def split_heads(matrix):
    return matrix.reshape(matrix.shape[0], matrix.shape[1] // HEAD_DIM, HEAD_DIM)


def scores_of(queries, keys_all, query_docs, key_docs):
    scores = jnp.einsum(
        "qhd,khd->hqk",
        split_heads(queries),
        split_heads(keys_all),
        preferred_element_type=jnp.float32,
    )
    same_doc = (query_docs[:, None] == key_docs[None, :])[None]
    return jnp.where(same_doc, scores, jnp.float32(far_below))


def attend_forward(item):
    queries, keys_all, values_all, query_docs, key_docs = item
    scores = scores_of(queries, keys_all, query_docs, key_docs)
    top_score = jnp.max(scores, axis=-1, keepdims=True)
    expo = jnp.exp(scores - top_score)
    total = jnp.sum(expo, axis=-1, keepdims=True)
    probs = (expo / total).astype(jnp.bfloat16)
    mixed = jnp.einsum(
        "hqk,khd->qhd", probs, split_heads(values_all), preferred_element_type=jnp.float32
    )
    return (
        mixed.reshape(queries.shape).astype(jnp.bfloat16),
        (top_score + jnp.log(total))[:, :, 0],
    )


def score_grads(queries, keys_all, values_all, query_docs, key_docs, grad_mixed, log_total):
    scores = scores_of(queries, keys_all, query_docs, key_docs)
    probs = jnp.exp(scores - log_total[:, :, None])
    grad_probs = jnp.einsum(
        "qhd,khd->hqk",
        split_heads(grad_mixed),
        split_heads(values_all),
        preferred_element_type=jnp.float32,
    )
    inner = jnp.sum(grad_probs * probs, axis=-1)
    grad_scores = (probs * (grad_probs - inner[:, :, None])).astype(jnp.bfloat16)
    return (probs, grad_scores, inner)


def attend_backward(item):
    queries, keys_all, values_all, query_docs, key_docs, grad_mixed, log_total = item
    probs, grad_scores, inner = score_grads(
        queries, keys_all, values_all, query_docs, key_docs, grad_mixed, log_total
    )
    grad_heads = split_heads(grad_mixed)
    grad_queries = jnp.einsum(
        "hqk,khd->qhd", grad_scores, split_heads(keys_all), preferred_element_type=jnp.float32
    )
    grad_keys = jnp.einsum(
        "hqk,qhd->khd", grad_scores, split_heads(queries), preferred_element_type=jnp.float32
    )
    grad_values = jnp.einsum(
        "hqk,qhd->khd", probs.astype(jnp.bfloat16), grad_heads, preferred_element_type=jnp.float32
    )
    return (
        grad_queries.reshape(queries.shape).astype(jnp.bfloat16),
        grad_keys.reshape(keys_all.shape),
        grad_values.reshape(values_all.shape),
    )


def shards(
    layer_input,
    segment_ids,
    query_proj,
    query_bias,
    key_proj,
    value_proj,
    value_bias,
    out_proj,
    out_bias,
    attn_gain,
    attn_shift,
    up_proj,
    up_bias,
    down_proj,
    down_bias,
    ffn_gain,
    ffn_shift,
    out_cotangent,
):
    seq_here, ctx_rows, width = layer_input.shape
    scale = 1.0 / math.sqrt(HEAD_DIM)
    full_query, full_key, full_value, full_out, full_up, full_down = (
        lax.all_gather(query_proj, "shard", axis=0, tiled=True),
        lax.all_gather(key_proj, "shard", axis=0, tiled=True),
        lax.all_gather(value_proj, "shard", axis=0, tiled=True),
        lax.all_gather(out_proj, "shard", axis=1, tiled=True),
        lax.all_gather(up_proj, "shard", axis=0, tiled=True),
        lax.all_gather(down_proj, "shard", axis=1, tiled=True),
    )
    local_width = full_query.shape[1]
    joined_proj = jnp.concatenate([full_query, full_key, full_value], axis=1)
    rows_in = layer_input.reshape(seq_here * ctx_rows, width)
    projected = jnp.dot(rows_in, joined_proj, preferred_element_type=jnp.float32)
    shaped = (seq_here, ctx_rows, local_width)
    queries = (
        ((projected[:, :local_width] + query_bias) * scale).astype(jnp.bfloat16).reshape(shaped)
    )
    keys_mine = projected[:, local_width : 2 * local_width].astype(jnp.bfloat16).reshape(shaped)
    values_mine = (
        (projected[:, 2 * local_width :] + value_bias).astype(jnp.bfloat16).reshape(shaped)
    )
    keys_all, values_all = (
        lax.all_gather(keys_mine, "ctx", axis=1, tiled=True),
        lax.all_gather(values_mine, "ctx", axis=1, tiled=True),
    )
    query_docs = lax.dynamic_slice_in_dim(
        segment_ids, lax.axis_index("ctx") * ctx_rows, ctx_rows, 1
    )
    mixed, log_total = lax.map(
        attend_forward, (queries, keys_all, values_all, query_docs, segment_ids)
    )
    mixed_rows = mixed.reshape(-1, local_width)
    attended = (
        lax.psum(
            jnp.dot(mixed_rows, full_out, preferred_element_type=jnp.float32).astype(jnp.bfloat16),
            "tp",
        ).astype(jnp.float32)
        + out_bias
    )
    hidden, normed_one, inv_one = norm_forward(
        rows_in.astype(jnp.float32) + attended, attn_gain, attn_shift
    )
    hidden_low = hidden.astype(jnp.bfloat16)
    pre_act = jnp.dot(hidden_low, full_up, preferred_element_type=jnp.float32) + up_bias
    acts_low = jax.nn.gelu(pre_act, approximate=False).astype(jnp.bfloat16)
    ffn_out = (
        lax.psum(
            jnp.dot(acts_low, full_down, preferred_element_type=jnp.float32).astype(jnp.bfloat16),
            "tp",
        ).astype(jnp.float32)
        + down_bias
    )
    output_rows, normed_two, inv_two = norm_forward(hidden + ffn_out, ffn_gain, ffn_shift)
    layer_output = output_rows.astype(jnp.bfloat16).reshape(layer_input.shape)
    grad_out = out_cotangent.reshape(-1, width).astype(jnp.float32)
    grad_two, ffn_gain_grad, ffn_shift_grad = norm_backward(grad_out, normed_two, inv_two, ffn_gain)
    grad_ffn = grad_two.astype(jnp.bfloat16)
    down_bias_grad = jnp.sum(grad_ffn, axis=0, dtype=jnp.float32)
    down_part = contract_rows(acts_low, grad_ffn)
    grad_acts = contract_last(grad_ffn, full_down)
    _, gelu_back = jax.vjp(partial(jax.nn.gelu, approximate=False), pre_act)
    grad_pre = gelu_back(grad_acts)[0].astype(jnp.bfloat16)
    up_bias_grad = jnp.sum(grad_pre, axis=0, dtype=jnp.float32)
    up_part = contract_rows(hidden_low, grad_pre)
    grad_hidden = grad_two + lax.psum(
        contract_last(grad_pre, full_up).astype(jnp.bfloat16), "tp"
    ).astype(jnp.float32)
    grad_one, attn_gain_grad, attn_shift_grad = norm_backward(
        grad_hidden, normed_one, inv_one, attn_gain
    )
    grad_attn = grad_one.astype(jnp.bfloat16)
    out_bias_grad = jnp.sum(grad_attn, axis=0, dtype=jnp.float32)
    out_part = contract_rows(mixed_rows, grad_attn)
    grad_mixed = contract_last(grad_attn, full_out).astype(jnp.bfloat16).reshape(shaped)
    keys_back, values_back = (
        lax.all_gather(keys_mine, "ctx", axis=1, tiled=True),
        lax.all_gather(values_mine, "ctx", axis=1, tiled=True),
    )
    grad_queries, grad_keys_all, grad_values_all = lax.map(
        attend_backward,
        (queries, keys_back, values_back, query_docs, segment_ids, grad_mixed, log_total),
    )
    grad_keys, grad_values = (
        lax.psum_scatter(
            grad_keys_all.astype(jnp.bfloat16), "ctx", scatter_dimension=1, tiled=True
        ).astype(jnp.float32),
        lax.psum_scatter(
            grad_values_all.astype(jnp.bfloat16), "ctx", scatter_dimension=1, tiled=True
        ).astype(jnp.float32),
    )
    grad_keys = grad_keys.astype(jnp.bfloat16).reshape(-1, local_width)
    grad_values = grad_values.astype(jnp.bfloat16).reshape(-1, local_width)
    grad_scaled = grad_queries.reshape(-1, local_width) * jnp.bfloat16(scale)
    grad_joined = jnp.concatenate([grad_scaled, grad_keys, grad_values], axis=1)
    joined_part = contract_rows(rows_in, grad_joined)
    query_part = joined_part[:, :local_width]
    key_part = joined_part[:, local_width : 2 * local_width]
    value_part = joined_part[:, 2 * local_width :]
    query_bias_grad = jnp.sum(grad_scaled, axis=0, dtype=jnp.float32)
    value_bias_grad = jnp.sum(grad_values, axis=0, dtype=jnp.float32)
    back_terms = contract_last(grad_joined, joined_proj)
    input_grad = (
        grad_one + lax.psum(back_terms.astype(jnp.bfloat16), "tp").astype(jnp.float32)
    ).reshape(layer_input.shape)
    sliced = (
        lax.psum_scatter(
            query_part.astype(jnp.bfloat16), "shard", scatter_dimension=0, tiled=True
        ).astype(jnp.float32),
        lax.psum_scatter(
            key_part.astype(jnp.bfloat16), "shard", scatter_dimension=0, tiled=True
        ).astype(jnp.float32),
        lax.psum_scatter(
            value_part.astype(jnp.bfloat16), "shard", scatter_dimension=0, tiled=True
        ).astype(jnp.float32),
        lax.psum_scatter(
            out_part.astype(jnp.bfloat16), "shard", scatter_dimension=1, tiled=True
        ).astype(jnp.float32),
        lax.psum_scatter(
            up_part.astype(jnp.bfloat16), "shard", scatter_dimension=0, tiled=True
        ).astype(jnp.float32),
        lax.psum_scatter(
            down_part.astype(jnp.bfloat16), "shard", scatter_dimension=1, tiled=True
        ).astype(jnp.float32),
    )
    reduced = (
        lax.psum(sliced[0].astype(jnp.bfloat16), "ctx").astype(jnp.float32),
        lax.psum(sliced[1].astype(jnp.bfloat16), "ctx").astype(jnp.float32),
        lax.psum(sliced[2].astype(jnp.bfloat16), "ctx").astype(jnp.float32),
        lax.psum(sliced[3].astype(jnp.bfloat16), "ctx").astype(jnp.float32),
        lax.psum(sliced[4].astype(jnp.bfloat16), "ctx").astype(jnp.float32),
        lax.psum(sliced[5].astype(jnp.bfloat16), "ctx").astype(jnp.float32),
    )
    small = lax.psum(
        (
            query_bias_grad,
            value_bias_grad,
            out_bias_grad,
            attn_gain_grad,
            attn_shift_grad,
            up_bias_grad,
            down_bias_grad,
            ffn_gain_grad,
            ffn_shift_grad,
        ),
        ("shard", "ctx"),
    )
    return (
        layer_output,
        input_grad,
        reduced[0],
        small[0],
        reduced[1],
        reduced[2],
        small[1],
        reduced[3],
        small[2],
        small[3],
        small[4],
        reduced[4],
        small[5],
        reduced[5],
        small[6],
        small[7],
        small[8],
    )


def solution(mesh):
    return jax.shard_map(
        shards,
        mesh=mesh,
        in_specs=(
            P("shard", "ctx", None),
            P("shard", None),
            P("shard", "tp"),
            P("tp"),
            P("shard", "tp"),
            P("shard", "tp"),
            P("tp"),
            P("tp", "shard"),
            P(),
            P(),
            P(),
            P("shard", "tp"),
            P("tp"),
            P("tp", "shard"),
            P(),
            P(),
            P(),
            P("shard", "ctx", None),
        ),
        out_specs=(
            P("shard", "ctx", None),
            P("shard", "ctx", None),
            P("shard", "tp"),
            P("tp"),
            P("shard", "tp"),
            P("shard", "tp"),
            P("tp"),
            P("tp", "shard"),
            P(),
            P(),
            P(),
            P("shard", "tp"),
            P("tp"),
            P("tp", "shard"),
            P(),
            P(),
            P(),
        ),
        check_vma=False,
    )
```

profile of v0, /device:TPU:1, one launch (start us, length us, event | category | flops | bytes accessed | tf_op | source)
XLA Modules:
  0.0 896.6 jit_solution(13864041985692882012)
XLA Ops:
  8.1 6.6 all_gather.26
  14.7 4.9 all_gather.27
  19.5 4.9 all_gather.28
  38.4 4.9 all_gather.31
  43.9 22.9 %all-gather.5.cloned.1.call-done = bf16[6,1024,192]{1,0,2:T(8,128)(2,1)} async-done(((bf16[6,256,192]{1,0,2:T(8,128)(2,1)}), bf16[6,1024,192]{1,0,2:T(8,128)(2,1)}) %all-gather.5.cloned.1.call-update) | async-done | bytes 2359312 | tf_op jit(solution)/shard_map/all_gather | solution.py:156
  66.8 4.6 copy.51
  71.4 26.5 %all-gather.7.cloned.1.call-done = bf16[6,1024,192]{1,0,2:T(8,128)(2,1)} async-done(((bf16[6,256,192]{1,0,2:T(8,128)(2,1)}), bf16[6,1024,192]{1,0,2:T(8,128)(2,1)}) %all-gather.7.cloned.1.call-update) | async-done | bytes 2359312 | tf_op jit(solution)/shard_map/all_gather | solution.py:155
  97.9 4.6 copy.53
  102.5 38.2 %while.26 = (s32[]{:T(128)}, bf16[6,256,192]{1,2,0:T(8,128)(2,1)S(1)}, f32[6,3,256]{2,1,0:T(4,128)}, bf16[6,1024,192]{1,2,0:T(8,128)(2,1)}, s32[6,256]{1,0:T(8,1...) while((s32[]{:T(128)}, ...), condition=%wide.region_3.4_spmd, body=%wide.region_0.3_spmd.sunk | while | flops 208715008 | bytes 13476465 | solution.py:161
  146.6 93.8 %all-reduce.8.cloned.1.call-done = bf16[1536,768]{1,0:T(8,128)(2,1)} async-done(((bf16[1536,768]{1,0:T(8,128)(2,1)}), bf16[1536,768]{1,0:T(8,128)(2,1)}) %all-reduce.8.cloned.1.call-update) | async-done | bytes 2359312 | tf_op jit(solution)/shard_map/psum | solution.py:166
  247.3 15.3 %multiply_convert_fusion.1 = (bf16[1536,768]{1,0:T(8,128)(2,1)}, f32[1536,768]{1,0:T(8,128)}, f32[1536,768]{1,0:T(8,128)}) fusion(f32[768]{0:T(1024)S(1)} %convert_element_type.215, bf16[768,768]{1,0:T(8,128)(2,1)} %all-gather.9.cloned.1.call-done, f32[1536,768]{1,0:T(8,128)} %subtract_multiply_fusion.2, f32[768]{0:T(1024)S(1)} %convert_element_type.213, ...), kind=kOutput, calls=%fused_computation.61 | convolution fusion | flops 1893335040 | bytes 17703936 | tf_op jit(solution)/shard_map/dot_general | solution.py:176
  262.6 5.5 convolution_convert_fusion.3
  270.4 92.6 %all-reduce.10.cloned.1.call-done = bf16[1536,768]{1,0:T(8,128)(2,1)} async-done(((bf16[1536,768]{1,0:T(8,128)(2,1)}), bf16[1536,768]{1,0:T(8,128)(2,1)}) %all-reduce.10.cloned.1.call-update) | async-done | bytes 2359312 | tf_op jit(solution)/shard_map/psum | solution.py:179
  382.6 94.6 %all-reduce.12.cloned.1.call-done = bf16[1536,768]{1,0:T(8,128)(2,1)} async-done(((bf16[1536,768]{1,0:T(8,128)(2,1)}), bf16[1536,768]{1,0:T(8,128)(2,1)}) %all-reduce.12.cloned.1.call-update) | async-done | bytes 2359312 | tf_op jit(solution)/shard_map/psum | solution.py:197
  477.2 7.5 multiply_reduce_fusion.1
  484.6 5.2 convert_reduce_fusion.3
  493.0 61.6 %while.27 = (s32[]{:T(128)}, bf16[6,256,192]{1,2,0:T(8,128)(2,1)S(1)}, bf16[6,1024,192]{1,2,0:T(8,128)(2,1)}, bf16[6,1024,192]{1,2,0:T(8,128)(2,1)}, bf16[6,1024...) while((s32[]{:T(128)}, ...), condition=%wide.region_17.18_spmd, body=%wide.region_15.17_spmd.sunk | while | flops 513064192 | bytes 30872212 | solution.py:211
  555.4 5.1 convolution_convert_fusion.6
  570.9 16.1 %reduce-scatter.19.cloned.1.call-done = bf16[6,256,192]{1,2,0:T(8,128)(2,1)} async-done(((bf16[6,1024,192]{1,2,0:T(8,128)(2,1)}), bf16[6,256,192]{1,2,0:T(8,128)(2,1)}) %reduce-scatter.19.cloned.1.call-update) | async-done | bytes 589840 | tf_op jit(solution)/shard_map/reduce_scatter | solution.py:216
  588.1 34.7 %reduce-scatter.21.cloned.1.call-done = bf16[6,256,192]{1,2,0:T(8,128)(2,1)} async-done(((bf16[6,1024,192]{1,2,0:T(8,128)(2,1)}), bf16[6,256,192]{1,2,0:T(8,128)(2,1)}) %reduce-scatter.21.cloned.1.call-update) | async-done | bytes 589840 | tf_op jit(solution)/shard_map/reduce_scatter | solution.py:219
  632.0 6.2 convolution_convert_fusion.7
  638.3 9.1 %reduce-scatter.33.cloned.1.call-done = bf16[384,768]{1,0:T(8,128)(2,1)} async-done(((bf16[768,768]{1,0:T(8,128)(2,1)}), bf16[384,768]{1,0:T(8,128)(2,1)}) %reduce-scatter.33.cloned.1.call-update) | async-done | bytes 589840
  649.5 13.4 %reduce-scatter.31.cloned.1.call-done = bf16[384,192]{1,0:T(8,128)(2,1)} async-done(((bf16[768,192]{1,0:T(8,128)(2,1)}), bf16[384,192]{1,0:T(8,128)(2,1)}) %reduce-scatter.31.cloned.1.call-update) | async-done | bytes 147472
  664.6 13.5 %reduce-scatter.25.cloned.1.call-done = bf16[384,192]{1,0:T(8,128)(2,1)} async-done(((bf16[768,192]{1,0:T(8,128)(2,1)}), bf16[384,192]{1,0:T(8,128)(2,1)}) %reduce-scatter.25.cloned.1.call-update) | async-done | bytes 147472
  679.8 13.8 %reduce-scatter.27.cloned.1.call-done = bf16[384,192]{1,0:T(8,128)(2,1)} async-done(((bf16[768,192]{1,0:T(8,128)(2,1)}), bf16[384,192]{1,0:T(8,128)(2,1)}) %reduce-scatter.27.cloned.1.call-update) | async-done | bytes 147472
  695.3 13.5 %reduce-scatter.29.cloned.1.call-done = bf16[384,192]{1,0:T(8,128)(2,1)} async-done(((bf16[768,192]{1,0:T(8,128)(2,1)}), bf16[384,192]{1,0:T(8,128)(2,1)}) %reduce-scatter.29.cloned.1.call-update) | async-done | bytes 147472
  710.5 23.0 %reduce-scatter.23.cloned.1.call-done = bf16[384,768]{1,0:T(8,128)(2,1)} async-done(((bf16[768,768]{1,0:T(8,128)(2,1)}), bf16[384,768]{1,0:T(8,128)(2,1)}) %reduce-scatter.23.cloned.1.call-update) | async-done | bytes 589840 | tf_op jit(solution)/shard_map/reduce_scatter | solution.py:250
  733.7 4.8 convolution_convert_fusion.1
  738.9 22.0 %all-reduce = (f32[192]{0:T(256)}, f32[192]{0:T(256)}, f32[768]{0:T(1024)}, f32[768]{0:T(1024)}, f32[768]{0:T(1024)}, /*index=5*/f32[768]{0:T(1024)}, f32[768]{0:T(1024)}, f32[768]{0:T(1024)}, f32[768]{0:T(1024)}) all-reduce(f32[192]{0:T(256)S(1)} %convert_reduce_fusion.5, ...), channel_id=1, replica_groups=mesh['shard'=2,'ctx'=4,'tp'=4] {'shard','ctx'}, use_global_device_ids=true, to_apply=%region_24.25 | all-reduce | flops 5760 | bytes 46080 | tf_op jit(solution)/shard_map/psum | solution.py:265
  760.9 23.6 %all-reduce.16.cloned.1.call-done = (bf16[384,192]{0,1:T(8,128)(2,1)}, bf16[384,192]{0,1:T(8,128)(2,1)}, bf16[384,192]{0,1:T(8,128)(2,1)}, bf16[192,384]{1,0:T(8...) async-done(((bf16[384,192]{0,1:T(8,128)(2,1)}, bf16[384,192]{0,1:T(8,128)(2,1)}, bf16[384,192]{0,1:T(8,128)(2,1)}, bf16[192,384]{1,0:T(8,128)(2,1)}, ...) | async-done | bytes 1769488 | tf_op jit(solution)/shard_map/psum | solution.py:258
  794.5 89.0 %all-reduce.14.cloned.1.call-done = bf16[1536,768]{1,0:T(8,128)(2,1)} async-done(((bf16[1536,768]{1,0:T(8,128)(2,1)}), bf16[1536,768]{1,0:T(8,128)(2,1)}) %all-reduce.14.cloned.1.call-update) | async-done | bytes 2359312 | tf_op jit(solution)/shard_map/psum | solution.py:235
  883.5 5.7 convert_add_fusion
  (336 shorter events, 191.9 us)
Async XLA Ops:
  8.0 58.8 %all-gather.5.cloned.1.call-start = ((), (), s32[]{:S(2)}) async-start(), calls=%async_computation.8 | async-start | bytes 3932160 | tf_op jit(solution)/shard_map/all_gather | solution.py:156
  33.0 64.9 %all-gather.7.cloned.1.call-start = ((), (), s32[]{:S(2)}) async-start(), calls=%async_computation.9 | async-start | bytes 3932160 | tf_op jit(solution)/shard_map/all_gather | solution.py:155
  36.3 204.1 %all-reduce.8.cloned.1.call-start = ((), (), s32[]{:S(2)}) async-start(), calls=%async_computation.10 | async-start | bytes 4718592 | tf_op jit(solution)/shard_map/psum | solution.py:166
  140.8 5.8 copy-start.20
  140.8 5.8 copy-start.21
  140.8 5.8 copy-start.22
  140.8 5.8 copy-start.23
  140.8 99.6 %copy-start.3 = (bf16[6,256,768]{2,1,0:T(8,128)(2,1)S(1)}, bf16[6,256,768]{2,1,0:T(8,128)(2,1)}, u32[]{:S(2)}) copy-start(bf16[6,256,768]{2,1,0:T(8,128)(2,1)} %param.22) | copy-start | bytes 7077892
  145.1 102.2 %all-gather.9.cloned.1.call-start = ((), (), s32[]{:S(2)}) async-start(), calls=%async_computation.11 | async-start | bytes 1769472 | tf_op jit(solution)/shard_map/all_gather | solution.py:139
  145.7 116.9 %all-gather.11.cloned.1.call-start = ((), (), s32[]{:S(2)}) async-start(), calls=%async_computation.12 | async-start | bytes 1769472 | tf_op jit(solution)/shard_map/all_gather | solution.py:140
  146.3 216.7 %all-reduce.10.cloned.1.call-start = ((), (), s32[]{:S(2)}) async-start(), calls=%async_computation.13 | async-start | bytes 4718592 | tf_op jit(solution)/shard_map/psum | solution.py:179
  146.6 216.4 %copy-start.16 = (f32[768]{0:T(1024)}, f32[768]{0:T(1024)S(1)}, u32[]{:S(2)}) copy-start(f32[768]{0:T(1024)S(1)} %convert_element_type.213) | copy-start | bytes 9220
  262.6 6.1 copy-start.24
  262.6 6.1 copy-start.25
  262.6 6.1 copy-start.2
  268.2 209.0 %all-reduce.12.cloned.1.call-start = ((), (), s32[]{:S(2)}) async-start(), calls=%async_computation.14 | async-start | bytes 4718592 | tf_op jit(solution)/shard_map/psum | solution.py:197
  367.8 5.4 slice-start
  373.2 5.6 copy-start.27
  382.4 204.6 %reduce-scatter.19.cloned.1.call-start = ((), (), s32[]{:S(2)}) async-start(), calls=%async_computation.15 | async-start | bytes 2949120 | tf_op jit(solution)/shard_map/reduce_scatter | solution.py:216
  477.2 7.5 copy-start.6
  554.6 68.1 %reduce-scatter.21.cloned.1.call-start = ((), (), s32[]{:S(2)}) async-start(), calls=%async_computation.16 | async-start | bytes 2949120 | tf_op jit(solution)/shard_map/reduce_scatter | solution.py:219
  555.4 92.0 %reduce-scatter.33.cloned.1.call-start = ((), (), s32[]{:S(2)}) async-start(), calls=%async_computation.23 | async-start | bytes 1769472
  562.0 100.8 %reduce-scatter.31.cloned.1.call-start = ((), (), s32[]{:S(2)}) async-start(), calls=%async_computation.22 | async-start | bytes 589824
  566.8 58.8 %copy-start.4 = (bf16[6,256,768]{2,1,0:T(8,128)(2,1)S(1)}, bf16[6,256,768]{2,1,0:T(8,128)(2,1)}, u32[]{:S(2)}) copy-start(bf16[6,256,768]{2,1,0:T(8,128)(2,1)} %param.22) | copy-start | bytes 7077892
  570.8 107.3 %reduce-scatter.25.cloned.1.call-start = ((), (), s32[]{:S(2)}) async-start(), calls=%async_computation.19 | async-start | bytes 589824
  629.7 63.9 %reduce-scatter.27.cloned.1.call-start = ((), (), s32[]{:S(2)}) async-start(), calls=%async_computation.20 | async-start | bytes 589824
  630.7 78.1 %reduce-scatter.29.cloned.1.call-start = ((), (), s32[]{:S(2)}) async-start(), calls=%async_computation.21 | async-start | bytes 589824
  631.8 101.8 %reduce-scatter.23.cloned.1.call-start = ((), (), s32[]{:S(2)}) async-start(), calls=%async_computation.18 | async-start | bytes 1769472 | tf_op jit(solution)/shard_map/reduce_scatter | solution.py:250
  638.2 95.5 %copy-start.9 = (bf16[1536,576]{0,1:T(8,128)(2,1)S(1)}, bf16[1536,576]{0,1:T(8,128)(2,1)}, u32[]{:S(2)}) copy-start(bf16[1536,576]{0,1:T(8,128)(2,1)} %constant_dynamic-update-slice_fusion.7) | copy-start | bytes 5308420
  638.2 146.2 %all-reduce.16.cloned.1.call-start = ((), (), s32[]{:S(2)}) async-start(), calls=%async_computation.24 | async-start | bytes 3538944 | tf_op jit(solution)/shard_map/psum | solution.py:258
  733.6 149.9 %all-reduce.14.cloned.1.call-start = ((), (), s32[]{:S(2)}) async-start(), calls=%async_computation.17 | async-start | bytes 4718592 | tf_op jit(solution)/shard_map/psum | solution.py:235
  784.5 9.3 %copy-start.10 = (bf16[192,384]{1,0:T(8,128)(2,1)S(1)}, bf16[192,384]{1,0:T(8,128)(2,1)}, u32[]{:S(2)}) copy-start(bf16[192,384]{1,0:T(8,128)(2,1)} %get-tuple-element.240) | copy-start | bytes 442372
  (19 other events, 72.1 us)
Sparse Core Ops, SparseCore 0:
  33.1 33.6 all-gather.4
  68.9 28.9 all-gather.6
  145.2 95.1 all-reduce.7
  268.3 94.6 all-reduce.9
  382.5 94.6 all-reduce.11
  554.8 32.1 reduce-scatter.18
  589.6 33.0 reduce-scatter.20
  625.6 21.7 reduce-scatter.32
  649.7 13.1 reduce-scatter.30
  664.9 13.1 reduce-scatter.24
  680.4 13.1 reduce-scatter.26
  695.7 13.1 reduce-scatter.28
  711.7 21.7 reduce-scatter.22
  737.3 47.0 all-reduce.15
  787.4 96.0 all-reduce.13
Sparse Core Ops, SparseCore 1:
  147.1 22.1 all-gather.8
  170.7 22.6 all-gather.10
where the time goes:
time: 908 us; the launch traced here: 897 us
  waiting for transfers between devices  582 us (64%)
  local copies, waits for them, and re-layouts  95.3 us (10%)
  matrix products  91.4 us (10%)
  other arithmetic  66 us (7%)
  blocking collectives  43.2 us (5%)
  between operations  16.3 us (2%)
    psum x1, waiting for transfers between devices, shards(): lax.psum(contract_last(grad_pre, full_up).astype(jnp.bfloat16), 'tp')  94.6 us
    psum x1, waiting for transfers between devices, shards(): lax.psum(jnp.dot(mixed_rows, full_out, preferred_element_type=jnp.float32...  93.8 us
    psum x1, waiting for transfers between devices, shards(): lax.psum(jnp.dot(acts_low, full_down, preferred_element_type=jnp.float32)...  92.6 us
    psum x1, waiting for transfers between devices, shards(): lax.psum(back_terms.astype(jnp.bfloat16), 'tp').astype(jnp.float32)  89 us
    unnamed x22, waiting for transfers between devices  65.3 us
    dynamic_slice x60, local copies, waits for them, and re-layouts, shards(): lax.map(attend_forward, (queries, keys_all, values_all, query_docs, segme...  39.6 us
    reduce_scatter x1, waiting for transfers between devices, shards(): lax.psum_scatter(grad_values_all.astype(jnp.bfloat16), 'ctx', scatter_dim...  34.7 us
    all_gather x1, waiting for transfers between devices, shards(): lax.all_gather(keys_mine, 'ctx', axis=1, tiled=True)  26.5 us
  transfers between devices with their start and end apart: 17, of which 15 were waited for; matrix products, arithmetic and copies ran while one was open for 10% of the time, Pallas kernels for 0%

commit v1 on v0

--- a/solution.py
+++ b/solution.py
@@ -4,6 +4,8 @@
 import jax
 import jax.numpy as jnp
 from jax import lax
+from jax.experimental import pallas as pl
+from jax.experimental.pallas import tpu as pltpu
 from jax.sharding import PartitionSpec as P
 
 HEAD_DIM = 64
@@ -109,7 +111,7 @@
     )
 
 
-def shards(
+def general_shards(
     layer_input,
     segment_ids,
     query_proj,
@@ -297,9 +299,471 @@
     )
 
 
+PAIR = 2 * HEAD_DIM
+QBLOCK = 128
+
+
+def dot32(left, right):
+    return jnp.dot(left, right, preferred_element_type=jnp.float32)
+
+
+def stack_heads(rows):
+    lane = lax.broadcasted_iota(jnp.int32, rows.shape, 1)
+    nought = jnp.zeros_like(rows)
+    return jnp.concatenate(
+        [jnp.where(lane < HEAD_DIM, rows, nought), jnp.where(lane >= HEAD_DIM, rows, nought)], axis=0
+    )
+
+
+def unstack_heads(wide):
+    return jnp.concatenate([wide[:HEAD_DIM, :QBLOCK], wide[HEAD_DIM:, QBLOCK:]], axis=0).T
+
+
+def masked_scores(span, queries, keys, key_docs, query_docs):
+    scores = contract_last(keys, queries)
+    same = key_docs == query_docs
+    return jnp.where(jnp.concatenate([same, same], axis=1), scores, jnp.float32(far_below))
+
+
+def attend_kernel(span, q_ref, k_ref, v_ref, kd_ref, qd_ref, o_ref, l_ref):
+    first = pl.multiple_of(pl.program_id(1) * QBLOCK, QBLOCK)
+    keys = k_ref[pl.ds(first, span), :]
+    values = v_ref[pl.ds(first, span), :]
+    scores = masked_scores(
+        span, stack_heads(q_ref[...]), keys, kd_ref[pl.ds(first, span), :], qd_ref[0]
+    )
+    top = jnp.max(scores, axis=0, keepdims=True)
+    expo = jnp.exp(scores - top)
+    total = jnp.sum(expo, axis=0, keepdims=True)
+    probs = (expo * (1.0 / total)).astype(jnp.bfloat16)
+    o_ref[...] = unstack_heads(contract_rows(values, probs)).astype(jnp.bfloat16)
+    l_ref[0, 0] = top + jnp.log(total)
+
+
+def attend_back_kernel(
+    span, q_ref, k_ref, v_ref, kd_ref, qd_ref, do_ref, l_ref, dq_ref, dk_ref, dv_ref, dk_acc, dv_acc
+):
+    step = pl.program_id(1)
+
+    @pl.when(step == 0)
+    def _():
+        dk_acc[...] = jnp.zeros_like(dk_acc)
+        dv_acc[...] = jnp.zeros_like(dv_acc)
+
+    first = pl.multiple_of(step * QBLOCK, QBLOCK)
+    here = pl.ds(first, span)
+    keys = k_ref[here, :]
+    values = v_ref[here, :]
+    queries = stack_heads(q_ref[...])
+    grads = stack_heads(do_ref[...])
+    scores = masked_scores(span, queries, keys, kd_ref[here, :], qd_ref[0])
+    probs = jnp.exp(scores - l_ref[0, 0])
+    grad_probs = contract_last(values, grads)
+    inner = jnp.sum(grad_probs * probs, axis=0, keepdims=True)
+    grad_scores = (probs * (grad_probs - inner)).astype(jnp.bfloat16)
+    dq_ref[...] = unstack_heads(contract_rows(keys, grad_scores)).astype(jnp.bfloat16)
+    dk_acc[here, :] += dot32(grad_scores, queries)
+    dv_acc[here, :] += dot32(probs.astype(jnp.bfloat16), grads)
+
+    @pl.when(step == pl.num_programs(1) - 1)
+    def _():
+        dk_ref[...] = dk_acc[...].astype(jnp.bfloat16)
+        dv_ref[...] = dv_acc[...].astype(jnp.bfloat16)
+
+
+def attention_specs(window):
+    rows = pl.BlockSpec((QBLOCK, PAIR), lambda h, i: (i, h))
+    keys = pl.BlockSpec((window, PAIR), lambda h, i: (0, h))
+    key_docs = pl.BlockSpec((window, QBLOCK), lambda h, i: (0, 0))
+    query_docs = pl.BlockSpec((1, 1, QBLOCK), lambda h, i: (i, 0, 0))
+    logs = pl.BlockSpec((1, 1, 1, 2 * QBLOCK), lambda h, i: (h, i, 0, 0))
+    return rows, keys, key_docs, query_docs, logs
+
+
+def attend(queries, keys, values, key_docs, query_docs, reach):
+    count, width = queries.shape
+    window = keys.shape[0]
+    blocks, pairs, span = count // QBLOCK, width // PAIR, QBLOCK + 2 * reach
+    rows, key_spec, kd_spec, qd_spec, logs = attention_specs(window)
+    return pl.pallas_call(
+        partial(attend_kernel, span),
+        grid=(pairs, blocks),
+        in_specs=[rows, key_spec, key_spec, kd_spec, qd_spec],
+        out_specs=[rows, logs],
+        out_shape=[
+            jax.ShapeDtypeStruct((count, width), jnp.bfloat16),
+            jax.ShapeDtypeStruct((pairs, blocks, 1, 2 * QBLOCK), jnp.float32),
+        ],
+        compiler_params=pltpu.CompilerParams(vmem_limit_bytes=40 << 20),
+        cost_estimate=pl.CostEstimate(
+            flops=16 * count * span * width, bytes_accessed=8 << 20, transcendentals=0
+        ),
+        name="attend",
+    )(queries, keys, values, key_docs, query_docs)
+
+
+def attend_back(queries, keys, values, key_docs, query_docs, grads, logs_in, reach):
+    count, width = queries.shape
+    window = keys.shape[0]
+    blocks, pairs, span = count // QBLOCK, width // PAIR, QBLOCK + 2 * reach
+    rows, key_spec, kd_spec, qd_spec, logs = attention_specs(window)
+    return pl.pallas_call(
+        partial(attend_back_kernel, span),
+        grid=(pairs, blocks),
+        in_specs=[rows, key_spec, key_spec, kd_spec, qd_spec, rows, logs],
+        out_specs=[rows, key_spec, key_spec],
+        out_shape=[
+            jax.ShapeDtypeStruct((count, width), jnp.bfloat16),
+            jax.ShapeDtypeStruct((window, width), jnp.bfloat16),
+            jax.ShapeDtypeStruct((window, width), jnp.bfloat16),
+        ],
+        scratch_shapes=[
+            pltpu.VMEM((window, PAIR), jnp.float32),
+            pltpu.VMEM((window, PAIR), jnp.float32),
+        ],
+        compiler_params=pltpu.CompilerParams(vmem_limit_bytes=40 << 20),
+        cost_estimate=pl.CostEstimate(
+            flops=40 * count * span * width, bytes_accessed=12 << 20, transcendentals=0
+        ),
+        name="attend_back",
+    )(queries, keys, values, key_docs, query_docs, grads, logs_in)
+
+
+def ctx_swap(array, bit):
+    return lax.ppermute(array, "ctx", [(i, i ^ bit) for i in range(4)])
+
+
+def core_swap(array):
+    return ctx_swap(array, 1)
+
+
+def across_swap(array):
+    return ctx_swap(array, 2)
+
+
+def in_order(flag, mine, other):
+    return jnp.where(flag == 0, mine, other), jnp.where(flag == 0, other, mine)
+
+
+def chain_pairs():
+    def at(across, core, tp):
+        return (2 * across + core) * 4 + tp
+
+    pairs = []
+    for group in (0, 2):
+        path = [(0, group), (0, group + 1), (1, group + 1), (1, group)]
+        for (across, tp), (next_across, next_tp) in zip(path[:-1], path[1:]):
+            pairs.append((at(across, 1, tp), at(next_across, 0, next_tp)))
+            pairs.append((at(next_across, 0, next_tp), at(across, 1, tp)))
+    return pairs
+
+
+def span_shards(
+    layer_input,
+    segment_ids,
+    query_proj,
+    query_bias,
+    key_proj,
+    value_proj,
+    value_bias,
+    out_proj,
+    out_bias,
+    attn_gain,
+    attn_shift,
+    up_proj,
+    up_bias,
+    down_proj,
+    down_bias,
+    ffn_gain,
+    ffn_shift,
+    out_cotangent,
+):
+    seqs, block, width = layer_input.shape
+    length = segment_ids.shape[1]
+    reach = length // 2
+    count = seqs * block // 4
+    window = count + 2 * reach
+    scale = 1.0 / math.sqrt(HEAD_DIM)
+    bf16, f32 = jnp.bfloat16, jnp.float32
+    ctx, tp = lax.axis_index("ctx"), lax.axis_index("tp")
+    core, across, side = ctx & 1, ctx >> 1, tp & 1
+    place = 2 * across + (side ^ across)
+    odd = across ^ side
+    both = ("tp", "shard")
+
+    half = query_proj.shape[0] // 2
+    own_in = lax.dynamic_slice_in_dim(
+        jnp.concatenate([query_proj, key_proj, value_proj], axis=1), core * half, half, 0
+    )
+    in_mine = lax.all_gather(own_in, both, axis=0, tiled=False)
+    in_lo, in_hi = in_order(core, in_mine, core_swap(in_mine))
+    heads = query_proj.shape[1]
+    joined = jnp.stack(
+        [in_lo.reshape(4, 2, half, 3, heads), in_hi.reshape(4, 2, half, 3, heads)], axis=2
+    )
+    joined = joined.transpose(4, 1, 2, 3, 0, 5).reshape(3, width, 4 * heads)
+    full_query, full_key, full_value = joined[0], joined[1], joined[2]
+
+    cut = up_proj.shape[1] // 2
+    out_half = out_proj.shape[0] // 2
+    own_rest = jnp.concatenate(
+        [
+            lax.dynamic_slice_in_dim(up_proj, core * cut, cut, 1),
+            lax.dynamic_slice_in_dim(down_proj, core * cut, cut, 0),
+            lax.dynamic_slice_in_dim(out_proj, core * out_half, out_half, 0),
+        ],
+        axis=0,
+    )
+    rest = lax.all_gather(own_rest, both, axis=0, tiled=False).reshape(4, 2, -1, cut)
+    up_here = rest[:, :, :cut].transpose(1, 2, 0, 3).reshape(width, 4 * cut)
+    down_here = rest[:, :, cut : 2 * cut].transpose(0, 2, 1, 3).reshape(4 * cut, width)
+    out_mine = rest[:, :, 2 * cut :]
+    out_lo, out_hi = in_order(core, out_mine, core_swap(out_mine))
+    full_out = (
+        jnp.stack([out_lo, out_hi], axis=1).transpose(0, 1, 3, 2, 4).reshape(width, width)
+    )
+    biases = lax.all_gather(
+        jnp.concatenate(
+            [query_bias, value_bias, lax.dynamic_slice_in_dim(up_bias, core * cut, cut, 0)]
+        ),
+        "tp",
+        axis=0,
+        tiled=False,
+    )
+    full_query_bias = biases[:, :heads].reshape(-1)
+    full_value_bias = biases[:, heads : 2 * heads].reshape(-1)
+    up_bias_here = biases[:, 2 * heads :].reshape(-1)
+
+    first_seq = 3 * (tp >> 1)
+    mine = lax.dynamic_slice_in_dim(layer_input, first_seq + across, 2, 0)
+    theirs = across_swap(lax.dynamic_slice_in_dim(layer_input, first_seq + 1 - across, 2, 0))
+    pair = jnp.stack([mine, theirs])
+    pair_lo, pair_hi = in_order(core, pair, core_swap(pair))
+    quads = jnp.stack([pair_lo, pair_hi], axis=1)
+    quads = jnp.where(across == 0, quads, quads[::-1])
+    near = quads.transpose(2, 0, 1, 3, 4).reshape(2 * length, width)
+    start = 2 * count * place + count * core - length * across
+    edge = jnp.zeros((reach, width), bf16)
+    in_window = lax.dynamic_slice_in_dim(
+        jnp.concatenate([edge, near, edge], axis=0), start, window, 0
+    )
+    ids = lax.dynamic_slice_in_dim(segment_ids, first_seq + across, 2, 0)
+    ids = (ids + jnp.array([[0], [1 << 16]], jnp.int32)).reshape(-1)
+    no_doc = jnp.full((reach,), -1, jnp.int32)
+    window_docs = lax.dynamic_slice_in_dim(
+        jnp.concatenate([no_doc, ids, no_doc]), start, window, 0
+    )
+    key_docs = jnp.broadcast_to(window_docs[:, None], (window, QBLOCK))
+    query_docs = window_docs[reach : reach + count].reshape(-1, 1, QBLOCK)
+    rows_in = in_window[reach : reach + count]
+
+    queries = ((dot32(rows_in, full_query) + full_query_bias) * scale).astype(bf16)
+    keys = dot32(in_window, full_key).astype(bf16)
+    values = (dot32(in_window, full_value) + full_value_bias).astype(bf16)
+    mixed, logs = attend(queries, keys, values, key_docs, query_docs, reach)
+    attended = dot32(mixed, full_out) + out_bias
+    hidden, normed_one, inv_one = norm_forward(
+        rows_in.astype(f32) + attended, attn_gain, attn_shift
+    )
+    hidden_low = hidden.astype(bf16)
+    hidden_both = jnp.concatenate(in_order(core, hidden_low, core_swap(hidden_low)), axis=0)
+    pre_act = dot32(hidden_both, up_here) + up_bias_here
+    cdf = 0.5 * (1.0 + lax.erf(pre_act * math.sqrt(0.5)))
+    acts_low = (pre_act * cdf).astype(bf16)
+    slope = cdf + pre_act * (jnp.exp(-0.5 * pre_act * pre_act) * (1.0 / math.sqrt(2 * math.pi)))
+
+    def chip_sum(partial_rows):
+        low, high = partial_rows[:count], partial_rows[count:]
+        keep = jnp.where(core == 0, low, high)
+        give = jnp.where(core == 0, high, low).astype(bf16)
+        return keep + core_swap(give).astype(f32)
+
+    ffn_out = chip_sum(dot32(acts_low, down_here)) + down_bias
+    output_rows, normed_two, inv_two = norm_forward(hidden + ffn_out, ffn_gain, ffn_shift)
+
+    def deliver(rows):
+        chip = jnp.concatenate(in_order(core, rows, core_swap(rows)), axis=0)
+        kept = lax.dynamic_slice_in_dim(chip, odd * block + core * block, block, 0)
+        half_block = block // 2
+        sent = lax.dynamic_slice_in_dim(
+            chip, (1 - odd) * 2 * block + core * half_block, half_block, 0
+        )
+        packed = jnp.concatenate([kept, across_swap(sent)], axis=0)
+        every = lax.all_gather(packed, "tp", axis=0, tiled=False)
+        halves = every[:, block:]
+        lo, hi = in_order(core, halves, core_swap(halves))
+        moved = jnp.concatenate([lo, hi], axis=1)
+        kept_all = every[:, :block]
+        from_side = 1 ^ across ^ core
+        parts = []
+        for group in (0, 2):
+            foreign = lax.dynamic_index_in_dim(moved, group + from_side, 0, keepdims=False)
+            near_one, mid_one = kept_all[group], kept_all[group + 1]
+            parts += [
+                jnp.where(across == 0, near_one, foreign),
+                mid_one,
+                jnp.where(across == 0, foreign, near_one),
+            ]
+        return jnp.stack(parts)
+
+    layer_output = deliver(output_rows.astype(bf16))
+
+    cot_mine = lax.dynamic_slice_in_dim(out_cotangent, first_seq + across, 2, 0)
+    cot_theirs = across_swap(
+        lax.dynamic_slice_in_dim(out_cotangent, first_seq + 1 - across, 2, 0)
+    )
+    cot_pair = jnp.stack([cot_mine, cot_theirs])
+    cot_lo, cot_hi = in_order(core, cot_pair, core_swap(cot_pair))
+    cots = jnp.stack([cot_lo, cot_hi], axis=1)
+    cots = jnp.where(across == 0, cots, cots[::-1])
+    cots = cots.transpose(2, 0, 1, 3, 4).reshape(2 * length, width)
+    grad_out = lax.dynamic_slice_in_dim(cots, start, count, 0).astype(f32)
+
+    grad_two, ffn_gain_grad, ffn_shift_grad = norm_backward(grad_out, normed_two, inv_two, ffn_gain)
+    grad_ffn = grad_two.astype(bf16)
+    down_bias_grad = jnp.sum(grad_ffn, axis=0, dtype=f32)
+    grad_ffn_both = jnp.concatenate(in_order(core, grad_ffn, core_swap(grad_ffn)), axis=0)
+    down_part = contract_rows(acts_low, grad_ffn_both)
+    grad_pre = (slope * contract_last(grad_ffn_both, down_here)).astype(bf16)
+    up_bias_part = jnp.sum(grad_pre, axis=0, dtype=f32)
+    up_part = contract_rows(hidden_both, grad_pre)
+    grad_hidden = grad_two + chip_sum(contract_last(grad_pre, up_here))
+    grad_one, attn_gain_grad, attn_shift_grad = norm_backward(
+        grad_hidden, normed_one, inv_one, attn_gain
+    )
+    grad_attn = grad_one.astype(bf16)
+    out_bias_grad = jnp.sum(grad_attn, axis=0, dtype=f32)
+    out_part = contract_rows(mixed, grad_attn).astype(bf16)
+    grad_mixed = contract_last(grad_attn, full_out).astype(bf16)
+    grad_queries, grad_keys, grad_values = attend_back(
+        queries, keys, values, key_docs, query_docs, grad_mixed, logs, reach
+    )
+    grad_scaled = grad_queries * bf16(scale)
+    grad_near = (contract_last(grad_keys, full_key) + contract_last(grad_values, full_value)).astype(
+        bf16
+    )
+    give = jnp.where(core == 0, grad_near[count + reach :], grad_near[:reach])
+    keep = jnp.where(core == 0, grad_near[: count + reach], grad_near[reach:]).astype(f32)
+    got = core_swap(give[: 2 * reach]).astype(f32)
+    shared = reach - count
+    own_sum = jnp.where(core == 0, keep[reach:] + got[shared:], keep[:count] + got[:count])
+    onward = jnp.where(
+        core == 0,
+        jnp.concatenate([keep[:count], keep[count:reach] + got[:shared]], axis=0),
+        jnp.concatenate([keep[count : count + shared] + got[count:], keep[count + shared :]], axis=0),
+    ).astype(bf16)
+    arrived = lax.ppermute(onward, ("ctx", "tp"), chain_pairs())
+    passed = core_swap(jnp.where(core == 0, arrived[count:], arrived[:shared])).astype(f32)
+    own_sum = own_sum + jnp.where(core == 0, arrived[:count], arrived[shared:]).astype(f32)
+    rest_rows = jnp.zeros((count - shared, width), f32)
+    own_sum = own_sum + jnp.where(
+        core == 0,
+        jnp.concatenate([rest_rows, passed], axis=0),
+        jnp.concatenate([passed, rest_rows], axis=0),
+    )
+    grad_rows = grad_one + own_sum + contract_last(grad_scaled, full_query)
+    input_grad = deliver(grad_rows.astype(bf16)).astype(f32)
+
+    query_part = contract_rows(rows_in, grad_scaled)
+    key_part = contract_rows(in_window, grad_keys)
+    value_part = contract_rows(in_window, grad_values)
+    in_part = jnp.stack([query_part, key_part, value_part]).astype(bf16)
+    in_part = in_part.reshape(3, 2, 2, half, 4, heads).transpose(2, 4, 1, 3, 0, 5)
+    in_part = in_part.reshape(2, 8 * half, 3 * heads)
+    out_part = out_part.reshape(4, 2, out_half, 2, cut).transpose(1, 0, 3, 2, 4)
+
+    def core_sum(parts):
+        return (
+            jnp.where(core == 0, parts[0], parts[1]).astype(f32)
+            + core_swap(jnp.where(core == 0, parts[1], parts[0])).astype(f32)
+        ).astype(bf16)
+
+    def finish(scattered):
+        total = (scattered.astype(f32) + across_swap(scattered).astype(f32)).astype(bf16)
+        return in_order(core, total, core_swap(total))
+
+    in_done = lax.psum_scatter(core_sum(in_part), both, scatter_dimension=0, tiled=True)
+    in_grads = jnp.concatenate(finish(in_done), axis=0).astype(f32)
+    rest_part = jnp.concatenate(
+        [
+            up_part.astype(bf16).reshape(2, cut, 4, cut).transpose(2, 0, 1, 3),
+            down_part.astype(bf16).reshape(4, cut, 2, cut).transpose(0, 2, 1, 3),
+            core_sum(out_part),
+        ],
+        axis=2,
+    ).reshape(-1, cut)
+    rest_done = lax.psum_scatter(rest_part, both, scatter_dimension=0, tiled=True)
+    rest_lo, rest_hi = finish(rest_done)
+    up_grad = jnp.concatenate([rest_lo[:cut], rest_hi[:cut]], axis=1).astype(f32)
+    down_grad = jnp.concatenate([rest_lo[cut : 2 * cut], rest_hi[cut : 2 * cut]], axis=0).astype(f32)
+    out_grad = jnp.concatenate([rest_lo[2 * cut :], rest_hi[2 * cut :]], axis=0).astype(f32)
+
+    up_bias_all = jnp.stack(
+        [jnp.where(core == 0, up_bias_part, 0.0), jnp.where(core == 1, up_bias_part, 0.0)]
+    )
+    small = lax.psum(
+        jnp.concatenate(
+            [
+                jnp.sum(grad_scaled, axis=0, dtype=f32),
+                jnp.sum(grad_values, axis=0, dtype=f32),
+                out_bias_grad,
+                attn_gain_grad,
+                attn_shift_grad,
+                down_bias_grad,
+                ffn_gain_grad,
+                ffn_shift_grad,
+                up_bias_all.reshape(-1),
+            ]
+        ),
+        ("shard", "ctx", "tp"),
+    )
+    flat = small[: 8 * width].reshape(8, width)
+    query_bias_grad = lax.dynamic_slice_in_dim(flat[0], tp * heads, heads, 0)
+    value_bias_grad = lax.dynamic_slice_in_dim(flat[1], tp * heads, heads, 0)
+    up_bias_grad = lax.dynamic_index_in_dim(
+        small[8 * width :].reshape(2, 4, cut), tp, 1, keepdims=False
+    ).reshape(-1)
+    return (
+        layer_output,
+        input_grad,
+        in_grads[:, :heads],
+        query_bias_grad,
+        in_grads[:, heads : 2 * heads],
+        in_grads[:, 2 * heads :],
+        value_bias_grad,
+        out_grad,
+        flat[2],
+        flat[3],
+        flat[4],
+        up_grad,
+        up_bias_grad,
+        down_grad,
+        flat[5],
+        flat[6],
+        flat[7],
+    )
+
+
+def pick_plan(mesh):
+    shape = dict(mesh.shape)
+
+    def plan(layer_input, segment_ids, *others):
+        seqs, block, _ = layer_input.shape
+        fits = (
+            (shape["shard"], shape["ctx"], shape["tp"]) == (2, 4, 4)
+            and seqs == 6
+            and segment_ids.shape[1] == 4 * block
+            and block == 2 * QBLOCK
+        )
+        chosen = span_shards if fits else general_shards
+        return chosen(layer_input, segment_ids, *others)
+
+    return plan
+
+
 def solution(mesh):
     return jax.shard_map(
-        shards,
+        pick_plan(mesh),
         mesh=mesh,
         in_specs=(
             P("shard", "ctx", None),

time: 908 us -> 597 us (0.66)
  waiting for transfers between devices: 582 us -> 181 us
  Pallas kernels: 0 us -> 48.5 us
  local copies, waits for them, and re-layouts: 95.3 us -> 142 us
  matrix products: 91.4 us -> 49.4 us
  starting transfers between devices: 1.7 us -> 21 us
  other arithmetic: 66 us -> 80.2 us
    psum x5 -> x0, waiting for transfers between devices: 394 us -> none  [the longest x1 94.6 us: shards(): lax.psum(contract_last(grad_pre, full_up).astype(jnp.bfloat16), 'tp')]
    ppermute x0 -> x25, waiting for transfers between devices: none -> 72.6 us  [the longest x24 47.7 us: ctx_swap(): return lax.ppermute(array, 'ctx', [(i, i ^ bit) for i in range(4)])]
    unnamed x22 -> x7, waiting for transfers between devices: 65.3 us -> 0.1 us
    pallas_call x0 -> x2, Pallas kernels: none -> 48.5 us  [the longest x1 27.2 us: attend_back(): pl.pallas_call(partial(attend_back_kernel, span), grid=(pairs, blocks), i...]
    dot_general x46 -> x6, matrix products: 59.9 us -> 14.1 us  [dot32(): return jnp.dot(left, right, preferred_element_type=jnp.float32)]
    dynamic_slice x61 -> x6, local copies, waits for them, and re-layouts: 40.3 us -> 2.65 us  [the longest x1 1.27 us: span_shards(): lax.dynamic_slice_in_dim(down_proj, core * cut, cut, 0)]
    concatenate x0 -> x12, other arithmetic: none -> 26.1 us  [the longest x1 15.1 us: span_shards(): jnp.concatenate([up_part.astype(bf16).reshape(2, cut, 4, cut).transpose(2...]
    another operation x2 -> x8, local copies, waits for them, and re-layouts: 0.08 us -> 22.3 us  [the longest x6 20.9 us: span_shards(): in_part = jnp.stack([query_part, key_part, value_part]).astype(bf16)]
  transfers between devices with their start and end apart: 17 -> 31, of which waited for: 15 -> 12; matrix products, arithmetic and copies ran while one was open for 10% -> 40% of each run, Pallas kernels for 0% -> 8%
where the time goes in v1:
time: 597 us; the launch traced here: 589 us
  waiting for transfers between devices  181 us (30%)
  local copies, waits for them, and re-layouts  142 us (24%)
  other arithmetic  80.2 us (13%)
  blocking collectives  50.6 us (8%)
  matrix products  49.4 us (8%)
  Pallas kernels  48.5 us (8%)
  starting transfers between devices  21 us (4%)
  between operations  16 us (3%)
    reduce_scatter x1, waiting for transfers between devices, span_shards(): lax.psum_scatter(rest_part, both, scatter_dimension=0, tiled=True)  58.6 us
    ppermute x24, waiting for transfers between devices, ctx_swap(): return lax.ppermute(array, 'ctx', [(i, i ^ bit) for i in range(4)])  47.7 us
    psum x1, blocking collectives, span_shards(): lax.psum(jnp.concatenate([jnp.sum(grad_scaled, axis=0, dtype=f32), jnp.su...  40.1 us
    all_gather x1, waiting for transfers between devices, span_shards(): lax.all_gather(own_rest, both, axis=0, tiled=False).reshape(4, 2, -1, cut)  37.5 us
    pallas_call x1, Pallas kernels, attend_back(): pl.pallas_call(partial(attend_back_kernel, span), grid=(pairs, blocks), i...  27.2 us
    unnamed x144, local copies, waits for them, and re-layouts  26.8 us
    ppermute x1, waiting for transfers between devices, span_shards(): arrived = lax.ppermute(onward, ('ctx', 'tp'), chain_pairs())  24.9 us
    dot_general x6, matrix products, contract_rows(): lax.dot_general(left, right, (((0,), (0,)), ((), ())), preferred_element_...  21.4 us
  transfers between devices with their start and end apart: 31, of which 12 were waited for; matrix products, arithmetic and copies ran while one was open for 40% of the time, Pallas kernels for 8%

profile of v1, /device:TPU:1, one launch (start us, length us, event | category | flops | bytes accessed | tf_op | source)
XLA Modules:
  0.0 588.8 jit_solution(16339683986799472558)
XLA Ops:
  15.9 17.4 %collective-permute-done = bf16[2,256,768]{2,1,0:T(8,128)(2,1)S(1)} collective-permute-done((bf16[2,256,768]{2,1,0:T(8,128)(2,1)S(1)}, bf16[2,256,768]{2,1,0:T(8,128)(2,1)S(1)}, u32[]{:S(2)}, u32[]{:S(2)}) %collective-permute-start) | collective-permute-done | bytes 786464 | tf_op jit(solution)/shard_map/ppermute | solution.py:433
  37.6 10.5 %all-gather.5 = bf16[4,1,768]{2,1,0:T(2,128)(2,1)S(1)} all-gather(bf16[1,1,768]{2,1,0:T(2,128)(2,1)S(1)} %reshape.260), channel_id=3, replica_groups=mesh['shard'=2,'ctx'=4,'tp'=4] {'tp'}, dimensions={0}, use_global_device_ids=true | all-gather | bytes 7680 | tf_op jit(solution)/shard_map/all_gather | solution.py:525
  48.1 12.5 %all-gather.11.cloned.1.call-done = bf16[1536,576]{1,0:T(8,128)(2,1)} async-done(((bf16[192,576]{1,0:T(8,128)(2,1)}), bf16[1536,576]{1,0:T(8,128)(2,1)}) %all-gather.11.cloned.1.call-update) | async-done | bytes 1769488 | tf_op jit(solution)/shard_map/all_gather | solution.py:498
  65.7 4.6 fusion.9
  70.3 4.0 broadcast_select_fusion.2
  77.6 4.2 copy.103
  86.0 4.0 copy.106
  90.0 4.0 squeeze.14
  96.3 4.0 squeeze.13
  103.8 3.9 convolution_convert_fusion.2.k_ref
  111.0 37.5 %all-gather.13.cloned.1.call-done = bf16[6912,384]{1,0:T(8,128)(2,1)} async-done(((bf16[864,384]{1,0:T(8,128)(2,1)}), bf16[6912,384]{1,0:T(8,128)(2,1)}) %all-gather.13.cloned.1.call-update) | async-done | bytes 5308432 | tf_op jit(solution)/shard_map/all_gather | solution.py:517
  154.1 21.2 %attend.1 = (bf16[384,768]{1,0:T(8,128)(2,1)S(1)}, f32[6,3,1,256]{3,2,1,0:T(1,128)S(1)}) custom-call(bf16[384,768]{1,0:T(8,128)(2,1)S(1)} %fusion.17.q_ref, bf16[1408,768]{1,0:T(8,128)(2,1)S(1)} %convolution_convert_fusion.2.k_ref, bf16[1408,768]{1,0:T(8,128)(2,1)S(1)} %copy-done.9, s32[1408,128]{1,0:T(8,128)S(1)} %broadcast_in_dim.12.kd_ref, ...), custom_call_target="tpu_custom_call" | custom-call | flops 5435817984 | bytes 8388608 | tf_op jit(solution)/shard_map/attend/pallas_call | solution.py:388
  205.2 4.6 convert_reduce_fusion
  222.0 27.2 %attend_back.1 = (bf16[384,768]{1,0:T(8,128)(2,1)S(1)}, bf16[1408,768]{1,0:T(8,128)(2,1)S(1)}, bf16[1408,768]{1,0:T(8,128)(2,1)S(1)}) custom-call(bf16[384,768]{1,0:T(8,128)(2,1)S(1)} %copy-done.6, bf16[1408,768]{1,0:T(8,128)(2,1)S(1)} %copy-done.8, bf16[1408,768]{1,0:T(8,128)(2,1)S(1)} %copy-done.10, s32[1408,128]{1,0:T(8,128)S(1)} %broadcast_in_dim.12.kd_ref, ...), custom_call_target="tpu_custom_call" | custom-call | flops 13589544960 | bytes 12582912 | tf_op jit(solution)/shard_map/attend_back/pallas_call | solution.py:410
  256.4 4.4 stack.97
  263.6 4.4 stack.98
  273.2 4.7 convolution_convert_fusion.4
  277.8 4.6 stack.99
  289.2 6.5 %copy.116 = bf16[1,4,2,192,3,192]{3,2,1,5,4,0:T(2,128)(2,1)} copy(bf16[1,4,2,192,3,192]{5,3,4,2,1,0:T(8,128)(2,1)} %get-tuple-element.44) | data formatting | bytes 3538944 | tf_op jit(solution)/shard_map/jit(_where)/select_n | solution.py:678
  295.8 6.3 %select_n.422 = bf16[1536,576]{0,1:T(8,128)(2,1)} reshape(bf16[1,4,2,192,3,192]{3,2,1,5,4,0:T(2,128)(2,1)} %copy.116) | data formatting | bytes 3538944 | tf_op jit(solution)/shard_map/jit(_where)/select_n | solution.py:678
  302.5 8.2 %copy.115 = f32[1,4,2,192,3,192]{3,2,1,5,4,0:T(2,128)} copy(f32[1,4,2,192,3,192]{5,3,4,2,1,0:T(8,128)} %get-tuple-element.45) | data formatting | bytes 7077888 | tf_op jit(solution)/shard_map/convert_element_type | solution.py:677
  310.7 6.8 %reshape.252 = f32[1536,576]{0,1:T(8,128)} reshape(f32[1,4,2,192,3,192]{3,2,1,5,4,0:T(2,128)} %copy.115) | data formatting | bytes 7077888 | tf_op jit(solution)/shard_map/convert_element_type | solution.py:677
  340.3 24.9 %collective-permute-done.14 = bf16[512,768]{1,0:T(8,128)(2,1)S(1)} collective-permute-done((bf16[512,768]{1,0:T(8,128)(2,1)S(1)}, bf16[512,768]{1,0:T(8,128)(2,1)S(1)}, u32[]{:S(2)}, u32[]{:S(2)}) %collective-permute-start.14) | collective-permute-done | bytes 786464 | tf_op jit(solution)/shard_map/ppermute | solution.py:655
  371.3 5.2 collective-permute-done.17
  392.8 5.3 reshape.244
  398.1 5.2 convolution_convert_fusion
  403.3 5.7 reshape.245
  414.6 15.1 %pad_maximum_fusion = bf16[4,2,864,384]{3,0,2,1:T(4,128)(2,1)S(1)} fusion(bf16[4,2,96,384]{3,0,2,1:T(4,128)(2,1)S(1)} %fusion.28, bf16[4,2,384,384]{3,0,2,1:T(4,128)(2,1)S(1)} %bitcast.107, bf16[4,2,384,384]{3,0,2,1:T(4,128)(2,1)S(1)} %bitcast.106), kind=kLoop, calls=%fused_computation.1 | loop fusion | flops 5308416 | bytes 10616832 | tf_op jit(solution)/shard_map/concatenate | solution.py:687
  434.9 40.1 %psum.7 = f32[9216]{0:T(1024)S(1)} all-reduce(f32[9216]{0:T(1024)S(1)} %constant_dynamic-update-slice_fusion.1), channel_id=1, replica_groups=mesh['shard'=2,'ctx'=4,'tp'=4] {'shard','ctx','tp'}, use_global_device_ids=true, to_apply=%region_18.19 | all-reduce | flops 9216 | bytes 73728 | tf_op jit(solution)/shard_map/psum | solution.py:704
  486.7 5.1 collective-permute-done.20
  499.1 58.6 %reduce-scatter.5.cloned.1.call-done = bf16[864,384]{1,0:T(8,128)(2,1)} async-done(((bf16[6912,384]{1,0:T(8,128)(2,1)}), bf16[864,384]{1,0:T(8,128)(2,1)}) %reduce-scatter.5.cloned.1.call-update) | async-done | bytes 663568 | tf_op jit(solution)/shard_map/reduce_scatter | solution.py:695
  560.2 13.4 %collective-permute-done.23 = bf16[864,384]{1,0:T(8,128)(2,1)S(1)} collective-permute-done((bf16[864,384]{1,0:T(8,128)(2,1)}, bf16[864,384]{1,0:T(8,128)(2,1)S(1)}, u32[]{:S(2)}, u32[]{:S(2)}) %collective-permute-start.23) | collective-permute-done | bytes 663584 | tf_op jit(solution)/shard_map/ppermute | solution.py:433
  (355 shorter events, 188.7 us)
Async XLA Ops:
  7.2 53.4 %all-gather.11.cloned.1.call-start = ((), (), s32[]{:S(2)}) async-start(), calls=%async_computation.3 | async-start | bytes 2211840 | tf_op jit(solution)/shard_map/all_gather | solution.py:498
  11.3 137.3 %all-gather.13.cloned.1.call-start = ((), (), s32[]{:S(2)}) async-start(), calls=%async_computation.4 | async-start | bytes 5971968 | tf_op jit(solution)/shard_map/all_gather | solution.py:517
  13.6 419.9 %all-gather.15.cloned.1.call-start = ((), (), s32[]{:S(2)}) async-start(), calls=%async_computation.5 | async-start | bytes 2949120 | tf_op jit(solution)/shard_map/all_gather | solution.py:592
  13.8 19.5 %collective-permute-start = (bf16[2,256,768]{2,1,0:T(8,128)(2,1)S(1)}, bf16[2,256,768]{2,1,0:T(8,128)(2,1)S(1)}, u32[]{:S(2)}, u32[]{:S(2)}) collective-permute-start(bf16[2,256,768]{2,1,0:T(8,128)(2,1)S(1)} %get-tuple-element.66), channel_id=1, source_target_pairs={{0,8},{4,12},{8,0},{12,4},{1,9},{5,13},{9,1},{13,5},{2,10},{6,14},... | collective-permute-start | bytes 2359304 | tf_op jit(solution)/shard_map/ppermute | solution.py:433
  33.5 29.5 %collective-permute-start.1 = (bf16[2,2,256,768]{3,2,1,0:T(8,128)(2,1)S(1)}, bf16[2,2,256,768]{3,2,1,0:T(8,128)(2,1)}, u32[]{:S(2)}, u32[]{:S(2)}) collective-permute-start(bf16[2,2,256,768]{3,2,1,0:T(8,128)(2,1)S(1)} %pad_maximum_fusion.3), channel_id=1, source_target_pairs={{0,4},{4,0},{8,12},{12,8},{1,5},{5,1},{9,13},{13,9},{2,6},{6,2},{1... | collective-permute-start | bytes 4718600 | tf_op jit(solution)/shard_map/ppermute | solution.py:433
  36.2 144.0 %collective-permute-start.9 = (bf16[2,256,768]{2,1,0:T(8,128)(2,1)}, bf16[2,256,768]{2,1,0:T(8,128)(2,1)}, u32[]{:S(2)}, u32[]{:S(2)}) collective-permute-start(bf16[2,256,768]{2,1,0:T(8,128)(2,1)} %get-tuple-element.64), channel_id=1, source_target_pairs={{0,8},{4,12},{8,0},{12,4},{1,9},{5,13},{9,1},{13,5},{2,10},{6,14},... | collective-permute-start | bytes 2359304 | tf_op jit(solution)/shard_map/ppermute | solution.py:433
  60.6 9.7 %collective-permute-start.2 = (bf16[8,192,576]{2,1,0:T(8,128)(2,1)}, bf16[8,192,576]{2,1,0:T(8,128)(2,1)}, u32[]{:S(2)}, u32[]{:S(2)}) collective-permute-start(bf16[8,192,576]{2,1,0:T(8,128)(2,1)} %bitcast.140), channel_id=1, source_target_pairs={{0,4},{4,0},{8,12},{12,8},{1,5},{5,1},{9,13},{13,9},{2,6},{6,2},{1... | collective-permute-start | bytes 5308424 | tf_op jit(solution)/shard_map/ppermute | solution.py:433
  107.8 46.3 %copy-start.7 = (bf16[1408,768]{1,0:T(8,128)(2,1)}, bf16[1408,768]{1,0:T(8,128)(2,1)S(1)}, u32[]{:S(2)}) copy-start(bf16[1408,768]{1,0:T(8,128)(2,1)S(1)} %convolution_convert_fusion.2.k_ref) | copy-start | bytes 6488068
  150.3 25.0 %collective-permute-start.3 = (bf16[4,2,96,384]{3,1,2,0:T(2,128)(2,1)S(1)}, bf16[4,2,96,384]{3,1,2,0:T(2,128)(2,1)S(1)}, u32[]{:S(2)}, u32[]{:S(2)}) collective-permute-start(bf16[4,2,96,384]{3,1,2,0:T(2,128)(2,1)S(1)} %copy.123), channel_id=1, source_target_pairs={{0,4},{4,0},{8,12},{12,8},{1,5},{5,1},{9,13},{13,9},{2,6},{6,2},{1... | collective-permute-start | bytes 1769480 | tf_op jit(solution)/shard_map/ppermute | solution.py:433
  179.9 10.1 %collective-permute-start.4 = (bf16[384,768]{1,0:T(8,128)(2,1)S(1)}, bf16[384,768]{1,0:T(8,128)(2,1)}, u32[]{:S(2)}, u32[]{:S(2)}) collective-permute-start(bf16[384,768]{1,0:T(8,128)(2,1)S(1)} %fusion.29), channel_id=1, source_target_pairs={{0,4},{4,0},{8,12},{12,8},{1,5},{5,1},{9,13},{13,9},{2,6},{6,2},{1... | collective-permute-start | bytes 1769480 | tf_op jit(solution)/shard_map/ppermute | solution.py:433
  181.8 16.1 %collective-permute-start.10 = (bf16[2,2,256,768]{3,2,1,0:T(8,128)(2,1)S(1)}, bf16[2,2,256,768]{3,2,1,0:T(8,128)(2,1)S(1)}, u32[]{:S(2)}, u32[]{:S(2)}) collective-permute-start(bf16[2,2,256,768]{3,2,1,0:T(8,128)(2,1)S(1)} %pad_maximum_fusion.4), channel_id=1, source_target_pairs={{0,4},{4,0},{8,12},{12,8},{1,5},{5,1},{9,13},{13,9},{2,6},{6,2},{1... | collective-permute-start | bytes 4718600 | tf_op jit(solution)/shard_map/ppermute | solution.py:433
  197.5 3.0 collective-permute-start.5
  203.0 2.1 collective-permute-start.11
  213.3 2.1 collective-permute-start.12
  220.6 31.7 %collective-permute-start.6 = (bf16[384,768]{1,0:T(8,128)(2,1)S(1)}, bf16[384,768]{1,0:T(8,128)(2,1)S(1)}, u32[]{:S(2)}, u32[]{:S(2)}) collective-permute-start(bf16[384,768]{1,0:T(8,128)(2,1)S(1)} %get-tuple-element.69), channel_id=1, source_target_pairs={{0,4},{4,0},{8,12},{12,8},{1,5},{5,1},{9,13},{13,9},{2,6},{6,2},{1... | collective-permute-start | bytes 1769480 | tf_op jit(solution)/shard_map/ppermute | solution.py:433
  253.3 18.0 %collective-permute-start.7 = (bf16[128,768]{1,0:T(8,128)(2,1)}, bf16[128,768]{1,0:T(8,128)(2,1)}, u32[]{:S(2)}, u32[]{:S(2)}) collective-permute-start(bf16[128,768]{1,0:T(8,128)(2,1)} %fusion.51), channel_id=1, source_target_pairs={{0,8},{4,12},{8,0},{12,4},{1,9},{5,13},{9,1},{13,5},{2,10},{6,14},... | collective-permute-start | bytes 589832 | tf_op jit(solution)/shard_map/ppermute | solution.py:433
  273.1 209.7 %reduce-scatter.7.cloned.1.call-start = ((), (), s32[]{:S(2)}) async-start(), calls=%async_computation.7 | async-start | bytes 2211840
  302.1 24.0 %collective-permute-start.19 = (bf16[1536,576]{0,1:T(8,128)(2,1)}, bf16[1536,576]{0,1:T(8,128)(2,1)}, u32[]{:S(2)}, u32[]{:S(2)}) collective-permute-start(bf16[1536,576]{0,1:T(8,128)(2,1)} %select_n.422), channel_id=1, source_target_pairs={{0,4},{4,0},{8,12},{12,8},{1,5},{5,1},{9,13},{13,9},{2,6},{6,2},{1... | collective-permute-start | bytes 5308424 | tf_op jit(solution)/shard_map/ppermute | solution.py:433
  324.3 12.3 %collective-permute-start.13 = (bf16[512,768]{1,0:T(8,128)(2,1)}, bf16[512,768]{1,0:T(8,128)(2,1)}, u32[]{:S(2)}, u32[]{:S(2)}) collective-permute-start(bf16[512,768]{1,0:T(8,128)(2,1)} %slice_select_fusion.1), channel_id=1, source_target_pairs={{0,4},{4,0},{8,12},{12,8},{1,5},{5,1},{9,13},{13,9},{2,6},{6,2},{1... | collective-permute-start | bytes 2359304 | tf_op jit(solution)/shard_map/ppermute | solution.py:433
  334.4 159.2 %all-gather.17.cloned.1.call-start = ((), (), s32[]{:S(2)}) async-start(), calls=%async_computation.6 | async-start | bytes 2949120 | tf_op jit(solution)/shard_map/all_gather | solution.py:592
  338.1 27.0 %collective-permute-start.14 = (bf16[512,768]{1,0:T(8,128)(2,1)S(1)}, bf16[512,768]{1,0:T(8,128)(2,1)S(1)}, u32[]{:S(2)}, u32[]{:S(2)}) collective-permute-start(bf16[512,768]{1,0:T(8,128)(2,1)S(1)} %fusion.13), channel_id=1, source_target_pairs={{4,1},{1,4},{5,9},{9,5},{13,8},{8,13},{6,3},{3,6},{7,11},{11,7},{1... | collective-permute-start | bytes 2359304 | tf_op jit(solution)/shard_map/ppermute | solution.py:655
  365.2 1.5 collective-permute-start.15
  367.6 2.1 collective-permute-start.16
  369.9 6.5 %collective-permute-start.17 = (bf16[128,768]{1,0:T(8,128)(2,1)S(1)}, bf16[128,768]{1,0:T(8,128)(2,1)S(1)}, u32[]{:S(2)}, u32[]{:S(2)}) collective-permute-start(bf16[128,768]{1,0:T(8,128)(2,1)S(1)} %fusion.50), channel_id=1, source_target_pairs={{0,8},{4,12},{8,0},{12,4},{1,9},{5,13},{9,1},{13,5},{2,10},{6,14},... | collective-permute-start | bytes 589832 | tf_op jit(solution)/shard_map/ppermute | solution.py:433
  377.3 180.4 %reduce-scatter.5.cloned.1.call-start = ((), (), s32[]{:S(2)}) async-start(), calls=%async_computation.2 | async-start | bytes 5971968 | tf_op jit(solution)/shard_map/reduce_scatter | solution.py:695
  388.5 24.3 %collective-permute-start.22 = (bf16[4,2,96,384]{3,0,2,1:T(4,128)(2,1)}, bf16[4,2,96,384]{3,0,2,1:T(4,128)(2,1)}, u32[]{:S(2)}, u32[]{:S(2)}) collective-permute-start(bf16[4,2,96,384]{3,0,2,1:T(4,128)(2,1)} %select_bitcast_fusion.4), channel_id=1, source_target_pairs={{0,4},{4,0},{8,12},{12,8},{1,5},{5,1},{9,13},{13,9},{2,6},{6,2},{1... | collective-permute-start | bytes 1769480 | tf_op jit(solution)/shard_map/ppermute | solution.py:433
  434.7 42.9 %collective-permute-start.8 = (bf16[4,128,768]{2,1,0:T(8,128)(2,1)S(1)}, bf16[4,128,768]{2,1,0:T(8,128)(2,1)S(1)}, u32[]{:S(2)}, u32[]{:S(2)}) collective-permute-start(bf16[4,128,768]{2,1,0:T(8,128)(2,1)S(1)} %slice.323), channel_id=1, source_target_pairs={{0,4},{4,0},{8,12},{12,8},{1,5},{5,1},{9,13},{13,9},{2,6},{6,2},{1... | collective-permute-start | bytes 2359304 | tf_op jit(solution)/shard_map/ppermute | solution.py:433
  483.9 7.9 %collective-permute-start.20 = (bf16[192,576]{0,1:T(8,128)(2,1)S(1)}, bf16[192,576]{0,1:T(8,128)(2,1)S(1)}, u32[]{:S(2)}, u32[]{:S(2)}) collective-permute-start(bf16[192,576]{0,1:T(8,128)(2,1)S(1)} %copy.121), channel_id=1, source_target_pairs={{0,8},{4,12},{8,0},{12,4},{1,9},{5,13},{9,1},{13,5},{2,10},{6,14},... | collective-permute-start | bytes 663560 | tf_op jit(solution)/shard_map/ppermute | solution.py:433
  491.9 4.8 collective-permute-start.21
  494.8 3.1 collective-permute-start.18
  557.7 15.8 %collective-permute-start.23 = (bf16[864,384]{1,0:T(8,128)(2,1)}, bf16[864,384]{1,0:T(8,128)(2,1)S(1)}, u32[]{:S(2)}, u32[]{:S(2)}) collective-permute-start(bf16[864,384]{1,0:T(8,128)(2,1)} %reduce-scatter.5.cloned.1.call-done), channel_id=1, source_target_pairs={{0,8},{4,12},{8,0},{12,4},{1,9},{5,13},{9,1},{13,5},{2,10},{6,14},... | collective-permute-start | bytes 1990664 | tf_op jit(solution)/shard_map/ppermute | solution.py:433
  573.7 4.6 collective-permute-start.24
  (58 other events, 353.8 us)
Sparse Core Ops, SparseCore 0:
  11.4 49.1 all-gather.10
  62.8 85.7 all-gather.12
  273.2 47.5 all-gather.14
  334.5 63.6 reduce-scatter.6
  399.7 51.0 all-gather.16
  454.7 102.9 reduce-scatter.4

commit v2 on v1

--- a/solution.py
+++ b/solution.py
@@ -361,7 +361,8 @@
     grad_probs = contract_last(values, grads)
     inner = jnp.sum(grad_probs * probs, axis=0, keepdims=True)
     grad_scores = (probs * (grad_probs - inner)).astype(jnp.bfloat16)
-    dq_ref[...] = unstack_heads(contract_rows(keys, grad_scores)).astype(jnp.bfloat16)
+    grad_queries = unstack_heads(contract_rows(keys, grad_scores))
+    dq_ref[...] = (grad_queries * (1.0 / math.sqrt(HEAD_DIM))).astype(jnp.bfloat16)
     dk_acc[here, :] += dot32(grad_scores, queries)
     dv_acc[here, :] += dot32(probs.astype(jnp.bfloat16), grads)
 
@@ -429,6 +430,467 @@
     )(queries, keys, values, key_docs, query_docs, grads, logs_in)
 
 
+def half_cols(position, half):
+    return pl.ds(pl.multiple_of(position * half, half), half)
+
+
+def add_or_set(first, ref, index, terms):
+    @pl.when(first)
+    def _():
+        ref[index] = terms
+
+    @pl.when(jnp.logical_not(first))
+    def _():
+        ref[index] += terms
+
+
+def ffn_kernel(
+    place_ref, hb_ref, up_ref, down_ref, bias_ref, acts_ref, slope_ref, own_ref, other_ref, total
+):
+    step = pl.program_id(0)
+    half = up_ref.shape[3]
+    count = own_ref.shape[0]
+    near, far = half_cols(place_ref[1], half), half_cols(1 - place_ref[1], half)
+    pre_act = dot32(hb_ref[:, near], up_ref[0, 0]) + dot32(hb_ref[:, far], up_ref[0, 1])
+    pre_act += bias_ref[0]
+    cdf = 0.5 * (1.0 + lax.erf(pre_act * math.sqrt(0.5)))
+    bell = jnp.exp(-0.5 * pre_act * pre_act) * (1.0 / math.sqrt(2 * math.pi))
+    acts = (pre_act * cdf).astype(jnp.bfloat16)
+    acts_ref[...] = acts
+    slope_ref[...] = (cdf + pre_act * bell).astype(jnp.bfloat16)
+    add_or_set(step == 0, total, (slice(None), near), dot32(acts, down_ref[0, 0]))
+    add_or_set(step == 0, total, (slice(None), far), dot32(acts, down_ref[0, 1]))
+
+    @pl.when(step == pl.num_programs(0) - 1)
+    def _():
+        own_ref[...] = total[:count]
+        other_ref[...] = total[count:].astype(jnp.bfloat16)
+
+
+def ffn_back_kernel(
+    place_ref,
+    dz_ref,
+    hb_ref,
+    acts_ref,
+    slope_ref,
+    up_ref,
+    down_ref,
+    own_ref,
+    other_ref,
+    up_ref_out,
+    down_ref_out,
+    sums_ref,
+    total,
+):
+    step = pl.program_id(0)
+    half = up_ref.shape[3]
+    count = own_ref.shape[0]
+    near, far = half_cols(place_ref[1], half), half_cols(1 - place_ref[1], half)
+    grad_acts = contract_last(dz_ref[:, near], down_ref[0, 0])
+    grad_acts += contract_last(dz_ref[:, far], down_ref[0, 1])
+    grad_pre = (slope_ref[...].astype(jnp.float32) * grad_acts).astype(jnp.bfloat16)
+    sums_ref[0] = jnp.sum(grad_pre.astype(jnp.float32), axis=0, keepdims=True)
+    add_or_set(step == 0, total, (slice(None), near), contract_last(grad_pre, up_ref[0, 0]))
+    add_or_set(step == 0, total, (slice(None), far), contract_last(grad_pre, up_ref[0, 1]))
+    for side, cols in enumerate((near, far)):
+        up_grad = contract_rows(hb_ref[:, cols], grad_pre).astype(jnp.bfloat16)
+        down_grad = contract_rows(acts_ref[...], dz_ref[:, cols]).astype(jnp.bfloat16)
+        for x, place in enumerate((place_ref[3], 1 - place_ref[3])):
+            rows = slice(x * half // 2, (x + 1) * half // 2)
+            up_ref_out[place, side, 0] = up_grad[rows]
+            down_ref_out[side, place, 0] = down_grad[rows]
+
+    @pl.when(step == pl.num_programs(0) - 1)
+    def _():
+        own_ref[...] = total[:count]
+        other_ref[...] = total[count:].astype(jnp.bfloat16)
+
+
+def whole(shape):
+    return pl.BlockSpec(shape, lambda *_: (0,) * len(shape))
+
+
+def ffn(place, rows, weights, bias):
+    both, width = rows.shape
+    tps, shards, _, half = weights.shape
+    count = both // 2
+    matrix = (1, shards, half, half)
+    block = pl.BlockSpec((both, half), lambda i, _: (0, i))
+    return pl.pallas_call(
+        ffn_kernel,
+        grid_spec=pltpu.PrefetchScalarGridSpec(
+            num_scalar_prefetch=1,
+            grid=(tps,),
+            in_specs=[
+                whole((both, width)),
+                pl.BlockSpec(matrix, lambda i, _: (i, 0, 0, 0)),
+                pl.BlockSpec(matrix, lambda i, _: (i, 0, 1, 0)),
+                pl.BlockSpec((1, 1, half), lambda i, _: (i, 0, 0)),
+            ],
+            out_specs=[block, block, whole((count, width)), whole((count, width))],
+            scratch_shapes=[pltpu.VMEM((both, width), jnp.float32)],
+        ),
+        out_shape=[
+            jax.ShapeDtypeStruct((both, tps * half), jnp.bfloat16),
+            jax.ShapeDtypeStruct((both, tps * half), jnp.bfloat16),
+            jax.ShapeDtypeStruct((count, width), jnp.float32),
+            jax.ShapeDtypeStruct((count, width), jnp.bfloat16),
+        ],
+        compiler_params=pltpu.CompilerParams(vmem_limit_bytes=40 << 20),
+        cost_estimate=pl.CostEstimate(
+            flops=12 * both * width * tps * half, bytes_accessed=12 << 20, transcendentals=0
+        ),
+        name="ffn",
+    )(place, rows, weights, weights, bias)
+
+
+def ffn_back(place, grads, rows, acts, slope, weights):
+    both, width = rows.shape
+    tps, shards, _, half = weights.shape
+    count = both // 2
+    matrix = (1, shards, half, half)
+    block = pl.BlockSpec((both, half), lambda i, _: (0, i))
+
+    def source(i, place_ref):
+        return (place_ref[2] + tps - i) % tps
+
+    parts = pl.BlockSpec(
+        (2, 2, 1, half // 2, half), lambda i, at: (0, 0, source(i, at), 0, 0)
+    )
+    return pl.pallas_call(
+        ffn_back_kernel,
+        grid_spec=pltpu.PrefetchScalarGridSpec(
+            num_scalar_prefetch=1,
+            grid=(tps,),
+            in_specs=[
+                whole((both, width)),
+                whole((both, width)),
+                block,
+                block,
+                pl.BlockSpec(matrix, lambda i, _: (i, 0, 0, 0)),
+                pl.BlockSpec(matrix, lambda i, _: (i, 0, 1, 0)),
+            ],
+            out_specs=[
+                whole((count, width)),
+                whole((count, width)),
+                parts,
+                parts,
+                pl.BlockSpec((1, 1, half), lambda i, at: (source(i, at), 0, 0)),
+            ],
+            scratch_shapes=[pltpu.VMEM((both, width), jnp.float32)],
+        ),
+        out_shape=[
+            jax.ShapeDtypeStruct((count, width), jnp.float32),
+            jax.ShapeDtypeStruct((count, width), jnp.bfloat16),
+            jax.ShapeDtypeStruct((2, 2, tps, half // 2, half), jnp.bfloat16),
+            jax.ShapeDtypeStruct((2, 2, tps, half // 2, half), jnp.bfloat16),
+            jax.ShapeDtypeStruct((tps, 1, half), jnp.float32),
+        ],
+        compiler_params=pltpu.CompilerParams(vmem_limit_bytes=48 << 20),
+        cost_estimate=pl.CostEstimate(
+            flops=12 * both * width * tps * half, bytes_accessed=20 << 20, transcendentals=0
+        ),
+        name="ffn_back",
+    )(place, grads, rows, acts, slope, weights, weights)
+
+
+def project_kernel(
+    place_ref, w_mine, w_other, x_mine, x_other, bias_ref, q_ref, k_ref, v_ref, x_ref, wt
+):
+    core, shard, tp, across, start = (place_ref[i] for i in range(5))
+    depth = w_mine.shape[3]
+    width = x_ref.shape[1]
+    part = width // 8
+    length = 4 * x_mine.shape[2]
+    reach = length // 2
+    for c, source in enumerate((w_mine, w_other)):
+        for y in (0, 1):
+            cols = half_cols(shard + y - 2 * shard * y, depth)
+            for k in range(4):
+                row = ((tp + 4 - k) & 3) * 2 + core + c - 2 * core * c
+                rows = pl.ds(pl.multiple_of(row * part, part), part)
+                for m in range(3):
+                    wt[m, rows, cols] = source[y, k, m * part : (m + 1) * part]
+    for i in range(x_ref.shape[0] // QBLOCK):
+        row = start - reach + i * QBLOCK
+        inside = jnp.logical_and(row >= 0, row < 2 * length)
+        at = jnp.where(inside, row, 0) // QBLOCK
+        seq, block, piece = at // 8, (at // 2) & 3, at & 1
+        here = jnp.where((block >> 1) == across, 0, 1)
+        rows = pl.ds(pl.multiple_of(piece * QBLOCK, QBLOCK), QBLOCK)
+        mine, other = x_mine[here, seq, rows], x_other[here, seq, rows]
+        found = jnp.where((block & 1) == core, mine, other)
+        x_ref[i * QBLOCK : (i + 1) * QBLOCK] = jnp.where(inside, found, jnp.zeros_like(found))
+    count = q_ref.shape[0]
+    scaled = contract_last(x_ref[reach : reach + count], wt[0]) + bias_ref[0:1]
+    q_ref[...] = (scaled * (1.0 / math.sqrt(HEAD_DIM))).astype(jnp.bfloat16)
+    chunk = x_ref.shape[0] // 4
+
+    @pl.loop(0, 4)
+    def _(step):
+        rows = pl.ds(pl.multiple_of(step * chunk, 32), chunk)
+        k_ref[rows] = contract_last(x_ref[rows], wt[1]).astype(jnp.bfloat16)
+        v_ref[rows] = (contract_last(x_ref[rows], wt[2]) + bias_ref[1:2]).astype(jnp.bfloat16)
+
+
+def project(place, w_mine, w_other, x_mine, x_other, biases, count, window):
+    width = x_mine.shape[-1]
+    return pl.pallas_call(
+        project_kernel,
+        in_specs=[pl.BlockSpec(memory_space=pltpu.SMEM)]
+        + [pl.BlockSpec(memory_space=pltpu.VMEM)] * 5,
+        out_specs=[pl.BlockSpec(memory_space=pltpu.VMEM)] * 5,
+        out_shape=[
+            jax.ShapeDtypeStruct((count, width), jnp.bfloat16),
+            jax.ShapeDtypeStruct((window, width), jnp.bfloat16),
+            jax.ShapeDtypeStruct((window, width), jnp.bfloat16),
+            jax.ShapeDtypeStruct((window, width), jnp.bfloat16),
+            jax.ShapeDtypeStruct((3, width, width), jnp.bfloat16),
+        ],
+        compiler_params=pltpu.CompilerParams(vmem_limit_bytes=40 << 20),
+        cost_estimate=pl.CostEstimate(
+            flops=4 * window * width * width, bytes_accessed=16 << 20, transcendentals=0
+        ),
+        name="project",
+    )(place, w_mine, w_other, x_mine, x_other, biases)
+
+
+def norm_pieces(resid):
+    center = resid - jnp.mean(resid, axis=-1, keepdims=True)
+    inv_std = lax.rsqrt(jnp.mean(center * center, axis=-1, keepdims=True) + eps_norm)
+    return center * inv_std, inv_std
+
+
+def norm_pull(grad_out, normed, inv_std, gain):
+    grad_normed = grad_out * gain
+    return inv_std * (
+        grad_normed
+        - jnp.mean(grad_normed, axis=-1, keepdims=True)
+        - normed * jnp.mean(grad_normed * normed, axis=-1, keepdims=True)
+    )
+
+
+def row_sum(rows):
+    return jnp.sum(rows, axis=0, keepdims=True)
+
+
+def attend_out_kernel(
+    place_ref, o_ref, x_ref, w_mine, w_other, vec_ref, h_ref, hb_ref, n_ref, i_ref, wo_ref
+):
+    core, shard, tp = (place_ref[i] for i in range(3))
+    part, depth = w_mine.shape[2:]
+    for c, source in enumerate((w_mine, w_other)):
+        for y in (0, 1):
+            cols = half_cols(shard + y - 2 * shard * y, depth)
+            for k in range(4):
+                row = ((tp + 4 - k) & 3) * 2 + core + c - 2 * core * c
+                rows = pl.ds(pl.multiple_of(row * part, part), part)
+                wo_ref[rows, cols] = source[k, y]
+    resid = x_ref[...].astype(jnp.float32) + dot32(o_ref[...], wo_ref[...]) + vec_ref[0:1]
+    normed, inv_std = norm_pieces(resid)
+    hidden = normed * vec_ref[1:2] + vec_ref[2:3]
+    h_ref[...] = hidden
+    hb_ref[...] = hidden.astype(jnp.bfloat16)
+    n_ref[...] = normed
+    i_ref[...] = jnp.broadcast_to(inv_std, i_ref.shape)
+
+
+def attend_out(place, mixed, rows, w_mine, w_other, vectors):
+    count, width = mixed.shape
+    vmem = pl.BlockSpec(memory_space=pltpu.VMEM)
+    return pl.pallas_call(
+        attend_out_kernel,
+        in_specs=[pl.BlockSpec(memory_space=pltpu.SMEM)] + [vmem] * 5,
+        out_specs=[vmem] * 5,
+        out_shape=[
+            jax.ShapeDtypeStruct((count, width), jnp.float32),
+            jax.ShapeDtypeStruct((count, width), jnp.bfloat16),
+            jax.ShapeDtypeStruct((count, width), jnp.float32),
+            jax.ShapeDtypeStruct((count, QBLOCK), jnp.float32),
+            jax.ShapeDtypeStruct((width, width), jnp.bfloat16),
+        ],
+        compiler_params=pltpu.CompilerParams(vmem_limit_bytes=40 << 20),
+        cost_estimate=pl.CostEstimate(
+            flops=2 * count * width * width, bytes_accessed=8 << 20, transcendentals=0
+        ),
+        name="attend_out",
+    )(place, mixed, rows, w_mine, w_other, vectors)
+
+
+def ffn_norm_kernel(h_ref, own_ref, got_ref, g_ref, vec_ref, y_ref, dr_ref, dz_ref, sums_ref):
+    resid = h_ref[...] + own_ref[...] + got_ref[...].astype(jnp.float32) + vec_ref[0:1]
+    normed, inv_std = norm_pieces(resid)
+    y_ref[...] = (normed * vec_ref[1:2] + vec_ref[2:3]).astype(jnp.bfloat16)
+    grad_out = g_ref[...].astype(jnp.float32)
+    grad = norm_pull(grad_out, normed, inv_std, vec_ref[1:2])
+    low = grad.astype(jnp.bfloat16)
+    dr_ref[...] = grad
+    dz_ref[...] = low
+    sums_ref[0:1] = row_sum(low.astype(jnp.float32))
+    sums_ref[1:2] = row_sum(grad_out * normed)
+    sums_ref[2:3] = row_sum(grad_out)
+
+
+def ffn_norm(hidden, own, got, cots, vectors):
+    count, width = hidden.shape
+    vmem = pl.BlockSpec(memory_space=pltpu.VMEM)
+    return pl.pallas_call(
+        ffn_norm_kernel,
+        in_specs=[vmem] * 5,
+        out_specs=[vmem] * 4,
+        out_shape=[
+            jax.ShapeDtypeStruct((count, width), jnp.bfloat16),
+            jax.ShapeDtypeStruct((count, width), jnp.float32),
+            jax.ShapeDtypeStruct((count, width), jnp.bfloat16),
+            jax.ShapeDtypeStruct((3, width), jnp.float32),
+        ],
+        compiler_params=pltpu.CompilerParams(vmem_limit_bytes=40 << 20),
+        cost_estimate=pl.CostEstimate(
+            flops=30 * count * width, bytes_accessed=7 << 20, transcendentals=0
+        ),
+        name="ffn_norm",
+    )(hidden, own, got, cots, vectors)
+
+
+def attend_norm_kernel(
+    dr_ref, own_ref, got_ref, n_ref, i_ref, vec_ref, wo_ref, out_ref, da_ref, do_ref, sums_ref
+):
+    grad_out = dr_ref[...] + own_ref[...] + got_ref[...].astype(jnp.float32)
+    normed = n_ref[...]
+    grad = norm_pull(grad_out, normed, i_ref[:, :1], vec_ref[1:2])
+    low = grad.astype(jnp.bfloat16)
+    out_ref[...] = grad
+    da_ref[...] = low
+    do_ref[...] = contract_last(low, wo_ref[...]).astype(jnp.bfloat16)
+    sums_ref[0:1] = row_sum(low.astype(jnp.float32))
+    sums_ref[1:2] = row_sum(grad_out * normed)
+    sums_ref[2:3] = row_sum(grad_out)
+
+
+def attend_norm(grads, own, got, normed, inv_std, vectors, weights):
+    count, width = grads.shape
+    vmem = pl.BlockSpec(memory_space=pltpu.VMEM)
+    return pl.pallas_call(
+        attend_norm_kernel,
+        in_specs=[vmem] * 7,
+        out_specs=[vmem] * 4,
+        out_shape=[
+            jax.ShapeDtypeStruct((count, width), jnp.float32),
+            jax.ShapeDtypeStruct((count, width), jnp.bfloat16),
+            jax.ShapeDtypeStruct((count, width), jnp.bfloat16),
+            jax.ShapeDtypeStruct((3, width), jnp.float32),
+        ],
+        compiler_params=pltpu.CompilerParams(vmem_limit_bytes=40 << 20),
+        cost_estimate=pl.CostEstimate(
+            flops=2 * count * width * width, bytes_accessed=9 << 20, transcendentals=0
+        ),
+        name="attend_norm",
+    )(grads, own, got, normed, inv_std, vectors, weights)
+
+
+def attn_grads_kernel(
+    place_ref, dq_ref, dk_ref, dv_ref, o_ref, da_ref, x_ref, w_ref, sums_ref, parts_ref
+):
+    core, shard, across = place_ref[0], place_ref[1], place_ref[3]
+    depth = parts_ref.shape[5]
+    part = depth // 4
+    sides = (
+        (dq_ref, x_ref),
+        (dk_ref, w_ref),
+        (dv_ref, w_ref),
+        (o_ref, da_ref),
+    )
+    for m, (left, right) in enumerate(sides):
+        grad = contract_rows(left[...], right[...]).astype(jnp.bfloat16)
+        group = across if m < 2 else 1 - across
+        rows = slice((m % 2) * part, (m % 2 + 1) * part)
+        for z in (0, 1):
+            for c in (0, 1):
+                piece = grad[(2 * z + c) * part : (2 * z + c + 1) * part]
+                to = c + core - 2 * c * core
+                parts_ref[to, group, shard, z, rows] = piece[:, :depth]
+                parts_ref[to, group, 1 - shard, z, rows] = piece[:, depth:]
+    extra = sums_ref.shape[3]
+    for c in (0, 1):
+        for y in (0, 1):
+            parts_ref[c, across, y, :, 2 * part :] = sums_ref[c, 0]
+            parts_ref[c, 1 - across, y, :, 2 * part :] = sums_ref[c, 1]
+
+
+def attn_grads(place, grad_queries, grad_keys, grad_values, mixed, grad_attn, rows, near, sums):
+    count, width = rows.shape
+    window = near.shape[0]
+    depth = width // 2
+    extra = sums.shape[3]
+    high = depth // 2 + extra
+    cols = pl.BlockSpec((count, depth), lambda i, _: (0, i))
+    near_cols = pl.BlockSpec((window, depth), lambda i, _: (0, i))
+    return pl.pallas_call(
+        attn_grads_kernel,
+        grid_spec=pltpu.PrefetchScalarGridSpec(
+            num_scalar_prefetch=1,
+            grid=(2,),
+            in_specs=[
+                cols,
+                near_cols,
+                near_cols,
+                cols,
+                whole((count, width)),
+                whole((count, width)),
+                whole((window, width)),
+                pl.BlockSpec((2, 2, 2, extra, depth), lambda i, _: (0, 0, i, 0, 0)),
+            ],
+            out_specs=pl.BlockSpec((2, 2, 2, 2, high, depth), lambda i, _: (0, 0, 0, i, 0, 0)),
+        ),
+        out_shape=jax.ShapeDtypeStruct((2, 2, 2, 4, high, depth), jnp.bfloat16),
+        compiler_params=pltpu.CompilerParams(vmem_limit_bytes=48 << 20),
+        cost_estimate=pl.CostEstimate(
+            flops=4 * (window + count) * width * width, bytes_accessed=16 << 20, transcendentals=0
+        ),
+        name="attn_grads",
+    )(place, grad_queries, grad_keys, grad_values, mixed, grad_attn, rows, near, sums)
+
+
+def span_grads_kernel(
+    place_ref, dq_ref, dk_ref, dv_ref, w_ref, base_ref, own_ref, onward_ref, give_ref
+):
+    core = place_ref[0]
+    count, reach = own_ref.shape[0], give_ref.shape[0]
+
+    def near(rows):
+        return dot32(dk_ref[rows], w_ref[1]) + dot32(dv_ref[rows], w_ref[2])
+
+    far = count + reach
+    low = pl.ds(pl.multiple_of(core * far, QBLOCK), reach)
+    high = pl.ds(pl.multiple_of((1 - core) * far, QBLOCK), reach)
+    give_ref[...] = near(high).astype(jnp.bfloat16)
+    onward_ref[...] = near(low).astype(jnp.bfloat16)
+    own_ref[...] = base_ref[...] + dot32(dq_ref[...], w_ref[0]) + near(pl.ds(reach, count))
+
+
+def span_grads(place, grad_queries, grad_keys, grad_values, weights, base):
+    count, width = base.shape
+    reach = (grad_keys.shape[0] - count) // 2
+    vmem = pl.BlockSpec(memory_space=pltpu.VMEM)
+    return pl.pallas_call(
+        span_grads_kernel,
+        in_specs=[pl.BlockSpec(memory_space=pltpu.SMEM)] + [vmem] * 5,
+        out_specs=[vmem] * 3,
+        out_shape=[
+            jax.ShapeDtypeStruct((count, width), jnp.float32),
+            jax.ShapeDtypeStruct((reach, width), jnp.bfloat16),
+            jax.ShapeDtypeStruct((reach, width), jnp.bfloat16),
+        ],
+        compiler_params=pltpu.CompilerParams(vmem_limit_bytes=40 << 20),
+        cost_estimate=pl.CostEstimate(
+            flops=4 * (count + 2 * reach) * width * width,
+            bytes_accessed=12 << 20,
+            transcendentals=0,
+        ),
+        name="span_grads",
+    )(place, grad_queries, grad_keys, grad_values, weights, base)
+
+
 def ctx_swap(array, bit):
     return lax.ppermute(array, "ctx", [(i, i ^ bit) for i in range(4)])
 
@@ -437,6 +899,10 @@
     return ctx_swap(array, 1)
 
 
+def tie(*arrays):
+    return lax.optimization_barrier(arrays)
+
+
 def across_swap(array):
     return ctx_swap(array, 2)
 
@@ -445,10 +911,53 @@
     return jnp.where(flag == 0, mine, other), jnp.where(flag == 0, other, mine)
 
 
+def at(across, core, tp):
+    return (2 * across + core) * 4 + tp
+
+
+def across_pairs():
+    pairs = []
+    for tp in range(4):
+        for across in (0, 1):
+            core = across ^ (tp & 1)
+            pairs.append((at(1 - across, core, tp), at(across, core, tp)))
+    return pairs
+
+
+def tp_shifts(array):
+    return [
+        lax.ppermute(array, "tp", [(i, (i + shift) % 4) for i in range(4)]) for shift in (1, 2, 3)
+    ]
+
+
+def by_tp(array, shifted):
+    one, two, three = shifted
+    line = jnp.stack([three, two, one, array, three, two, one])
+    return lax.dynamic_slice_in_dim(line, 3 - lax.axis_index("tp"), 4, 0)
+
+
+def shard_swap(array):
+    return lax.ppermute(array, "shard", [(0, 1), (1, 0)])
+
+
+def low_sum(left, right):
+    return (left.astype(jnp.float32) + right.astype(jnp.float32)).astype(jnp.bfloat16)
+
+
+def scatter_tp_start(parts):
+    tp = lax.axis_index("tp")
+    moved = [lax.dynamic_index_in_dim(parts, tp, 0, keepdims=False)]
+    for shift in (1, 2, 3):
+        sent = lax.dynamic_index_in_dim(parts, (tp + shift) & 3, 0, keepdims=False)
+        moved.append(lax.ppermute(sent, "tp", [(i, (i + shift) % 4) for i in range(4)]))
+    return moved
+
+
+def scatter_tp_end(moved):
+    return sum(part.astype(jnp.float32) for part in moved).astype(jnp.bfloat16)
+
+
 def chain_pairs():
-    def at(across, core, tp):
-        return (2 * across + core) * 4 + tp
-
     pairs = []
     for group in (0, 2):
         path = [(0, group), (0, group + 1), (1, group + 1), (1, group)]
@@ -483,28 +992,27 @@
     reach = length // 2
     count = seqs * block // 4
     window = count + 2 * reach
-    scale = 1.0 / math.sqrt(HEAD_DIM)
     bf16, f32 = jnp.bfloat16, jnp.float32
     ctx, tp = lax.axis_index("ctx"), lax.axis_index("tp")
+    shard = lax.axis_index("shard")
     core, across, side = ctx & 1, ctx >> 1, tp & 1
     place = 2 * across + (side ^ across)
     odd = across ^ side
-    both = ("tp", "shard")
-
-    half = query_proj.shape[0] // 2
+
+    heads = query_proj.shape[1]
+    half = heads // 2
+    depth = query_proj.shape[0]
+    cut = up_proj.shape[1] // 2
     own_in = lax.dynamic_slice_in_dim(
-        jnp.concatenate([query_proj, key_proj, value_proj], axis=1), core * half, half, 0
-    )
-    in_mine = lax.all_gather(own_in, both, axis=0, tiled=False)
-    in_lo, in_hi = in_order(core, in_mine, core_swap(in_mine))
-    heads = query_proj.shape[1]
-    joined = jnp.stack(
-        [in_lo.reshape(4, 2, half, 3, heads), in_hi.reshape(4, 2, half, 3, heads)], axis=2
-    )
-    joined = joined.transpose(4, 1, 2, 3, 0, 5).reshape(3, width, 4 * heads)
-    full_query, full_key, full_value = joined[0], joined[1], joined[2]
-
-    cut = up_proj.shape[1] // 2
+        jnp.stack([query_proj.T, key_proj.T, value_proj.T]), core * half, half, 1
+    ).reshape(3 * half, depth)
+    own_biases = jnp.stack(
+        [
+            jnp.concatenate([query_bias, value_bias]),
+            lax.dynamic_slice_in_dim(up_bias, core * cut, cut, 0),
+        ]
+    )
+    own_in = jnp.concatenate([own_in, own_biases, jnp.zeros((14, depth), bf16)], axis=0)
     out_half = out_proj.shape[0] // 2
     own_rest = jnp.concatenate(
         [
@@ -514,39 +1022,25 @@
         ],
         axis=0,
     )
-    rest = lax.all_gather(own_rest, both, axis=0, tiled=False).reshape(4, 2, -1, cut)
-    up_here = rest[:, :, :cut].transpose(1, 2, 0, 3).reshape(width, 4 * cut)
-    down_here = rest[:, :, cut : 2 * cut].transpose(0, 2, 1, 3).reshape(4 * cut, width)
-    out_mine = rest[:, :, 2 * cut :]
-    out_lo, out_hi = in_order(core, out_mine, core_swap(out_mine))
-    full_out = (
-        jnp.stack([out_lo, out_hi], axis=1).transpose(0, 1, 3, 2, 4).reshape(width, width)
-    )
-    biases = lax.all_gather(
-        jnp.concatenate(
-            [query_bias, value_bias, lax.dynamic_slice_in_dim(up_bias, core * cut, cut, 0)]
-        ),
-        "tp",
-        axis=0,
-        tiled=False,
-    )
-    full_query_bias = biases[:, :heads].reshape(-1)
-    full_value_bias = biases[:, heads : 2 * heads].reshape(-1)
-    up_bias_here = biases[:, 2 * heads :].reshape(-1)
-
     first_seq = 3 * (tp >> 1)
     mine = lax.dynamic_slice_in_dim(layer_input, first_seq + across, 2, 0)
     theirs = across_swap(lax.dynamic_slice_in_dim(layer_input, first_seq + 1 - across, 2, 0))
+    in_shifted = tp_shifts(own_in)
+    rest_far = [shard_swap(own_rest)]
+    *in_shifted, theirs, rest_far[0] = tie(*in_shifted, theirs, rest_far[0])
+    in_near = jnp.stack([own_in] + in_shifted)
+    rest_near = [own_rest] + tp_shifts(tie(own_rest, in_near)[0])
+    in_far, rest_near[1] = tie(shard_swap(in_near), rest_near[1])
+    in_mine = jnp.stack([in_near, in_far])
+    in_other = core_swap(in_mine)
+    bias_rows = in_mine[0, :, 3 * half]
+    in_biases = by_tp(bias_rows[0], [bias_rows[1], bias_rows[2], bias_rows[3]]).astype(f32)
+    in_biases = jnp.stack([in_biases[:, :heads].reshape(-1), in_biases[:, heads:].reshape(-1)])
+    up_bias_here = in_mine[0, :, 3 * half + 1].reshape(4, 1, cut).astype(f32)
+
     pair = jnp.stack([mine, theirs])
-    pair_lo, pair_hi = in_order(core, pair, core_swap(pair))
-    quads = jnp.stack([pair_lo, pair_hi], axis=1)
-    quads = jnp.where(across == 0, quads, quads[::-1])
-    near = quads.transpose(2, 0, 1, 3, 4).reshape(2 * length, width)
+    pair_other = core_swap(pair)
     start = 2 * count * place + count * core - length * across
-    edge = jnp.zeros((reach, width), bf16)
-    in_window = lax.dynamic_slice_in_dim(
-        jnp.concatenate([edge, near, edge], axis=0), start, window, 0
-    )
     ids = lax.dynamic_slice_in_dim(segment_ids, first_seq + across, 2, 0)
     ids = (ids + jnp.array([[0], [1 << 16]], jnp.int32)).reshape(-1)
     no_doc = jnp.full((reach,), -1, jnp.int32)
@@ -555,33 +1049,29 @@
     )
     key_docs = jnp.broadcast_to(window_docs[:, None], (window, QBLOCK))
     query_docs = window_docs[reach : reach + count].reshape(-1, 1, QBLOCK)
+
+    place = jnp.stack([core, shard, tp, across, start])
+    far_one = shard_swap(rest_near[1])
+    queries, keys, values, in_window, weights_t = project(
+        place, in_mine, in_other, pair, pair_other, in_biases, count, window
+    )
     rows_in = in_window[reach : reach + count]
-
-    queries = ((dot32(rows_in, full_query) + full_query_bias) * scale).astype(bf16)
-    keys = dot32(in_window, full_key).astype(bf16)
-    values = (dot32(in_window, full_value) + full_value_bias).astype(bf16)
+    queries, rest_near[3], far_one = tie(queries, rest_near[3], far_one)
+    far_three = shard_swap(rest_near[3])
     mixed, logs = attend(queries, keys, values, key_docs, query_docs, reach)
-    attended = dot32(mixed, full_out) + out_bias
-    hidden, normed_one, inv_one = norm_forward(
-        rows_in.astype(f32) + attended, attn_gain, attn_shift
-    )
-    hidden_low = hidden.astype(bf16)
-    hidden_both = jnp.concatenate(in_order(core, hidden_low, core_swap(hidden_low)), axis=0)
-    pre_act = dot32(hidden_both, up_here) + up_bias_here
-    cdf = 0.5 * (1.0 + lax.erf(pre_act * math.sqrt(0.5)))
-    acts_low = (pre_act * cdf).astype(bf16)
-    slope = cdf + pre_act * (jnp.exp(-0.5 * pre_act * pre_act) * (1.0 / math.sqrt(2 * math.pi)))
-
-    def chip_sum(partial_rows):
-        low, high = partial_rows[:count], partial_rows[count:]
-        keep = jnp.where(core == 0, low, high)
-        give = jnp.where(core == 0, high, low).astype(bf16)
-        return keep + core_swap(give).astype(f32)
-
-    ffn_out = chip_sum(dot32(acts_low, down_here)) + down_bias
-    output_rows, normed_two, inv_two = norm_forward(hidden + ffn_out, ffn_gain, ffn_shift)
-
-    def deliver(rows):
+    mixed, far_three, rest_near[2] = tie(mixed, far_three, rest_near[2])
+    far_two = shard_swap(rest_near[2])
+    rest_far += [far_one, far_two, far_three]
+    rest = jnp.stack([jnp.stack(both) for both in zip(rest_near, rest_far)])
+    out_mine = rest[:, :, 2 * cut :]
+    attn_vectors = jnp.stack([out_bias, attn_gain, attn_shift]).astype(f32)
+    hidden, hidden_low, normed_one, inv_one, full_out = attend_out(
+        place, mixed, rows_in, out_mine, core_swap(out_mine), attn_vectors
+    )
+    hidden_both = jnp.concatenate([hidden_low, core_swap(hidden_low)], axis=0)
+    acts, slope, ffn_own, ffn_other = ffn(place, hidden_both, rest, up_bias_here)
+
+    def deliver_start(rows):
         chip = jnp.concatenate(in_order(core, rows, core_swap(rows)), axis=0)
         kept = lax.dynamic_slice_in_dim(chip, odd * block + core * block, block, 0)
         half_block = block // 2
@@ -589,7 +1079,10 @@
             chip, (1 - odd) * 2 * block + core * half_block, half_block, 0
         )
         packed = jnp.concatenate([kept, across_swap(sent)], axis=0)
-        every = lax.all_gather(packed, "tp", axis=0, tiled=False)
+        return packed, tp_shifts(packed)
+
+    def deliver_end(packed, shifted):
+        every = by_tp(packed, shifted)
         halves = every[:, block:]
         lo, hi = in_order(core, halves, core_swap(halves))
         moved = jnp.concatenate([lo, hi], axis=1)
@@ -606,141 +1099,164 @@
             ]
         return jnp.stack(parts)
 
-    layer_output = deliver(output_rows.astype(bf16))
-
-    cot_mine = lax.dynamic_slice_in_dim(out_cotangent, first_seq + across, 2, 0)
-    cot_theirs = across_swap(
-        lax.dynamic_slice_in_dim(out_cotangent, first_seq + 1 - across, 2, 0)
-    )
-    cot_pair = jnp.stack([cot_mine, cot_theirs])
-    cot_lo, cot_hi = in_order(core, cot_pair, core_swap(cot_pair))
-    cots = jnp.stack([cot_lo, cot_hi], axis=1)
-    cots = jnp.where(across == 0, cots, cots[::-1])
-    cots = cots.transpose(2, 0, 1, 3, 4).reshape(2 * length, width)
-    grad_out = lax.dynamic_slice_in_dim(cots, start, count, 0).astype(f32)
-
-    grad_two, ffn_gain_grad, ffn_shift_grad = norm_backward(grad_out, normed_two, inv_two, ffn_gain)
-    grad_ffn = grad_two.astype(bf16)
-    down_bias_grad = jnp.sum(grad_ffn, axis=0, dtype=f32)
-    grad_ffn_both = jnp.concatenate(in_order(core, grad_ffn, core_swap(grad_ffn)), axis=0)
-    down_part = contract_rows(acts_low, grad_ffn_both)
-    grad_pre = (slope * contract_last(grad_ffn_both, down_here)).astype(bf16)
-    up_bias_part = jnp.sum(grad_pre, axis=0, dtype=f32)
-    up_part = contract_rows(hidden_both, grad_pre)
-    grad_hidden = grad_two + chip_sum(contract_last(grad_pre, up_here))
-    grad_one, attn_gain_grad, attn_shift_grad = norm_backward(
-        grad_hidden, normed_one, inv_one, attn_gain
-    )
-    grad_attn = grad_one.astype(bf16)
-    out_bias_grad = jnp.sum(grad_attn, axis=0, dtype=f32)
-    out_part = contract_rows(mixed, grad_attn).astype(bf16)
-    grad_mixed = contract_last(grad_attn, full_out).astype(bf16)
-    grad_queries, grad_keys, grad_values = attend_back(
+    near_cot = lax.dynamic_index_in_dim(
+        out_cotangent, first_seq + odd + across, 0, keepdims=False
+    )
+    far_cot = lax.ppermute(
+        lax.dynamic_index_in_dim(out_cotangent, first_seq + 2 - 2 * across, 0, keepdims=False),
+        ("ctx", "tp"),
+        across_pairs(),
+    )
+    cot_pair = jnp.stack([near_cot, far_cot])
+    cot_swapped = core_swap(cot_pair)
+    low_cot, high_cot = in_order(core, near_cot, cot_swapped[0])
+    far_cot = jnp.where(core == odd, far_cot, cot_swapped[1])
+    chip_cot = jnp.where(
+        odd == 0,
+        jnp.concatenate([low_cot, high_cot, far_cot], axis=0),
+        jnp.concatenate([far_cot, low_cot, high_cot], axis=0),
+    )
+    cot_rows = lax.dynamic_slice_in_dim(chip_cot, core * count, count, 0)
+
+
+    ffn_vectors = jnp.stack([down_bias, ffn_gain, ffn_shift]).astype(f32)
+    output_rows, grad_two, grad_ffn, ffn_sums = ffn_norm(
+        hidden, ffn_own, core_swap(ffn_other), cot_rows, ffn_vectors
+    )
+    grad_ffn_both = jnp.concatenate([grad_ffn, core_swap(grad_ffn)], axis=0)
+    out_packed, out_shifted = deliver_start(output_rows)
+    grad_ffn_both, out_packed = lax.optimization_barrier((grad_ffn_both, out_packed))
+    back_own, back_other, up_parts, down_parts, up_sums = ffn_back(
+        place, grad_ffn_both, hidden_both, acts, slope, rest
+    )
+    back_own, out_shifted[0] = tie(back_own, out_shifted[0])
+    grad_one, grad_attn, grad_mixed, attn_sums = attend_norm(
+        grad_two, back_own, core_swap(back_other), normed_one, inv_one, attn_vectors, full_out
+    )
+    up_got = across_swap(up_parts[1])
+    down_got = shard_swap(down_parts[1])
+    grad_scaled, grad_keys, grad_values = attend_back(
         queries, keys, values, key_docs, query_docs, grad_mixed, logs, reach
     )
-    grad_scaled = grad_queries * bf16(scale)
-    grad_near = (contract_last(grad_keys, full_key) + contract_last(grad_values, full_value)).astype(
-        bf16
-    )
-    give = jnp.where(core == 0, grad_near[count + reach :], grad_near[:reach])
-    keep = jnp.where(core == 0, grad_near[: count + reach], grad_near[reach:]).astype(f32)
-    got = core_swap(give[: 2 * reach]).astype(f32)
+    grad_keys, grad_values, up_got, down_got = tie(grad_keys, grad_values, up_got, down_got)
+    up_parts = low_sum(up_parts[0], up_got)
+    down_parts = low_sum(down_parts[0], down_got)
+    up_got = shard_swap(up_parts[1])
+    down_got = across_swap(down_parts[1])
+    own_sum, onward, give = span_grads(
+        place, grad_scaled, grad_keys, grad_values, weights_t, grad_one
+    )
+    got = core_swap(give)
+    got, *out_shifted = tie(got, *out_shifted)
     shared = reach - count
-    own_sum = jnp.where(core == 0, keep[reach:] + got[shared:], keep[:count] + got[:count])
-    onward = jnp.where(
-        core == 0,
-        jnp.concatenate([keep[:count], keep[count:reach] + got[:shared]], axis=0),
-        jnp.concatenate([keep[count : count + shared] + got[count:], keep[count + shared :]], axis=0),
+    to_own = lax.dynamic_slice_in_dim(got, (1 - core) * shared, count, 0)
+    to_next = lax.dynamic_slice_in_dim(got, core * count, shared, 0)
+    next_at = (1 - core) * count
+    to_next = low_sum(lax.dynamic_slice_in_dim(onward, next_at, shared, 0), to_next)
+    onward = lax.dynamic_update_slice_in_dim(onward, to_next, next_at, 0)
+    arrived = lax.ppermute(onward, ("ctx", "tp"), chain_pairs())
+    head_sums = jnp.concatenate(
+        [
+            jnp.sum(grad_scaled, axis=0, dtype=f32).reshape(4, 1, heads),
+            jnp.sum(grad_values, axis=0, dtype=f32).reshape(4, 1, heads),
+        ],
+        axis=2,
+    )
+    row_sums = jnp.concatenate([attn_sums, ffn_sums], axis=0).reshape(12, depth)
+    sums = jnp.concatenate(
+        [head_sums, jnp.broadcast_to(row_sums, (4, 12, depth))], axis=1
     ).astype(bf16)
-    arrived = lax.ppermute(onward, ("ctx", "tp"), chain_pairs())
-    passed = core_swap(jnp.where(core == 0, arrived[count:], arrived[:shared])).astype(f32)
-    own_sum = own_sum + jnp.where(core == 0, arrived[:count], arrived[shared:]).astype(f32)
+    up_sums = up_sums.astype(bf16)
+    no_sum = jnp.zeros_like(up_sums)
+    sums = jnp.stack(
+        [
+            jnp.concatenate([sums, up_sums, no_sum, no_sum], axis=1),
+            jnp.concatenate([sums, no_sum, no_sum, no_sum], axis=1),
+        ]
+    )
+    sums = sums.reshape(2, 4, 2, 8, depth).transpose(0, 2, 1, 3, 4)
+    grad_keys, onward = tie(grad_keys, onward)
+    attn_parts = attn_grads(
+        place,
+        grad_scaled,
+        grad_keys,
+        grad_values,
+        mixed,
+        grad_attn,
+        rows_in,
+        in_window,
+        sums,
+    )
+    arrived, up_got, down_got, attn_parts = tie(arrived, up_got, down_got, attn_parts)
+    ffn_parts = jnp.concatenate(
+        [low_sum(up_parts[0], up_got), low_sum(down_parts[0], down_got)], axis=1
+    )
+    ffn_near = scatter_tp_start(ffn_parts)
+    attn_parts = low_sum(attn_parts[0], core_swap(attn_parts[1]))
+    passed = core_swap(lax.dynamic_slice_in_dim(arrived, next_at, shared, 0)).astype(f32)
+    own_sum += to_own.astype(f32)
+    own_sum += lax.dynamic_slice_in_dim(arrived, core * shared, count, 0).astype(f32)
     rest_rows = jnp.zeros((count - shared, width), f32)
-    own_sum = own_sum + jnp.where(
+    own_sum += jnp.where(
         core == 0,
         jnp.concatenate([rest_rows, passed], axis=0),
         jnp.concatenate([passed, rest_rows], axis=0),
     )
-    grad_rows = grad_one + own_sum + contract_last(grad_scaled, full_query)
-    input_grad = deliver(grad_rows.astype(bf16)).astype(f32)
-
-    query_part = contract_rows(rows_in, grad_scaled)
-    key_part = contract_rows(in_window, grad_keys)
-    value_part = contract_rows(in_window, grad_values)
-    in_part = jnp.stack([query_part, key_part, value_part]).astype(bf16)
-    in_part = in_part.reshape(3, 2, 2, half, 4, heads).transpose(2, 4, 1, 3, 0, 5)
-    in_part = in_part.reshape(2, 8 * half, 3 * heads)
-    out_part = out_part.reshape(4, 2, out_half, 2, cut).transpose(1, 0, 3, 2, 4)
-
-    def core_sum(parts):
-        return (
-            jnp.where(core == 0, parts[0], parts[1]).astype(f32)
-            + core_swap(jnp.where(core == 0, parts[1], parts[0])).astype(f32)
-        ).astype(bf16)
-
-    def finish(scattered):
-        total = (scattered.astype(f32) + across_swap(scattered).astype(f32)).astype(bf16)
-        return in_order(core, total, core_swap(total))
-
-    in_done = lax.psum_scatter(core_sum(in_part), both, scatter_dimension=0, tiled=True)
-    in_grads = jnp.concatenate(finish(in_done), axis=0).astype(f32)
-    rest_part = jnp.concatenate(
-        [
-            up_part.astype(bf16).reshape(2, cut, 4, cut).transpose(2, 0, 1, 3),
-            down_part.astype(bf16).reshape(4, cut, 2, cut).transpose(0, 2, 1, 3),
-            core_sum(out_part),
-        ],
-        axis=2,
-    ).reshape(-1, cut)
-    rest_done = lax.psum_scatter(rest_part, both, scatter_dimension=0, tiled=True)
-    rest_lo, rest_hi = finish(rest_done)
-    up_grad = jnp.concatenate([rest_lo[:cut], rest_hi[:cut]], axis=1).astype(f32)
-    down_grad = jnp.concatenate([rest_lo[cut : 2 * cut], rest_hi[cut : 2 * cut]], axis=0).astype(f32)
-    out_grad = jnp.concatenate([rest_lo[2 * cut :], rest_hi[2 * cut :]], axis=0).astype(f32)
-
-    up_bias_all = jnp.stack(
-        [jnp.where(core == 0, up_bias_part, 0.0), jnp.where(core == 1, up_bias_part, 0.0)]
-    )
-    small = lax.psum(
+    own_sum, attn_parts = tie(own_sum, attn_parts)
+    attn_got = across_swap(attn_parts[1])
+    in_packed, in_moved = deliver_start(own_sum.astype(bf16))
+    attn_got, ffn_near = tie(attn_got, ffn_near)
+    attn_mid = low_sum(attn_parts[0], attn_got)
+    attn_got = shard_swap(attn_mid[1])
+    ffn_low = scatter_tp_end(ffn_near)
+    ffn_got = across_swap(ffn_low)
+    in_moved, attn_got, ffn_got = tie(in_moved, attn_got, ffn_got)
+    attn_near = scatter_tp_start(low_sum(attn_mid[0], attn_got))
+    layer_output = deliver_end(out_packed, out_shifted)
+    input_grad = deliver_end(in_packed, in_moved).astype(f32)
+
+
+    def spread(low, got):
+        mine = jnp.stack(in_order(across, low, got))
+        return in_order(core, mine, core_swap(mine))
+
+    ffn_lo, ffn_hi = spread(ffn_low, ffn_got)
+    attn_low = scatter_tp_end(attn_near)
+    attn_lo, attn_hi = spread(attn_low, across_swap(attn_low))
+    quarter = cut // 2
+    up_grad, down_grad = (
+        [part[:, at : at + quarter].reshape(cut, cut) for part in (ffn_lo, ffn_hi)]
+        for at in (0, quarter)
+    )
+    up_grad = jnp.concatenate(up_grad, axis=1).astype(f32)
+    down_grad = jnp.concatenate(down_grad, axis=0).astype(f32)
+    weight_grads = [
         jnp.concatenate(
-            [
-                jnp.sum(grad_scaled, axis=0, dtype=f32),
-                jnp.sum(grad_values, axis=0, dtype=f32),
-                out_bias_grad,
-                attn_gain_grad,
-                attn_shift_grad,
-                down_bias_grad,
-                ffn_gain_grad,
-                ffn_shift_grad,
-                up_bias_all.reshape(-1),
-            ]
-        ),
-        ("shard", "ctx", "tp"),
-    )
-    flat = small[: 8 * width].reshape(8, width)
-    query_bias_grad = lax.dynamic_slice_in_dim(flat[0], tp * heads, heads, 0)
-    value_bias_grad = lax.dynamic_slice_in_dim(flat[1], tp * heads, heads, 0)
-    up_bias_grad = lax.dynamic_index_in_dim(
-        small[8 * width :].reshape(2, 4, cut), tp, 1, keepdims=False
-    ).reshape(-1)
+            [part[m // 2, (m % 2) * half : (m % 2 + 1) * half] for part in (attn_lo, attn_hi)], axis=0
+        ).astype(f32)
+        for m in range(4)
+    ]
+    sums = attn_lo[:, 2 * half :].astype(f32).reshape(16, depth)
+    row_sums = sums[1:13].reshape(6, width)
+    up_bias_grad = jnp.concatenate([sums[13], attn_hi[1, 2 * half + 5].astype(f32)])
     return (
         layer_output,
         input_grad,
-        in_grads[:, :heads],
-        query_bias_grad,
-        in_grads[:, heads : 2 * heads],
-        in_grads[:, 2 * heads :],
-        value_bias_grad,
-        out_grad,
-        flat[2],
-        flat[3],
-        flat[4],
+        weight_grads[0].T,
+        sums[0, :heads],
+        weight_grads[1].T,
+        weight_grads[2].T,
+        sums[0, heads:],
+        weight_grads[3],
+        row_sums[0],
+        row_sums[1],
+        row_sums[2],
         up_grad,
         up_bias_grad,
         down_grad,
-        flat[5],
-        flat[6],
-        flat[7],
+        row_sums[3],
+        row_sums[4],
+        row_sums[5],
     )
 
 

time: 597 us -> 436 us (0.73)
  local copies, waits for them, and re-layouts: 142 us -> 67.4 us
  starting transfers between devices: 21 us -> 89.6 us
  waiting for transfers between devices: 181 us -> 123 us
  Pallas kernels: 48.5 us -> 105 us
  blocking collectives: 50.6 us -> 0 us
  matrix products: 49.4 us -> 0 us
  other arithmetic: 80.2 us -> 39.5 us
  between operations: 16 us -> 2.62 us
    ppermute x0 -> x27, waiting for transfers between devices: none -> 84.9 us  [the longest x12 65 us: tp_shifts(): lax.ppermute(array, 'tp', [(i, (i + shift) % 4) for i in range(4)])]
    ppermute x0 -> x27, starting transfers between devices: none -> 65.4 us  [the longest x12 35.2 us: tp_shifts(): lax.ppermute(array, 'tp', [(i, (i + shift) % 4) for i in range(4)])]
    reduce_scatter x1 -> x0, waiting for transfers between devices: 58.6 us -> none  [span_shards(): lax.psum_scatter(rest_part, both, scatter_dimension=0, tiled=True)]
    pallas_call x0 -> x8, Pallas kernels: none -> 56.9 us  [the longest x1 18.6 us: ffn_back(): pl.pallas_call(ffn_back_kernel, grid_spec=pltpu.PrefetchScalarGridSpec(nu...]
    all_gather x4 -> x0, waiting for transfers between devices: 50 us -> none  [the longest x1 37.5 us: span_shards(): lax.all_gather(own_rest, both, axis=0, tiled=False).reshape(4, 2, -1, cut)]
    dot_general x18 -> x0, matrix products: 49.4 us -> none  [the longest x6 21.4 us: contract_rows(): lax.dot_general(left, right, (((0,), (0,)), ((), ())), preferred_element_...]
    psum x1 -> x0, blocking collectives: 40.1 us -> none  [span_shards(): lax.psum(jnp.concatenate([jnp.sum(grad_scaled, axis=0, dtype=f32), jnp.su...]
    ppermute x1, waiting for transfers between devices: 24.9 us -> 0.01 us  [span_shards(): arrived = lax.ppermute(onward, ('ctx', 'tp'), chain_pairs())]
  transfers between devices with their start and end apart: 31 -> 53, of which waited for: 12 -> 16; matrix products, arithmetic and copies ran while one was open for 40% -> 14% of each run, Pallas kernels for 8% -> 24%
where the time goes in v2:
time: 436 us; the launch traced here: 427 us
  waiting for transfers between devices  123 us (28%)
  Pallas kernels  105 us (24%)
  starting transfers between devices  89.6 us (21%)
  local copies, waits for them, and re-layouts  67.4 us (15%)
  other arithmetic  39.5 us (9%)
    ppermute x12, waiting for transfers between devices, tp_shifts(): lax.ppermute(array, 'tp', [(i, (i + shift) % 4) for i in range(4)])  65 us
    unnamed x195, local copies, waits for them, and re-layouts  43.3 us
    ppermute x25, waiting for transfers between devices, ctx_swap(): return lax.ppermute(array, 'ctx', [(i, i ^ bit) for i in range(4)])  37.9 us
    ppermute x12, starting transfers between devices, tp_shifts(): lax.ppermute(array, 'tp', [(i, (i + shift) % 4) for i in range(4)])  35.2 us
    pallas_call x1, Pallas kernels, attend_back(): pl.pallas_call(partial(attend_back_kernel, span), grid=(pairs, blocks), i...  26.9 us
    ppermute x25, starting transfers between devices, ctx_swap(): return lax.ppermute(array, 'ctx', [(i, i ^ bit) for i in range(4)])  22.2 us
    ppermute x6, starting transfers between devices, scatter_tp_start(): lax.ppermute(sent, 'tp', [(i, (i + shift) % 4) for i in range(4)])  21.8 us
    pallas_call x1, Pallas kernels, attend(): pl.pallas_call(partial(attend_kernel, span), grid=(pairs, blocks), in_spe...  21.2 us
  transfers between devices with their start and end apart: 53, of which 16 were waited for; matrix products, arithmetic and copies ran while one was open for 14% of the time, Pallas kernels for 24%

profile of v2, /device:TPU:1, one launch (start us, length us, event | category | flops | bytes accessed | tf_op | source)
XLA Modules:
  0.0 427.1 jit_solution(18071685684324141625)
XLA Ops:
  0.7 2.5 dynamic-slice_bitcast_fusion
  9.4 2.3 collective-permute-start.1
  12.9 3.1 collective-permute-done
  16.0 11.6 %collective-permute-done.1 = bf16[304,384]{1,0:T(8,128)(2,1)S(1)} collective-permute-done((bf16[304,384]{1,0:T(8,128)(2,1)S(1)}, bf16[304,384]{1,0:T(8,128)(2,1)S(1)}, u32[]{:S(2)}, u32[]{:S(2)}) %collective-permute-start.1) | collective-permute-done | bytes 233504 | tf_op jit(solution)/shard_map/ppermute | solution.py:929
  28.1 5.3 %collective-permute-start.6 = (bf16[864,384]{1,0:T(8,128)(2,1)S(1)}, bf16[864,384]{1,0:T(8,128)(2,1)S(1)}, u32[]{:S(2)}, u32[]{:S(2)}) collective-permute-start(bf16[864,384]{1,0:T(8,128)(2,1)S(1)} %get-tuple-element.98), channel_id=1, source_target_pairs={{0,1},{1,2},{2,3},{3,0},{4,5},{5,6},{6,7},{7,4},{8,9},{9,10},{10,1... | collective-permute-start | bytes 1990664 | tf_op jit(solution)/shard_map/ppermute | solution.py:929
  33.4 13.5 %collective-permute-done.6 = bf16[864,384]{1,0:T(8,128)(2,1)S(1)} collective-permute-done((bf16[864,384]{1,0:T(8,128)(2,1)S(1)}, bf16[864,384]{1,0:T(8,128)(2,1)S(1)}, u32[]{:S(2)}, u32[]{:S(2)}) %collective-permute-start.6) | collective-permute-done | bytes 663584 | tf_op jit(solution)/shard_map/ppermute | solution.py:929
  46.9 2.7 collective-permute-done.5
  53.6 4.7 %collective-permute-start.9 = (bf16[864,384]{1,0:T(8,128)(2,1)}, bf16[864,384]{1,0:T(8,128)(2,1)}, u32[]{:S(2)}, u32[]{:S(2)}) collective-permute-start(bf16[864,384]{1,0:T(8,128)(2,1)} %copy-done.61), channel_id=1, source_target_pairs={{0,3},{1,0},{2,1},{3,2},{4,7},{5,4},{6,5},{7,6},{8,11},{9,8},{10,9... | collective-permute-start | bytes 1990664 | tf_op jit(solution)/shard_map/ppermute | solution.py:929
  61.4 8.0 %project.1 = (bf16[384,768]{1,0:T(8,128)(2,1)S(1)}, bf16[1408,768]{1,0:T(8,128)(2,1)S(1)}, bf16[1408,768]{1,0:T(8,128)(2,1)S(1)}, bf16[1408,768]{1,0:T(8,128)(2,1)S(1)}, bf16[3,768,768]{2,1,0:T(8,128)(2,1)}) custom-call(s32[5]{0:T(128)S(1)} %stack.239.place_ref, bf16[2,4,304,384]{3,2,1,0:T(8,128)(2,1)S(1)} %pad_maximum_fusion.1.w_mine, ...), custom_call_target="tpu_custom_call" | custom-call | flops 3321888768 | bytes 16777216 | tf_op jit(solution)/shard_map/project/pallas_call | solution.py:638
  74.4 2.6 collective-permute-done.10
  82.8 21.2 %attend.1 = (bf16[384,768]{1,0:T(8,128)(2,1)S(1)}, f32[6,3,1,256]{3,2,1,0:T(1,128)S(1)}) custom-call(bf16[384,768]{1,0:T(8,128)(2,1)S(1)} %copy-done.44, bf16[1408,768]{1,0:T(8,128)(2,1)S(1)} %copy-done.38, bf16[1408,768]{1,0:T(8,128)(2,1)S(1)} %copy-done.41, s32[1408,128]{1,0:T(8,128)S(1)} %broadcast_in_dim.18.kd_ref, s32[3,1,128]{2,1,0:T(1,128)S(1)} %slice.238.qd_ref), custom_call_target="tpu_custom_call" | custom-call | flops 5435817984 | bytes 8388608 | tf_op jit(solution)/shard_map/attend/pallas_call | solution.py:389
  108.1 10.9 %collective-permute-done.13 = bf16[864,384]{1,0:T(8,128)(2,1)S(1)} collective-permute-done((bf16[864,384]{1,0:T(8,128)(2,1)}, bf16[864,384]{1,0:T(8,128)(2,1)S(1)}, u32[]{:S(2)}, u32[]{:S(2)}) %collective-permute-start.13) | collective-permute-done | bytes 663584 | tf_op jit(solution)/shard_map/ppermute | solution.py:940
  123.5 2.7 collective-permute-start.14
  128.3 3.1 collective-permute-start.17
  140.3 11.3 %ffn.1 = (bf16[768,1536]{1,0:T(8,128)(2,1)S(1)}, bf16[768,1536]{1,0:T(8,128)(2,1)S(1)}, f32[384,768]{1,0:T(8,128)S(1)}, bf16[384,768]{1,0:T(8,128)(2,1)S(1)}) custom-call(s32[5]{0:T(128)S(1)} %stack.239.place_ref, bf16[768,768]{1,0:T(8,128)(2,1)S(1)} %constant_dynamic-update-slice_fusion.hb_ref, bf16[4,2,864,384]{3,2,1,0:T(8,128)(2,1)S(1)} %copy-done.3, ...), custom_call_target="tpu_custom_call" | custom-call | flops 10871635968 | bytes 12582912 | tf_op jit(solution)/shard_map/ffn/pallas_call | solution.py:519
  159.9 2.6 collective-permute-done.20
  166.8 3.2 collective-permute-done.21
  170.8 12.9 %collective-permute-start.22 = (bf16[384,768]{1,0:T(8,128)(2,1)}, bf16[384,768]{1,0:T(8,128)(2,1)}, u32[]{:S(2)}, u32[]{:S(2)}) collective-permute-start(bf16[384,768]{1,0:T(8,128)(2,1)} %pad_maximum_fusion.7), channel_id=1, source_target_pairs={{0,1},{1,2},{2,3},{3,0},{4,5},{5,6},{6,7},{7,4},{8,9},{9,10},{10,1... | collective-permute-start | bytes 1769480 | tf_op jit(solution)/shard_map/ppermute | solution.py:929
  183.8 18.6 %ffn_back.1 = (f32[384,768]{1,0:T(8,128)S(1)}, bf16[384,768]{1,0:T(8,128)(2,1)}, bf16[2,2,4,192,384]{4,3,2,1,0:T(8,128)(2,1)}, bf16[2,2,4,192,384]{4,3,2,1,0:T(8,128)(2,1)}, f32[4,1,384]{2,1,0:T(1,128)S(1)}) custom-call(s32[5]{0:T(128)S(1)} %stack.239.place_ref, bf16[768,768]{1,0:T(8,128)(2,1)S(1)} %pad_maximum_fusion.3.dz_ref, ...), custom_call_target="tpu_custom_call" | custom-call | flops 10871635968 | bytes 20971520 | tf_op jit(solution)/shard_map/ffn_back/pallas_call | solution.py:560
  207.9 2.5 slice_bitcast_fusion.3
  211.9 2.4 slice_bitcast_fusion.2
  219.4 26.9 %attend_back.1 = (bf16[384,768]{1,0:T(8,128)(2,1)S(1)}, bf16[1408,768]{1,0:T(8,128)(2,1)S(1)}, bf16[1408,768]{1,0:T(8,128)(2,1)S(1)}) custom-call(bf16[384,768]{1,0:T(8,128)(2,1)S(1)} %copy-done.45, bf16[1408,768]{1,0:T(8,128)(2,1)S(1)} %copy-done.39, bf16[1408,768]{1,0:T(8,128)(2,1)S(1)} %copy-done.42, s32[1408,128]{1,0:T(8,128)S(1)} %copy-done.10, ...), custom_call_target="tpu_custom_call" | custom-call | flops 13589544960 | bytes 12582912 | tf_op jit(solution)/shard_map/attend_back/pallas_call | solution.py:411
  253.4 4.6 %span_grads.1 = (f32[384,768]{1,0:T(8,128)S(1)}, bf16[512,768]{1,0:T(8,128)(2,1)S(1)}, bf16[512,768]{1,0:T(8,128)(2,1)S(1)}) custom-call(s32[5]{0:T(128)S(1)} %stack.239.place_ref, bf16[384,768]{1,0:T(8,128)(2,1)S(1)} %get-tuple-element.132.dq_ref, bf16[1408,768]{1,0:T(8,128)(2,1)S(1)} %copy-done.34, bf16[1408,768]{1,0:T(8,128)(2,1)S(1)} %get-tuple-element.138.dv_ref, ...), custom_call_target="tpu_custom_call" | custom-call | flops 3321888768 | bytes 12582912 | tf_op jit(solution)/shard_map/span_grads/pallas_call | solution.py:875
  269.7 9.4 %attn_grads.1 = bf16[2,2,2,4,200,384]{5,4,3,2,1,0:T(8,128)(2,1)} custom-call(s32[5]{0:T(128)S(1)} %stack.239.place_ref, bf16[384,768]{1,0:T(8,128)(2,1)S(1)} %get-tuple-element.132.dq_ref, bf16[1408,768]{1,0:T(8,128)(2,1)S(1)} %copy-done.35, bf16[1408,768]{1,0:T(8,128)(2,1)} %copy-done.4, bf16[384,768]{1,0:T(8,128)(2,1)S(1)} %copy-done.13, ...), custom_call_target="tpu_custom_call" | custom-call | flops 4227858432 | bytes 16777216 | tf_op jit(solution)/shard_map/attn_grads/pallas_call | solution.py:828
  289.9 3.5 collective-permute-start.41
  293.4 2.6 collective-permute-start.42
  301.7 29.8 %collective-permute-done.36 = bf16[128,768]{1,0:T(8,128)(2,1)S(1)} collective-permute-done((bf16[128,768]{1,0:T(8,128)(2,1)S(1)}, bf16[128,768]{1,0:T(8,128)(2,1)S(1)}, u32[]{:S(2)}, u32[]{:S(2)}) %collective-permute-start.36) | collective-permute-done | bytes 196640 | tf_op jit(solution)/shard_map/ppermute | solution.py:895
  337.2 10.3 %collective-permute-done.37 = bf16[384,768]{1,0:T(8,128)(2,1)S(1)} collective-permute-done((bf16[384,768]{1,0:T(8,128)(2,1)S(1)}, bf16[384,768]{1,0:T(8,128)(2,1)S(1)}, u32[]{:S(2)}, u32[]{:S(2)}) %collective-permute-start.37) | collective-permute-done | bytes 589856 | tf_op jit(solution)/shard_map/ppermute | solution.py:929
  347.5 26.4 %collective-permute-done.38 = bf16[384,768]{1,0:T(8,128)(2,1)S(1)} collective-permute-done((bf16[384,768]{1,0:T(8,128)(2,1)S(1)}, bf16[384,768]{1,0:T(8,128)(2,1)S(1)}, u32[]{:S(2)}, u32[]{:S(2)}) %collective-permute-start.38) | collective-permute-done | bytes 589856 | tf_op jit(solution)/shard_map/ppermute | solution.py:929
  375.0 12.9 %collective-permute-start.47 = (bf16[200,384]{1,0:T(8,128)(2,1)S(1)}, bf16[200,384]{1,0:T(8,128)(2,1)S(1)}, u32[]{:S(2)}, u32[]{:S(2)}) collective-permute-start(bf16[200,384]{1,0:T(8,128)(2,1)S(1)} %get-tuple-element.203), channel_id=1, source_target_pairs={{0,1},{1,2},{2,3},{3,0},{4,5},{5,6},{6,7},{7,4},{8,9},{9,10},{10,1... | collective-permute-start | bytes 460808 | tf_op jit(solution)/shard_map/ppermute | solution.py:952
  395.2 3.7 collective-permute-done.48
  424.0 2.6 convert_element_type.228
  (422 shorter events, 144.0 us)
Async XLA Ops:
  3.2 24.4 %collective-permute-start.3 = (bf16[2,256,768]{2,1,0:T(8,128)(2,1)S(1)}, bf16[2,256,768]{2,1,0:T(8,128)(2,1)S(1)}, u32[]{:S(2)}, u32[]{:S(2)}) collective-permute-start(bf16[2,256,768]{2,1,0:T(8,128)(2,1)S(1)} %get-tuple-element.176), channel_id=1, source_target_pairs={{0,8},{4,12},{8,0},{12,4},{1,9},{5,13},{9,1},{13,5},{2,10},{6,14},... | collective-permute-start | bytes 2359304 | tf_op jit(solution)/shard_map/ppermute | solution.py:895
  6.4 21.2 %collective-permute-start.4 = (bf16[864,384]{1,0:T(8,128)(2,1)S(1)}, bf16[864,384]{1,0:T(8,128)(2,1)S(1)}, u32[]{:S(2)}, u32[]{:S(2)}) collective-permute-start(bf16[864,384]{1,0:T(8,128)(2,1)S(1)} %get-tuple-element.98), channel_id=1, source_target_pairs={{0,16},{16,0},{1,17},{17,1},{2,18},{18,2},{3,19},{19,3},{4,20},{20... | collective-permute-start | bytes 1990664 | tf_op jit(solution)/shard_map/ppermute | solution.py:940
  9.4 18.2 %collective-permute-start.1 = (bf16[304,384]{1,0:T(8,128)(2,1)S(1)}, bf16[304,384]{1,0:T(8,128)(2,1)S(1)}, u32[]{:S(2)}, u32[]{:S(2)}) collective-permute-start(bf16[304,384]{1,0:T(8,128)(2,1)S(1)} %maximum_maximum_fusion), channel_id=1, source_target_pairs={{0,2},{1,3},{2,0},{3,1},{4,6},{5,7},{6,4},{7,5},{8,10},{9,11},{10,... | collective-permute-start | bytes 700424 | tf_op jit(solution)/shard_map/ppermute | solution.py:929
  11.7 15.9 %collective-permute-start.2 = (bf16[304,384]{1,0:T(8,128)(2,1)S(1)}, bf16[304,384]{1,0:T(8,128)(2,1)S(1)}, u32[]{:S(2)}, u32[]{:S(2)}) collective-permute-start(bf16[304,384]{1,0:T(8,128)(2,1)S(1)} %maximum_maximum_fusion), channel_id=1, source_target_pairs={{0,3},{1,0},{2,1},{3,2},{4,7},{5,4},{6,5},{7,6},{8,11},{9,8},{10,9... | collective-permute-start | bytes 700424 | tf_op jit(solution)/shard_map/ppermute | solution.py:929
  27.8 21.7 %collective-permute-start.5 = (bf16[4,304,384]{2,1,0:T(8,128)(2,1)S(1)}, bf16[4,304,384]{2,1,0:T(8,128)(2,1)S(1)}, u32[]{:S(2)}, u32[]{:S(2)}) collective-permute-start(bf16[4,304,384]{2,1,0:T(8,128)(2,1)S(1)} %get-tuple-element.198), channel_id=1, source_target_pairs={{0,16},{16,0},{1,17},{17,1},{2,18},{18,2},{3,19},{19,3},{4,20},{20... | collective-permute-start | bytes 2801672 | tf_op jit(solution)/shard_map/ppermute | solution.py:940
  28.1 18.7 %collective-permute-start.6 = (bf16[864,384]{1,0:T(8,128)(2,1)S(1)}, bf16[864,384]{1,0:T(8,128)(2,1)S(1)}, u32[]{:S(2)}, u32[]{:S(2)}) collective-permute-start(bf16[864,384]{1,0:T(8,128)(2,1)S(1)} %get-tuple-element.98), channel_id=1, source_target_pairs={{0,1},{1,2},{2,3},{3,0},{4,5},{5,6},{6,7},{7,4},{8,9},{9,10},{10,1... | collective-permute-start | bytes 1990664 | tf_op jit(solution)/shard_map/ppermute | solution.py:929
  53.6 20.8 %collective-permute-start.9 = (bf16[864,384]{1,0:T(8,128)(2,1)}, bf16[864,384]{1,0:T(8,128)(2,1)}, u32[]{:S(2)}, u32[]{:S(2)}) collective-permute-start(bf16[864,384]{1,0:T(8,128)(2,1)} %copy-done.61), channel_id=1, source_target_pairs={{0,3},{1,0},{2,1},{3,2},{4,7},{5,4},{6,5},{7,6},{8,11},{9,8},{10,9... | collective-permute-start | bytes 1990664 | tf_op jit(solution)/shard_map/ppermute | solution.py:929
  58.2 45.8 %collective-permute-start.12 = (bf16[864,384]{1,0:T(8,128)(2,1)}, bf16[864,384]{1,0:T(8,128)(2,1)}, u32[]{:S(2)}, u32[]{:S(2)}) collective-permute-start(bf16[864,384]{1,0:T(8,128)(2,1)} %copy-done.61), channel_id=1, source_target_pairs={{0,2},{1,3},{2,0},{3,1},{4,6},{5,7},{6,4},{7,5},{8,10},{9,11},{10,... | collective-permute-start | bytes 1990664 | tf_op jit(solution)/shard_map/ppermute | solution.py:929
  60.8 16.2 %collective-permute-start.10 = (bf16[864,384]{1,0:T(8,128)(2,1)}, bf16[864,384]{1,0:T(8,128)(2,1)}, u32[]{:S(2)}, u32[]{:S(2)}) collective-permute-start(bf16[864,384]{1,0:T(8,128)(2,1)} %copy-done.62), channel_id=1, source_target_pairs={{0,16},{16,0},{1,17},{17,1},{2,18},{18,2},{3,19},{19,3},{4,20},{20... | collective-permute-start | bytes 1990664 | tf_op jit(solution)/shard_map/ppermute | solution.py:940
  77.1 27.0 %collective-permute-start.11 = (bf16[864,384]{1,0:T(8,128)(2,1)}, bf16[864,384]{1,0:T(8,128)(2,1)S(1)}, u32[]{:S(2)}, u32[]{:S(2)}) collective-permute-start(bf16[864,384]{1,0:T(8,128)(2,1)} %collective-permute-done.9), channel_id=1, source_target_pairs={{0,16},{16,0},{1,17},{17,1},{2,18},{18,2},{3,19},{19,3},{4,20},{20... | collective-permute-start | bytes 1990664 | tf_op jit(solution)/shard_map/ppermute | solution.py:940
  104.0 14.9 %collective-permute-start.13 = (bf16[864,384]{1,0:T(8,128)(2,1)}, bf16[864,384]{1,0:T(8,128)(2,1)S(1)}, u32[]{:S(2)}, u32[]{:S(2)}) collective-permute-start(bf16[864,384]{1,0:T(8,128)(2,1)} %collective-permute-done.12), channel_id=1, source_target_pairs={{0,16},{16,0},{1,17},{17,1},{2,18},{18,2},{3,19},{19,3},{4,20},{20... | collective-permute-start | bytes 1990664 | tf_op jit(solution)/shard_map/ppermute | solution.py:940
  138.6 14.5 %collective-permute-start.18 = (bf16[2,256,768]{2,1,0:T(8,128)(2,1)S(1)}, bf16[2,256,768]{2,1,0:T(8,128)(2,1)S(1)}, u32[]{:S(2)}, u32[]{:S(2)}) collective-permute-start(bf16[2,256,768]{2,1,0:T(8,128)(2,1)S(1)} %pad_maximum_fusion.5), channel_id=1, source_target_pairs={{0,4},{4,0},{8,12},{12,8},{1,5},{5,1},{9,13},{13,9},{2,6},{6,2},{1... | collective-permute-start | bytes 2359304 | tf_op jit(solution)/shard_map/ppermute | solution.py:895
  170.8 43.5 %collective-permute-start.22 = (bf16[384,768]{1,0:T(8,128)(2,1)}, bf16[384,768]{1,0:T(8,128)(2,1)}, u32[]{:S(2)}, u32[]{:S(2)}) collective-permute-start(bf16[384,768]{1,0:T(8,128)(2,1)} %pad_maximum_fusion.7), channel_id=1, source_target_pairs={{0,1},{1,2},{2,3},{3,0},{4,5},{5,6},{6,7},{7,4},{8,9},{9,10},{10,1... | collective-permute-start | bytes 1769480 | tf_op jit(solution)/shard_map/ppermute | solution.py:929
  205.8 58.6 %collective-permute-start.27 = (bf16[384,768]{1,0:T(8,128)(2,1)}, bf16[384,768]{1,0:T(8,128)(2,1)}, u32[]{:S(2)}, u32[]{:S(2)}) collective-permute-start(bf16[384,768]{1,0:T(8,128)(2,1)} %pad_maximum_fusion.7), channel_id=1, source_target_pairs={{0,2},{1,3},{2,0},{3,1},{4,6},{5,7},{6,4},{7,5},{8,10},{9,11},{10,... | collective-permute-start | bytes 1769480 | tf_op jit(solution)/shard_map/ppermute | solution.py:929
  205.8 58.6 %collective-permute-start.28 = (bf16[384,768]{1,0:T(8,128)(2,1)}, bf16[384,768]{1,0:T(8,128)(2,1)}, u32[]{:S(2)}, u32[]{:S(2)}) collective-permute-start(bf16[384,768]{1,0:T(8,128)(2,1)} %pad_maximum_fusion.7), channel_id=1, source_target_pairs={{0,3},{1,0},{2,1},{3,2},{4,7},{5,4},{6,5},{7,6},{8,11},{9,8},{10,9... | collective-permute-start | bytes 1769480 | tf_op jit(solution)/shard_map/ppermute | solution.py:929
  210.4 37.6 %collective-permute-start.24 = (bf16[2,4,192,384]{3,2,1,0:T(8,128)(2,1)}, bf16[2,4,192,384]{3,2,1,0:T(8,128)(2,1)}, u32[]{:S(2)}, u32[]{:S(2)}) collective-permute-start(bf16[2,4,192,384]{3,2,1,0:T(8,128)(2,1)} %slice_bitcast_fusion.3), channel_id=1, source_target_pairs={{0,8},{4,12},{8,0},{12,4},{1,9},{5,13},{9,1},{13,5},{2,10},{6,14},... | collective-permute-start | bytes 3538952 | tf_op jit(solution)/shard_map/ppermute | solution.py:895
  214.3 33.6 %collective-permute-start.25 = (bf16[2,4,192,384]{3,2,1,0:T(8,128)(2,1)}, bf16[2,4,192,384]{3,2,1,0:T(8,128)(2,1)}, u32[]{:S(2)}, u32[]{:S(2)}) collective-permute-start(bf16[2,4,192,384]{3,2,1,0:T(8,128)(2,1)} %slice_bitcast_fusion.2), channel_id=1, source_target_pairs={{0,16},{16,0},{1,17},{17,1},{2,18},{18,2},{3,19},{19,3},{4,20},{20... | collective-permute-start | bytes 3538952 | tf_op jit(solution)/shard_map/ppermute | solution.py:940
  260.9 18.2 %collective-permute-start.32 = (bf16[4,192,384]{2,1,0:T(8,128)(2,1)S(1)}, bf16[4,192,384]{2,1,0:T(8,128)(2,1)S(1)}, u32[]{:S(2)}, u32[]{:S(2)}) collective-permute-start(bf16[4,192,384]{2,1,0:T(8,128)(2,1)S(1)} %slice_bitcast_fusion.8), channel_id=1, source_target_pairs={{0,8},{4,12},{8,0},{12,4},{1,9},{5,13},{9,1},{13,5},{2,10},{6,14},... | collective-permute-start | bytes 1769480 | tf_op jit(solution)/shard_map/ppermute | solution.py:895
  263.8 15.3 %collective-permute-start.31 = (bf16[4,192,384]{2,1,0:T(8,128)(2,1)}, bf16[4,192,384]{2,1,0:T(8,128)(2,1)S(1)}, u32[]{:S(2)}, u32[]{:S(2)}) collective-permute-start(bf16[4,192,384]{2,1,0:T(8,128)(2,1)} %slice_bitcast_fusion.9), channel_id=1, source_target_pairs={{0,16},{16,0},{1,17},{17,1},{2,18},{18,2},{3,19},{19,3},{4,20},{20... | collective-permute-start | bytes 1769480 | tf_op jit(solution)/shard_map/ppermute | solution.py:940
  282.1 15.0 %collective-permute-start.34 = (bf16[2,2,4,200,384]{4,3,2,1,0:T(8,128)(2,1)S(1)}, bf16[2,2,4,200,384]{4,3,2,1,0:T(8,128)(2,1)S(1)}, u32[]{:S(2)}, u32[]{:S(2)}) collective-permute-start(bf16[2,2,4,200,384]{4,3,2,1,0:T(8,128)(2,1)S(1)} %slice_bitcast_fusion), channel_id=1, source_target_pairs={{0,4},{4,0},{8,12},{12,8},{1,5},{5,1},{9,13},{13,9},{2,6},{6,2},{1... | collective-permute-start | bytes 7372808 | tf_op jit(solution)/shard_map/ppermute | solution.py:895
  289.9 43.2 %collective-permute-start.41 = (bf16[384,384]{1,0:T(8,128)(2,1)S(1)}, bf16[384,384]{1,0:T(8,128)(2,1)S(1)}, u32[]{:S(2)}, u32[]{:S(2)}) collective-permute-start(bf16[384,384]{1,0:T(8,128)(2,1)S(1)} %get-tuple-element.185), channel_id=1, source_target_pairs={{0,1},{1,2},{2,3},{3,0},{4,5},{5,6},{6,7},{7,4},{8,9},{9,10},{10,1... | collective-permute-start | bytes 884744 | tf_op jit(solution)/shard_map/ppermute | solution.py:952
  293.4 39.7 %collective-permute-start.42 = (bf16[384,384]{1,0:T(8,128)(2,1)S(1)}, bf16[384,384]{1,0:T(8,128)(2,1)S(1)}, u32[]{:S(2)}, u32[]{:S(2)}) collective-permute-start(bf16[384,384]{1,0:T(8,128)(2,1)S(1)} %get-tuple-element.186), channel_id=1, source_target_pairs={{0,2},{1,3},{2,0},{3,1},{4,6},{5,7},{6,4},{7,5},{8,10},{9,11},{10,... | collective-permute-start | bytes 884744 | tf_op jit(solution)/shard_map/ppermute | solution.py:952
  296.0 39.2 %collective-permute-start.43 = (bf16[384,384]{1,0:T(8,128)(2,1)S(1)}, bf16[384,384]{1,0:T(8,128)(2,1)S(1)}, u32[]{:S(2)}, u32[]{:S(2)}) collective-permute-start(bf16[384,384]{1,0:T(8,128)(2,1)S(1)} %get-tuple-element.183), channel_id=1, source_target_pairs={{0,3},{1,0},{2,1},{3,2},{4,7},{5,4},{6,5},{7,6},{8,11},{9,8},{10,9... | collective-permute-start | bytes 884744 | tf_op jit(solution)/shard_map/ppermute | solution.py:952
  298.6 36.6 %collective-permute-start.40 = (bf16[2,4,200,384]{3,2,1,0:T(8,128)(2,1)S(1)}, bf16[2,4,200,384]{3,2,1,0:T(8,128)(2,1)S(1)}, u32[]{:S(2)}, u32[]{:S(2)}) collective-permute-start(bf16[2,4,200,384]{3,2,1,0:T(8,128)(2,1)S(1)} %slice_bitcast_fusion.1), channel_id=1, source_target_pairs={{0,8},{4,12},{8,0},{12,4},{1,9},{5,13},{9,1},{13,5},{2,10},{6,14},... | collective-permute-start | bytes 3686408 | tf_op jit(solution)/shard_map/ppermute | solution.py:895
  300.3 31.2 %collective-permute-start.36 = (bf16[128,768]{1,0:T(8,128)(2,1)S(1)}, bf16[128,768]{1,0:T(8,128)(2,1)S(1)}, u32[]{:S(2)}, u32[]{:S(2)}) collective-permute-start(bf16[128,768]{1,0:T(8,128)(2,1)S(1)} %fusion.33), channel_id=1, source_target_pairs={{0,8},{4,12},{8,0},{12,4},{1,9},{5,13},{9,1},{13,5},{2,10},{6,14},... | collective-permute-start | bytes 589832 | tf_op jit(solution)/shard_map/ppermute | solution.py:895
  331.6 16.0 %collective-permute-start.37 = (bf16[384,768]{1,0:T(8,128)(2,1)S(1)}, bf16[384,768]{1,0:T(8,128)(2,1)S(1)}, u32[]{:S(2)}, u32[]{:S(2)}) collective-permute-start(bf16[384,768]{1,0:T(8,128)(2,1)S(1)} %pad_maximum_fusion.8), channel_id=1, source_target_pairs={{0,1},{1,2},{2,3},{3,0},{4,5},{5,6},{6,7},{7,4},{8,9},{9,10},{10,1... | collective-permute-start | bytes 1769480 | tf_op jit(solution)/shard_map/ppermute | solution.py:929
  333.1 40.9 %collective-permute-start.38 = (bf16[384,768]{1,0:T(8,128)(2,1)S(1)}, bf16[384,768]{1,0:T(8,128)(2,1)S(1)}, u32[]{:S(2)}, u32[]{:S(2)}) collective-permute-start(bf16[384,768]{1,0:T(8,128)(2,1)S(1)} %pad_maximum_fusion.8), channel_id=1, source_target_pairs={{0,2},{1,3},{2,0},{3,1},{4,6},{5,7},{6,4},{7,5},{8,10},{9,11},{10,... | collective-permute-start | bytes 1769480 | tf_op jit(solution)/shard_map/ppermute | solution.py:929
  333.1 40.9 %collective-permute-start.39 = (bf16[384,768]{1,0:T(8,128)(2,1)S(1)}, bf16[384,768]{1,0:T(8,128)(2,1)S(1)}, u32[]{:S(2)}, u32[]{:S(2)}) collective-permute-start(bf16[384,768]{1,0:T(8,128)(2,1)S(1)} %pad_maximum_fusion.8), channel_id=1, source_target_pairs={{0,3},{1,0},{2,1},{3,2},{4,7},{5,4},{6,5},{7,6},{8,11},{9,8},{10,9... | collective-permute-start | bytes 1769480 | tf_op jit(solution)/shard_map/ppermute | solution.py:929
  335.6 38.3 %collective-permute-start.44 = (bf16[4,200,384]{2,1,0:T(8,128)(2,1)S(1)}, bf16[4,200,384]{2,1,0:T(8,128)(2,1)S(1)}, u32[]{:S(2)}, u32[]{:S(2)}) collective-permute-start(bf16[4,200,384]{2,1,0:T(8,128)(2,1)S(1)} %slice_bitcast_fusion.5), channel_id=1, source_target_pairs={{0,16},{16,0},{1,17},{17,1},{2,18},{18,2},{3,19},{19,3},{4,20},{20... | collective-permute-start | bytes 1843208 | tf_op jit(solution)/shard_map/ppermute | solution.py:940
  336.2 37.8 %collective-permute-start.45 = (bf16[384,384]{1,0:T(8,128)(2,1)S(1)}, bf16[384,384]{1,0:T(8,128)(2,1)S(1)}, u32[]{:S(2)}, u32[]{:S(2)}) collective-permute-start(bf16[384,384]{1,0:T(8,128)(2,1)S(1)} %add_convert_fusion), channel_id=1, source_target_pairs={{0,8},{4,12},{8,0},{12,4},{1,9},{5,13},{9,1},{13,5},{2,10},{6,14},... | collective-permute-start | bytes 884744 | tf_op jit(solution)/shard_map/ppermute | solution.py:895
  374.1 31.5 %collective-permute-start.52 = (bf16[2,384,384]{2,1,0:T(8,128)(2,1)S(1)}, bf16[2,384,384]{2,1,0:T(8,128)(2,1)S(1)}, u32[]{:S(2)}, u32[]{:S(2)}) collective-permute-start(bf16[2,384,384]{2,1,0:T(8,128)(2,1)S(1)} %pad_maximum_fusion.9), channel_id=1, source_target_pairs={{0,4},{4,0},{8,12},{12,8},{1,5},{5,1},{9,13},{13,9},{2,6},{6,2},{1... | collective-permute-start | bytes 1769480 | tf_op jit(solution)/shard_map/ppermute | solution.py:895
  375.0 20.2 %collective-permute-start.47 = (bf16[200,384]{1,0:T(8,128)(2,1)S(1)}, bf16[200,384]{1,0:T(8,128)(2,1)S(1)}, u32[]{:S(2)}, u32[]{:S(2)}) collective-permute-start(bf16[200,384]{1,0:T(8,128)(2,1)S(1)} %get-tuple-element.203), channel_id=1, source_target_pairs={{0,1},{1,2},{2,3},{3,0},{4,5},{5,6},{6,7},{7,4},{8,9},{9,10},{10,1... | collective-permute-start | bytes 460808 | tf_op jit(solution)/shard_map/ppermute | solution.py:952
  (110 other events, 748.0 us)

commit v3 on v2

--- a/solution.py
+++ b/solution.py
@@ -325,7 +325,8 @@
     return jnp.where(jnp.concatenate([same, same], axis=1), scores, jnp.float32(far_below))
 
 
-def attend_kernel(span, q_ref, k_ref, v_ref, kd_ref, qd_ref, o_ref, l_ref):
+def attend_kernel(span, q_ref, k_ref, v_ref, kd_ref, qd_ref, *refs):
+    o_ref, l_ref = refs[-2:]
     first = pl.multiple_of(pl.program_id(1) * QBLOCK, QBLOCK)
     keys = k_ref[pl.ds(first, span), :]
     values = v_ref[pl.ds(first, span), :]
@@ -340,9 +341,8 @@
     l_ref[0, 0] = top + jnp.log(total)
 
 
-def attend_back_kernel(
-    span, q_ref, k_ref, v_ref, kd_ref, qd_ref, do_ref, l_ref, dq_ref, dk_ref, dv_ref, dk_acc, dv_acc
-):
+def attend_back_kernel(span, q_ref, k_ref, v_ref, kd_ref, qd_ref, do_ref, l_ref, *refs):
+    dq_ref, dk_ref, dv_ref, dk_acc, dv_acc = refs[-5:]
     step = pl.program_id(1)
 
     @pl.when(step == 0)
@@ -362,7 +362,8 @@
     inner = jnp.sum(grad_probs * probs, axis=0, keepdims=True)
     grad_scores = (probs * (grad_probs - inner)).astype(jnp.bfloat16)
     grad_queries = unstack_heads(contract_rows(keys, grad_scores))
-    dq_ref[...] = (grad_queries * (1.0 / math.sqrt(HEAD_DIM))).astype(jnp.bfloat16)
+    grad_queries = (grad_queries * (1.0 / math.sqrt(HEAD_DIM))).astype(jnp.bfloat16)
+    dq_ref[...] = grad_queries
     dk_acc[here, :] += dot32(grad_scores, queries)
     dv_acc[here, :] += dot32(probs.astype(jnp.bfloat16), grads)
 
@@ -372,46 +373,51 @@
         dv_ref[...] = dv_acc[...].astype(jnp.bfloat16)
 
 
-def attention_specs(window):
-    rows = pl.BlockSpec((QBLOCK, PAIR), lambda h, i: (i, h))
-    keys = pl.BlockSpec((window, PAIR), lambda h, i: (0, h))
+def attention_specs(window, at=0):
+    rows = pl.BlockSpec((QBLOCK, PAIR), lambda h, i: (i, at + h))
+    keys = pl.BlockSpec((window, PAIR), lambda h, i: (0, at + h))
     key_docs = pl.BlockSpec((window, QBLOCK), lambda h, i: (0, 0))
     query_docs = pl.BlockSpec((1, 1, QBLOCK), lambda h, i: (i, 0, 0))
-    logs = pl.BlockSpec((1, 1, 1, 2 * QBLOCK), lambda h, i: (h, i, 0, 0))
+    logs = pl.BlockSpec((1, 1, 1, 2 * QBLOCK), lambda h, i: (at + h, i, 0, 0))
     return rows, keys, key_docs, query_docs, logs
 
 
-def attend(queries, keys, values, key_docs, query_docs, reach):
+def attend(queries, keys, values, key_docs, query_docs, reach, at, pairs, prior=()):
     count, width = queries.shape
     window = keys.shape[0]
-    blocks, pairs, span = count // QBLOCK, width // PAIR, QBLOCK + 2 * reach
-    rows, key_spec, kd_spec, qd_spec, logs = attention_specs(window)
+    blocks, span = count // QBLOCK, QBLOCK + 2 * reach
+    rows, key_spec, kd_spec, qd_spec, logs = attention_specs(window, at)
     return pl.pallas_call(
         partial(attend_kernel, span),
         grid=(pairs, blocks),
-        in_specs=[rows, key_spec, key_spec, kd_spec, qd_spec],
+        in_specs=[rows, key_spec, key_spec, kd_spec, qd_spec]
+        + [pl.BlockSpec(memory_space=pl.ANY)] * len(prior),
         out_specs=[rows, logs],
         out_shape=[
             jax.ShapeDtypeStruct((count, width), jnp.bfloat16),
-            jax.ShapeDtypeStruct((pairs, blocks, 1, 2 * QBLOCK), jnp.float32),
+            jax.ShapeDtypeStruct((width // PAIR, blocks, 1, 2 * QBLOCK), jnp.float32),
         ],
-        compiler_params=pltpu.CompilerParams(vmem_limit_bytes=40 << 20),
+        input_output_aliases={5 + i: i for i in range(len(prior))},
+        compiler_params=pltpu.CompilerParams(vmem_limit_bytes=12 << 20),
         cost_estimate=pl.CostEstimate(
-            flops=16 * count * span * width, bytes_accessed=8 << 20, transcendentals=0
+            flops=16 * count * span * PAIR * pairs, bytes_accessed=4 << 20, transcendentals=0
         ),
         name="attend",
-    )(queries, keys, values, key_docs, query_docs)
-
-
-def attend_back(queries, keys, values, key_docs, query_docs, grads, logs_in, reach):
+    )(queries, keys, values, key_docs, query_docs, *prior)
+
+
+def attend_back(
+    queries, keys, values, key_docs, query_docs, grads, logs_in, reach, at, pairs, prior=()
+):
     count, width = queries.shape
     window = keys.shape[0]
-    blocks, pairs, span = count // QBLOCK, width // PAIR, QBLOCK + 2 * reach
-    rows, key_spec, kd_spec, qd_spec, logs = attention_specs(window)
+    blocks, span = count // QBLOCK, QBLOCK + 2 * reach
+    rows, key_spec, kd_spec, qd_spec, logs = attention_specs(window, at)
     return pl.pallas_call(
         partial(attend_back_kernel, span),
         grid=(pairs, blocks),
-        in_specs=[rows, key_spec, key_spec, kd_spec, qd_spec, rows, logs],
+        in_specs=[rows, key_spec, key_spec, kd_spec, qd_spec, rows, logs]
+        + [pl.BlockSpec(memory_space=pl.ANY)] * len(prior),
         out_specs=[rows, key_spec, key_spec],
         out_shape=[
             jax.ShapeDtypeStruct((count, width), jnp.bfloat16),
@@ -422,12 +428,13 @@
             pltpu.VMEM((window, PAIR), jnp.float32),
             pltpu.VMEM((window, PAIR), jnp.float32),
         ],
-        compiler_params=pltpu.CompilerParams(vmem_limit_bytes=40 << 20),
+        input_output_aliases={7 + i: i for i in range(len(prior))},
+        compiler_params=pltpu.CompilerParams(vmem_limit_bytes=16 << 20),
         cost_estimate=pl.CostEstimate(
-            flops=40 * count * span * width, bytes_accessed=12 << 20, transcendentals=0
+            flops=40 * count * span * PAIR * pairs, bytes_accessed=6 << 20, transcendentals=0
         ),
         name="attend_back",
-    )(queries, keys, values, key_docs, query_docs, grads, logs_in)
+    )(queries, keys, values, key_docs, query_docs, grads, logs_in, *prior)
 
 
 def half_cols(position, half):
@@ -444,27 +451,42 @@
         ref[index] += terms
 
 
-def ffn_kernel(
-    place_ref, hb_ref, up_ref, down_ref, bias_ref, acts_ref, slope_ref, own_ref, other_ref, total
-):
-    step = pl.program_id(0)
+def ffn_kernel(place_ref, hb_ref, up_ref, down_ref, bias_ref, *refs):
     half = up_ref.shape[3]
-    count = own_ref.shape[0]
     near, far = half_cols(place_ref[1], half), half_cols(1 - place_ref[1], half)
-    pre_act = dot32(hb_ref[:, near], up_ref[0, 0]) + dot32(hb_ref[:, far], up_ref[0, 1])
-    pre_act += bias_ref[0]
-    cdf = 0.5 * (1.0 + lax.erf(pre_act * math.sqrt(0.5)))
-    bell = jnp.exp(-0.5 * pre_act * pre_act) * (1.0 / math.sqrt(2 * math.pi))
-    acts = (pre_act * cdf).astype(jnp.bfloat16)
-    acts_ref[...] = acts
-    slope_ref[...] = (cdf + pre_act * bell).astype(jnp.bfloat16)
-    add_or_set(step == 0, total, (slice(None), near), dot32(acts, down_ref[0, 0]))
-    add_or_set(step == 0, total, (slice(None), far), dot32(acts, down_ref[0, 1]))
-
-    @pl.when(step == pl.num_programs(0) - 1)
-    def _():
-        own_ref[...] = total[:count]
-        other_ref[...] = total[count:].astype(jnp.bfloat16)
+    last = len(refs) > 3
+    if last:
+        base_ref, _, _, acts_ref, slope_ref, own_ref, other_ref = refs
+    else:
+        acts_ref, slope_ref, total = refs
+
+        @pl.when(pl.program_id(0) == 0)
+        def _():
+            total[...] = jnp.zeros_like(total)
+
+    def chunk(rows):
+        pre_act = dot32(hb_ref[rows, near], up_ref[0, 0]) + dot32(hb_ref[rows, far], up_ref[0, 1])
+        pre_act += bias_ref[0]
+        cdf = 0.5 * (1.0 + lax.erf(pre_act * math.sqrt(0.5)))
+        bell = jnp.exp(-0.5 * pre_act * pre_act) * (1.0 / math.sqrt(2 * math.pi))
+        acts = (pre_act * cdf).astype(jnp.bfloat16)
+        acts_ref[rows] = acts
+        slope_ref[rows] = (cdf + pre_act * bell).astype(jnp.bfloat16)
+        return dot32(acts, down_ref[0, 0]), dot32(acts, down_ref[0, 1])
+
+    count = hb_ref.shape[0] // 2
+    if last:
+        for part, to in enumerate((own_ref, other_ref)):
+            rows = slice(part * count, (part + 1) * count)
+            for cols, terms in zip((near, far), chunk(rows)):
+                to[:, cols] = (base_ref[rows, cols] + terms).astype(to.dtype)
+    else:
+
+        @pl.loop(0, 2)
+        def _(part):
+            rows = pl.ds(pl.multiple_of(part * count, count), count)
+            for cols, terms in zip((near, far), chunk(rows)):
+                total[rows, cols] += terms
 
 
 def ffn_back_kernel(
@@ -477,28 +499,50 @@
     down_ref,
     own_ref,
     other_ref,
-    up_ref_out,
-    down_ref_out,
+    up_keep,
+    up_give,
+    down_keep,
+    down_give,
     sums_ref,
     total,
+    grad_pre,
 ):
     step = pl.program_id(0)
     half = up_ref.shape[3]
+    quarter = half // 2
     count = own_ref.shape[0]
     near, far = half_cols(place_ref[1], half), half_cols(1 - place_ref[1], half)
-    grad_acts = contract_last(dz_ref[:, near], down_ref[0, 0])
-    grad_acts += contract_last(dz_ref[:, far], down_ref[0, 1])
-    grad_pre = (slope_ref[...].astype(jnp.float32) * grad_acts).astype(jnp.bfloat16)
-    sums_ref[0] = jnp.sum(grad_pre.astype(jnp.float32), axis=0, keepdims=True)
-    add_or_set(step == 0, total, (slice(None), near), contract_last(grad_pre, up_ref[0, 0]))
-    add_or_set(step == 0, total, (slice(None), far), contract_last(grad_pre, up_ref[0, 1]))
+    @pl.when(step == 0)
+    def _():
+        total[...] = jnp.zeros_like(total)
+
+    sums_ref[...] = jnp.zeros_like(sums_ref)
+
+    @pl.loop(0, 2)
+    def _(part):
+        rows = pl.ds(pl.multiple_of(part * count, count), count)
+        grad_acts = contract_last(dz_ref[rows, near], down_ref[0, 0])
+        grad_acts += contract_last(dz_ref[rows, far], down_ref[0, 1])
+        low = (slope_ref[rows].astype(jnp.float32) * grad_acts).astype(jnp.bfloat16)
+        grad_pre[rows] = low
+        sums_ref[0] += row_sum(low.astype(jnp.float32))
+        total[rows, near] += contract_last(low, up_ref[0, 0])
+        total[rows, far] += contract_last(low, up_ref[0, 1])
+
     for side, cols in enumerate((near, far)):
-        up_grad = contract_rows(hb_ref[:, cols], grad_pre).astype(jnp.bfloat16)
+        up_grad = contract_rows(hb_ref[:, cols], grad_pre[...]).astype(jnp.bfloat16)
         down_grad = contract_rows(acts_ref[...], dz_ref[:, cols]).astype(jnp.bfloat16)
-        for x, place in enumerate((place_ref[3], 1 - place_ref[3])):
-            rows = slice(x * half // 2, (x + 1) * half // 2)
-            up_ref_out[place, side, 0] = up_grad[rows]
-            down_ref_out[side, place, 0] = down_grad[rows]
+        down_to = down_give if side else down_keep
+        for across in (0, 1):
+            mine = slice(across * quarter, (across + 1) * quarter)
+            theirs = slice((1 - across) * quarter, (2 - across) * quarter)
+
+            @pl.when(place_ref[3] == across)
+            def _():
+                up_keep[side, 0] = up_grad[mine]
+                up_give[side, 0] = up_grad[theirs]
+                down_to[0, 0] = down_grad[mine]
+                down_to[1, 0] = down_grad[theirs]
 
     @pl.when(step == pl.num_programs(0) - 1)
     def _():
@@ -510,38 +554,47 @@
     return pl.BlockSpec(shape, lambda *_: (0,) * len(shape))
 
 
-def ffn(place, rows, weights, bias):
+def ffn(place, rows, weights, bias, steps, prior=()):
     both, width = rows.shape
     tps, shards, _, half = weights.shape
     count = both // 2
+    at = tps - steps if prior else 0
     matrix = (1, shards, half, half)
-    block = pl.BlockSpec((both, half), lambda i, _: (0, i))
+    block = pl.BlockSpec((both, half), lambda i, _: (0, at + i))
+    hidden = jax.ShapeDtypeStruct((both, tps * half), jnp.bfloat16)
+    if prior:
+        last_specs = [whole((count, width)), whole((count, width))]
+        last_shapes = [
+            jax.ShapeDtypeStruct((count, width), jnp.float32),
+            jax.ShapeDtypeStruct((count, width), jnp.bfloat16),
+        ]
+        prior_specs = [whole((both, width))] + [pl.BlockSpec(memory_space=pl.ANY)] * 2
+    else:
+        last_specs = [whole((both, width))]
+        last_shapes = [jax.ShapeDtypeStruct((both, width), jnp.float32)]
+        prior_specs = []
     return pl.pallas_call(
         ffn_kernel,
         grid_spec=pltpu.PrefetchScalarGridSpec(
             num_scalar_prefetch=1,
-            grid=(tps,),
+            grid=(steps,),
             in_specs=[
                 whole((both, width)),
-                pl.BlockSpec(matrix, lambda i, _: (i, 0, 0, 0)),
-                pl.BlockSpec(matrix, lambda i, _: (i, 0, 1, 0)),
-                pl.BlockSpec((1, 1, half), lambda i, _: (i, 0, 0)),
-            ],
-            out_specs=[block, block, whole((count, width)), whole((count, width))],
-            scratch_shapes=[pltpu.VMEM((both, width), jnp.float32)],
-        ),
-        out_shape=[
-            jax.ShapeDtypeStruct((both, tps * half), jnp.bfloat16),
-            jax.ShapeDtypeStruct((both, tps * half), jnp.bfloat16),
-            jax.ShapeDtypeStruct((count, width), jnp.float32),
-            jax.ShapeDtypeStruct((count, width), jnp.bfloat16),
-        ],
-        compiler_params=pltpu.CompilerParams(vmem_limit_bytes=40 << 20),
+                pl.BlockSpec(matrix, lambda i, _: (at + i, 0, 0, 0)),
+                pl.BlockSpec(matrix, lambda i, _: (at + i, 0, 1, 0)),
+                pl.BlockSpec((1, 1, half), lambda i, _: (at + i, 0, 0)),
+            ]
+            + prior_specs,
+            out_specs=[block, block] + last_specs,
+        ),
+        out_shape=[hidden, hidden] + last_shapes,
+        input_output_aliases={6: 0, 7: 1} if prior else {},
+        compiler_params=pltpu.CompilerParams(vmem_limit_bytes=20 << 20),
         cost_estimate=pl.CostEstimate(
-            flops=12 * both * width * tps * half, bytes_accessed=12 << 20, transcendentals=0
+            flops=12 * both * width * steps * half, bytes_accessed=3 * steps << 20, transcendentals=0
         ),
         name="ffn",
-    )(place, rows, weights, weights, bias)
+    )(place, rows, weights, weights, bias, *prior)
 
 
 def ffn_back(place, grads, rows, acts, slope, weights):
@@ -552,10 +605,10 @@
     block = pl.BlockSpec((both, half), lambda i, _: (0, i))
 
     def source(i, place_ref):
-        return (place_ref[2] + tps - i) % tps
+        return (place_ref[2] + tps - jnp.where(i < 2, i, 5 - i)) % tps
 
     parts = pl.BlockSpec(
-        (2, 2, 1, half // 2, half), lambda i, at: (0, 0, source(i, at), 0, 0)
+        (2, 1, half // 2, half), lambda i, at: (0, source(i, at), 0, 0)
     )
     return pl.pallas_call(
         ffn_back_kernel,
@@ -575,18 +628,22 @@
                 whole((count, width)),
                 parts,
                 parts,
+                parts,
+                parts,
                 pl.BlockSpec((1, 1, half), lambda i, at: (source(i, at), 0, 0)),
             ],
-            scratch_shapes=[pltpu.VMEM((both, width), jnp.float32)],
+            scratch_shapes=[
+                pltpu.VMEM((both, width), jnp.float32),
+                pltpu.VMEM((both, half), jnp.bfloat16),
+            ],
         ),
         out_shape=[
             jax.ShapeDtypeStruct((count, width), jnp.float32),
             jax.ShapeDtypeStruct((count, width), jnp.bfloat16),
-            jax.ShapeDtypeStruct((2, 2, tps, half // 2, half), jnp.bfloat16),
-            jax.ShapeDtypeStruct((2, 2, tps, half // 2, half), jnp.bfloat16),
+            *[jax.ShapeDtypeStruct((2, tps, half // 2, half), jnp.bfloat16)] * 4,
             jax.ShapeDtypeStruct((tps, 1, half), jnp.float32),
         ],
-        compiler_params=pltpu.CompilerParams(vmem_limit_bytes=48 << 20),
+        compiler_params=pltpu.CompilerParams(vmem_limit_bytes=26 << 20),
         cost_estimate=pl.CostEstimate(
             flops=12 * both * width * tps * half, bytes_accessed=20 << 20, transcendentals=0
         ),
@@ -647,7 +704,7 @@
             jax.ShapeDtypeStruct((window, width), jnp.bfloat16),
             jax.ShapeDtypeStruct((3, width, width), jnp.bfloat16),
         ],
-        compiler_params=pltpu.CompilerParams(vmem_limit_bytes=40 << 20),
+        compiler_params=pltpu.CompilerParams(vmem_limit_bytes=24 << 20),
         cost_estimate=pl.CostEstimate(
             flops=4 * window * width * width, bytes_accessed=16 << 20, transcendentals=0
         ),
@@ -709,7 +766,7 @@
             jax.ShapeDtypeStruct((count, QBLOCK), jnp.float32),
             jax.ShapeDtypeStruct((width, width), jnp.bfloat16),
         ],
-        compiler_params=pltpu.CompilerParams(vmem_limit_bytes=40 << 20),
+        compiler_params=pltpu.CompilerParams(vmem_limit_bytes=10 << 20),
         cost_estimate=pl.CostEstimate(
             flops=2 * count * width * width, bytes_accessed=8 << 20, transcendentals=0
         ),
@@ -744,7 +801,7 @@
             jax.ShapeDtypeStruct((count, width), jnp.bfloat16),
             jax.ShapeDtypeStruct((3, width), jnp.float32),
         ],
-        compiler_params=pltpu.CompilerParams(vmem_limit_bytes=40 << 20),
+        compiler_params=pltpu.CompilerParams(vmem_limit_bytes=12 << 20),
         cost_estimate=pl.CostEstimate(
             flops=30 * count * width, bytes_accessed=7 << 20, transcendentals=0
         ),
@@ -780,7 +837,7 @@
             jax.ShapeDtypeStruct((count, width), jnp.bfloat16),
             jax.ShapeDtypeStruct((3, width), jnp.float32),
         ],
-        compiler_params=pltpu.CompilerParams(vmem_limit_bytes=40 << 20),
+        compiler_params=pltpu.CompilerParams(vmem_limit_bytes=12 << 20),
         cost_estimate=pl.CostEstimate(
             flops=2 * count * width * width, bytes_accessed=9 << 20, transcendentals=0
         ),
@@ -789,10 +846,11 @@
 
 
 def attn_grads_kernel(
-    place_ref, dq_ref, dk_ref, dv_ref, o_ref, da_ref, x_ref, w_ref, sums_ref, parts_ref
+    place_ref, dq_ref, dk_ref, dv_ref, o_ref, da_ref, x_ref, w_ref, sums_ref, *parts
 ):
     core, shard, across = place_ref[0], place_ref[1], place_ref[3]
-    depth = parts_ref.shape[5]
+    grad_ref = parts[2]
+    depth = x_ref.shape[1] // 2
     part = depth // 4
     sides = (
         (dq_ref, x_ref),
@@ -801,20 +859,18 @@
         (o_ref, da_ref),
     )
     for m, (left, right) in enumerate(sides):
-        grad = contract_rows(left[...], right[...]).astype(jnp.bfloat16)
+        grad_ref[...] = contract_rows(left[...], right[...]).astype(jnp.bfloat16)
         group = across if m < 2 else 1 - across
         rows = slice((m % 2) * part, (m % 2 + 1) * part)
         for z in (0, 1):
             for c in (0, 1):
-                piece = grad[(2 * z + c) * part : (2 * z + c + 1) * part]
-                to = c + core - 2 * c * core
-                parts_ref[to, group, shard, z, rows] = piece[:, :depth]
-                parts_ref[to, group, 1 - shard, z, rows] = piece[:, depth:]
-    extra = sums_ref.shape[3]
+                at = pl.ds(pl.multiple_of((2 * z + c + core - 2 * c * core) * part, part), part)
+                parts[c][shard, group, z, rows] = grad_ref[at, :depth]
+                parts[c][1 - shard, group, z, rows] = grad_ref[at, depth:]
     for c in (0, 1):
         for y in (0, 1):
-            parts_ref[c, across, y, :, 2 * part :] = sums_ref[c, 0]
-            parts_ref[c, 1 - across, y, :, 2 * part :] = sums_ref[c, 1]
+            parts[c][y, across, :, 2 * part :] = sums_ref[c, 0]
+            parts[c][y, 1 - across, :, 2 * part :] = sums_ref[c, 1]
 
 
 def attn_grads(place, grad_queries, grad_keys, grad_values, mixed, grad_attn, rows, near, sums):
@@ -840,10 +896,11 @@
                 whole((window, width)),
                 pl.BlockSpec((2, 2, 2, extra, depth), lambda i, _: (0, 0, i, 0, 0)),
             ],
-            out_specs=pl.BlockSpec((2, 2, 2, 2, high, depth), lambda i, _: (0, 0, 0, i, 0, 0)),
-        ),
-        out_shape=jax.ShapeDtypeStruct((2, 2, 2, 4, high, depth), jnp.bfloat16),
-        compiler_params=pltpu.CompilerParams(vmem_limit_bytes=48 << 20),
+            out_specs=[pl.BlockSpec((2, 2, 2, high, depth), lambda i, _: (0, 0, i, 0, 0))] * 2,
+            scratch_shapes=[pltpu.VMEM((depth, width), jnp.bfloat16)],
+        ),
+        out_shape=[jax.ShapeDtypeStruct((2, 2, 4, high, depth), jnp.bfloat16)] * 2,
+        compiler_params=pltpu.CompilerParams(vmem_limit_bytes=24 << 20),
         cost_estimate=pl.CostEstimate(
             flops=4 * (window + count) * width * width, bytes_accessed=16 << 20, transcendentals=0
         ),
@@ -852,20 +909,35 @@
 
 
 def span_grads_kernel(
-    place_ref, dq_ref, dk_ref, dv_ref, w_ref, base_ref, own_ref, onward_ref, give_ref
+    place_ref,
+    dq_ref,
+    dk_ref,
+    dv_ref,
+    w_ref,
+    base_ref,
+    own_ref,
+    first_ref,
+    second_ref,
+    give_ref,
+    near,
 ):
     core = place_ref[0]
     count, reach = own_ref.shape[0], give_ref.shape[0]
-
-    def near(rows):
-        return dot32(dk_ref[rows], w_ref[1]) + dot32(dv_ref[rows], w_ref[2])
-
     far = count + reach
-    low = pl.ds(pl.multiple_of(core * far, QBLOCK), reach)
-    high = pl.ds(pl.multiple_of((1 - core) * far, QBLOCK), reach)
-    give_ref[...] = near(high).astype(jnp.bfloat16)
-    onward_ref[...] = near(low).astype(jnp.bfloat16)
-    own_ref[...] = base_ref[...] + dot32(dq_ref[...], w_ref[0]) + near(pl.ds(reach, count))
+    size = near.shape[0] // 4
+
+    @pl.loop(0, 4)
+    def _(step):
+        rows = pl.ds(pl.multiple_of(step * size, 32), size)
+        near[rows] = dot32(dk_ref[rows], w_ref[1]) + dot32(dv_ref[rows], w_ref[2])
+
+    def rows_at(start, size):
+        return near[pl.ds(pl.multiple_of(start, QBLOCK), size)].astype(jnp.bfloat16)
+
+    give_ref[...] = rows_at((1 - core) * far, reach)
+    first_ref[...] = rows_at(jnp.where(core == 0, reach - count, far), count)
+    second_ref[...] = rows_at(jnp.where(core == 0, 0, far + count), reach - count)
+    own_ref[...] = base_ref[...] + dot32(dq_ref[...], w_ref[0]) + near[reach:far]
 
 
 def span_grads(place, grad_queries, grad_keys, grad_values, weights, base):
@@ -875,13 +947,15 @@
     return pl.pallas_call(
         span_grads_kernel,
         in_specs=[pl.BlockSpec(memory_space=pltpu.SMEM)] + [vmem] * 5,
-        out_specs=[vmem] * 3,
+        out_specs=[vmem] * 4,
         out_shape=[
             jax.ShapeDtypeStruct((count, width), jnp.float32),
-            jax.ShapeDtypeStruct((reach, width), jnp.bfloat16),
+            jax.ShapeDtypeStruct((count, width), jnp.bfloat16),
+            jax.ShapeDtypeStruct((reach - count, width), jnp.bfloat16),
             jax.ShapeDtypeStruct((reach, width), jnp.bfloat16),
         ],
-        compiler_params=pltpu.CompilerParams(vmem_limit_bytes=40 << 20),
+        scratch_shapes=[pltpu.VMEM(grad_keys.shape, jnp.float32)],
+        compiler_params=pltpu.CompilerParams(vmem_limit_bytes=16 << 20),
         cost_estimate=pl.CostEstimate(
             flops=4 * (count + 2 * reach) * width * width,
             bytes_accessed=12 << 20,
@@ -889,6 +963,125 @@
         ),
         name="span_grads",
     )(place, grad_queries, grad_keys, grad_values, weights, base)
+
+
+def assemble_kernel(place_ref, one, two, three, four, halves, out_ref):
+    core, tp, across = place_ref[0], place_ref[2], place_ref[3]
+    block = out_ref.shape[1]
+    part = block // 2
+    mine = pl.ds(pl.multiple_of(core * part, part), part)
+    other = pl.ds(pl.multiple_of((1 - core) * part, part), part)
+    for k, source in enumerate((one, two, three, four)):
+        z = (tp + 4 - k) & 3
+        group, side = 3 * (z >> 1), z & 1
+        out_ref[group + jnp.where(side == 1, 1, 2 * across)] = source[:block].astype(out_ref.dtype)
+        foreign = group + 2 - 2 * across
+
+        @pl.when(((side + across + core) & 1) == 1)
+        def _():
+            out_ref[foreign, mine] = source[block:].astype(out_ref.dtype)
+            out_ref[foreign, other] = halves[k].astype(out_ref.dtype)
+
+
+def assemble_late_kernel(place_ref, one, two, three, four, middle, foreign, out_ref):
+    core, tp, across = place_ref[0], place_ref[2], place_ref[3]
+    block = out_ref.shape[1]
+    part = block // 2
+    for k, source in enumerate((one, two, three, four)):
+        z = (tp + 4 - k) & 3
+        group, side = 3 * (z >> 1), z & 1
+        at = group + jnp.where(side == 1, 1, 2 * across)
+        odd = (across + side) & 1
+
+        @pl.when(jnp.logical_and(odd == 0, core == 0))
+        def _():
+            out_ref[at] = source[:block]
+
+        @pl.when(jnp.logical_and(odd == 0, core == 1))
+        def _():
+            out_ref[at, :part] = middle[k]
+            out_ref[at, part:] = source[:part]
+
+        @pl.when(jnp.logical_and(odd == 1, core == 0))
+        def _():
+            out_ref[at, :part] = source[block:]
+            out_ref[at, part:] = middle[k]
+
+        @pl.when(jnp.logical_and(odd == 1, core == 1))
+        def _():
+            out_ref[at] = source[part:]
+
+        @pl.when(((side + across + core) & 1) == 1)
+        def _():
+            out_ref[group + 2 - 2 * across] = foreign[k // 2]
+
+
+def assemble(kernel, place, pieces, others, seqs, dtype):
+    rows, width = pieces[0].shape
+    vmem = pl.BlockSpec(memory_space=pltpu.VMEM)
+    return pl.pallas_call(
+        kernel,
+        in_specs=[pl.BlockSpec(memory_space=pltpu.SMEM)] + [vmem] * (4 + len(others)),
+        out_specs=vmem,
+        out_shape=jax.ShapeDtypeStruct((seqs, rows * 2 // 3, width), dtype),
+        compiler_params=pltpu.CompilerParams(vmem_limit_bytes=10 << 20),
+        cost_estimate=pl.CostEstimate(flops=1 << 20, bytes_accessed=8 << 20, transcendentals=0),
+        name="assemble",
+    )(place, *pieces, *others)
+
+
+def finish_ffn_kernel(place_ref, mine, across_got, core_got, both_got, up_ref, down_ref):
+    core, across = place_ref[0], place_ref[3]
+    depth = mine.shape[1]
+    part = depth // 2
+    for c, x, source in (
+        (core, across, mine),
+        (core, 1 - across, across_got),
+        (1 - core, across, core_got),
+        (1 - core, 1 - across, both_got),
+    ):
+        rows = pl.ds(pl.multiple_of(x * part, part), part)
+        up_ref[rows, half_cols(c, depth)] = source[:part].astype(jnp.float32)
+        rows = pl.ds(pl.multiple_of(c * depth + x * part, part), part)
+        down_ref[rows] = source[part:].astype(jnp.float32)
+
+
+def finish_attn_kernel(
+    place_ref, mine, across_got, core_got, both_got, q_ref, k_ref, v_ref, o_ref, sums_ref
+):
+    core, across = place_ref[0], place_ref[3]
+    part = q_ref.shape[0] // 2
+    for c, x, source in (
+        (core, across, mine),
+        (core, 1 - across, across_got),
+        (1 - core, across, core_got),
+        (1 - core, 1 - across, both_got),
+    ):
+        rows = pl.ds(pl.multiple_of(c * part, part), part)
+        one = source[:part].astype(jnp.float32)
+        two = source[part : 2 * part].astype(jnp.float32)
+        sums_ref[c, x] = source[2 * part :].astype(jnp.float32)
+
+        @pl.when(x == 0)
+        def _():
+            q_ref[rows], k_ref[rows] = one, two
+
+        @pl.when(x == 1)
+        def _():
+            v_ref[rows], o_ref[rows] = one, two
+
+
+def finish(kernel, place, pieces, shapes, name):
+    vmem = pl.BlockSpec(memory_space=pltpu.VMEM)
+    return pl.pallas_call(
+        kernel,
+        in_specs=[pl.BlockSpec(memory_space=pltpu.SMEM)] + [vmem] * 4,
+        out_specs=[vmem] * len(shapes),
+        out_shape=[jax.ShapeDtypeStruct(shape, jnp.float32) for shape in shapes],
+        compiler_params=pltpu.CompilerParams(vmem_limit_bytes=8 << 20),
+        cost_estimate=pl.CostEstimate(flops=1 << 20, bytes_accessed=4 << 20, transcendentals=0),
+        name=name,
+    )(place, *pieces)
 
 
 def ctx_swap(array, bit):
@@ -924,9 +1117,11 @@
     return pairs
 
 
-def tp_shifts(array):
+def tp_shifts(array, cuts=(slice(None), slice(None), slice(None))):
     return [
-        lax.ppermute(array, "tp", [(i, (i + shift) % 4) for i in range(4)]) for shift in (1, 2, 3)
+        lax.ppermute(array[cut], "tp", [(i, (i + shift) % 4) for i in range(4)])
+        for shift, cut in zip((1, 2, 3), cuts)
+        if cut is not None
     ]
 
 
@@ -957,13 +1152,22 @@
     return sum(part.astype(jnp.float32) for part in moved).astype(jnp.bfloat16)
 
 
-def chain_pairs():
+def chain_pairs(turn):
     pairs = []
     for group in (0, 2):
         path = [(0, group), (0, group + 1), (1, group + 1), (1, group)]
         for (across, tp), (next_across, next_tp) in zip(path[:-1], path[1:]):
-            pairs.append((at(across, 1, tp), at(next_across, 0, next_tp)))
-            pairs.append((at(next_across, 0, next_tp), at(across, 1, tp)))
+            pairs.append((at(across, 1, tp), at(next_across, 1 ^ turn, next_tp)))
+            pairs.append((at(next_across, 0, next_tp), at(across, turn, tp)))
+    return pairs
+
+
+def block_pairs(core):
+    pairs = []
+    for tp in range(4):
+        for across in (0, 1):
+            source = 1 ^ across ^ (tp & 1)
+            pairs.append((at(across, source, tp), at(1 - across, core, tp)))
     return pairs
 
 
@@ -1026,12 +1230,17 @@
     mine = lax.dynamic_slice_in_dim(layer_input, first_seq + across, 2, 0)
     theirs = across_swap(lax.dynamic_slice_in_dim(layer_input, first_seq + 1 - across, 2, 0))
     in_shifted = tp_shifts(own_in)
-    rest_far = [shard_swap(own_rest)]
-    *in_shifted, theirs, rest_far[0] = tie(*in_shifted, theirs, rest_far[0])
+    far_rest = shard_swap(own_rest)
+    *in_shifted, theirs, far_rest = tie(*in_shifted, theirs, far_rest)
     in_near = jnp.stack([own_in] + in_shifted)
-    rest_near = [own_rest] + tp_shifts(tie(own_rest, in_near)[0])
-    in_far, rest_near[1] = tie(shard_swap(in_near), rest_near[1])
+    (rest_one,) = tp_shifts(tie(own_rest, in_near)[0], (slice(None), None, None))
+    own_pair = jnp.stack([own_rest[: 2 * cut], far_rest[: 2 * cut]])
+    in_far, rest_one, own_pair = tie(shard_swap(in_near), rest_one, own_pair)
     in_mine = jnp.stack([in_near, in_far])
+    own_late = tie(own_rest, in_far)[0]
+    (rest_three,) = tp_shifts(own_late, (None, None, slice(None)))
+    (some_two,) = tp_shifts(own_late, (None, slice(cut, None), None))
+    (up_two,) = tp_shifts(own_late, (None, slice(cut), None))
     in_other = core_swap(in_mine)
     bias_rows = in_mine[0, :, 3 * half]
     in_biases = by_tp(bias_rows[0], [bias_rows[1], bias_rows[2], bias_rows[3]]).astype(f32)
@@ -1051,53 +1260,83 @@
     query_docs = window_docs[reach : reach + count].reshape(-1, 1, QBLOCK)
 
     place = jnp.stack([core, shard, tp, across, start])
-    far_one = shard_swap(rest_near[1])
+    far_one = shard_swap(rest_one)
     queries, keys, values, in_window, weights_t = project(
         place, in_mine, in_other, pair, pair_other, in_biases, count, window
     )
     rows_in = in_window[reach : reach + count]
-    queries, rest_near[3], far_one = tie(queries, rest_near[3], far_one)
-    far_three = shard_swap(rest_near[3])
-    mixed, logs = attend(queries, keys, values, key_docs, query_docs, reach)
-    mixed, far_three, rest_near[2] = tie(mixed, far_three, rest_near[2])
-    far_two = shard_swap(rest_near[2])
-    rest_far += [far_one, far_two, far_three]
-    rest = jnp.stack([jnp.stack(both) for both in zip(rest_near, rest_far)])
-    out_mine = rest[:, :, 2 * cut :]
+    queries, far_one, out_cotangent = tie(queries, far_one, out_cotangent)
+    split = width // PAIR // 2
+    attention = queries, keys, values, key_docs, query_docs, reach
+    mixed, logs = attend(*attention, 0, split)
+    mixed, rest_three, some_two = tie(mixed, rest_three, some_two)
+    far_three, far_some_two = shard_swap(rest_three), shard_swap(some_two)
+    mixed, logs = attend(*attention, split, width // PAIR - split, (mixed, logs))
+    mixed, far_three, far_some_two, up_two = tie(mixed, far_three, far_some_two, up_two)
+    far_up_two = shard_swap(up_two)
+    out_mine = jnp.stack(
+        [
+            jnp.stack([one[-out_half:], two[-out_half:]])
+            for one, two in (
+                (own_rest, far_rest),
+                (rest_one, far_one),
+                (some_two, far_some_two),
+                (rest_three, far_three),
+            )
+        ]
+    )
     attn_vectors = jnp.stack([out_bias, attn_gain, attn_shift]).astype(f32)
     hidden, hidden_low, normed_one, inv_one, full_out = attend_out(
         place, mixed, rows_in, out_mine, core_swap(out_mine), attn_vectors
     )
-    hidden_both = jnp.concatenate([hidden_low, core_swap(hidden_low)], axis=0)
-    acts, slope, ffn_own, ffn_other = ffn(place, hidden_both, rest, up_bias_here)
+    hidden_other = core_swap(hidden_low)
+    hidden_both = jnp.concatenate([hidden_low, hidden_other], axis=0)
+    ffn_weights = jnp.stack(
+        [
+            own_pair,
+            jnp.stack([rest_one[: 2 * cut], far_one[: 2 * cut]]),
+            jnp.stack([rest_three[: 2 * cut], far_three[: 2 * cut]]),
+            own_pair,
+        ]
+    )
+    ffn_bias = jnp.stack([up_bias_here[k] for k in (0, 1, 3, 2)])
+    acts, slope, ffn_sum = ffn(place, hidden_both, ffn_weights, ffn_bias, 3)
+    ffn_sum, far_up_two = tie(ffn_sum, far_up_two)
+    rest = ffn_weights.at[3].set(
+        jnp.stack(
+            [
+                jnp.concatenate([up_two, some_two[:cut]], axis=0),
+                jnp.concatenate([far_up_two, far_some_two[:cut]], axis=0),
+            ]
+        )
+    )
+    acts, slope, ffn_own, ffn_other = ffn(
+        place, hidden_both, rest, ffn_bias, 1, (ffn_sum, acts, slope)
+    )
+
+    half_block = block // 2
 
     def deliver_start(rows):
-        chip = jnp.concatenate(in_order(core, rows, core_swap(rows)), axis=0)
-        kept = lax.dynamic_slice_in_dim(chip, odd * block + core * block, block, 0)
-        half_block = block // 2
-        sent = lax.dynamic_slice_in_dim(
-            chip, (1 - odd) * 2 * block + core * half_block, half_block, 0
+        far_rows = jnp.where(odd == 0, rows[-block:], rows[:block])
+        return (
+            core_swap(jnp.where(odd == 0, rows[block:], rows[:half_block])),
+            lax.ppermute(far_rows[:half_block], ("ctx", "tp"), block_pairs(0)),
+            lax.ppermute(far_rows[half_block:], ("ctx", "tp"), block_pairs(1)),
         )
-        packed = jnp.concatenate([kept, across_swap(sent)], axis=0)
-        return packed, tp_shifts(packed)
-
-    def deliver_end(packed, shifted):
-        every = by_tp(packed, shifted)
-        halves = every[:, block:]
-        lo, hi = in_order(core, halves, core_swap(halves))
-        moved = jnp.concatenate([lo, hi], axis=1)
-        kept_all = every[:, :block]
-        from_side = 1 ^ across ^ core
-        parts = []
-        for group in (0, 2):
-            foreign = lax.dynamic_index_in_dim(moved, group + from_side, 0, keepdims=False)
-            near_one, mid_one = kept_all[group], kept_all[group + 1]
-            parts += [
-                jnp.where(across == 0, near_one, foreign),
-                mid_one,
-                jnp.where(across == 0, foreign, near_one),
-            ]
-        return jnp.stack(parts)
+
+    def deliver_pack(rows, middle, low, high):
+        where_kept = [
+            rows[:block],
+            jnp.concatenate([middle, rows[:half_block]], axis=0),
+            jnp.concatenate([rows[block:], middle], axis=0),
+            rows[half_block:],
+        ]
+        kept = jnp.where(
+            odd == 0,
+            jnp.where(core == 0, where_kept[0], where_kept[1]),
+            jnp.where(core == 0, where_kept[2], where_kept[3]),
+        )
+        return jnp.concatenate([kept, low + high], axis=0)
 
     near_cot = lax.dynamic_index_in_dim(
         out_cotangent, first_seq + odd + across, 0, keepdims=False
@@ -1123,38 +1362,49 @@
     output_rows, grad_two, grad_ffn, ffn_sums = ffn_norm(
         hidden, ffn_own, core_swap(ffn_other), cot_rows, ffn_vectors
     )
-    grad_ffn_both = jnp.concatenate([grad_ffn, core_swap(grad_ffn)], axis=0)
-    out_packed, out_shifted = deliver_start(output_rows)
-    grad_ffn_both, out_packed = lax.optimization_barrier((grad_ffn_both, out_packed))
-    back_own, back_other, up_parts, down_parts, up_sums = ffn_back(
+    grad_other = core_swap(grad_ffn)
+    grad_ffn_both = jnp.concatenate([grad_ffn, grad_other], axis=0)
+    out_pieces = [output_rows] + tp_shifts(output_rows)
+    back_own, back_other, up_keep, up_give, down_keep, down_give, up_sums = ffn_back(
         place, grad_ffn_both, hidden_both, acts, slope, rest
     )
-    back_own, out_shifted[0] = tie(back_own, out_shifted[0])
+    back_own, out_pieces[1] = tie(back_own, out_pieces[1])
     grad_one, grad_attn, grad_mixed, attn_sums = attend_norm(
         grad_two, back_own, core_swap(back_other), normed_one, inv_one, attn_vectors, full_out
     )
-    up_got = across_swap(up_parts[1])
-    down_got = shard_swap(down_parts[1])
+    up_got = across_swap(up_give)
+    down_got = shard_swap(down_give)
+    attention = queries, keys, values, key_docs, query_docs, grad_mixed, logs, reach
+    back = attend_back(*attention, 0, split)
+    *back, up_got, down_got, out_pieces[3] = tie(*back, up_got, down_got, out_pieces[3])
+    up_parts, down_parts = low_sum(up_keep, up_got), low_sum(down_keep, down_got)
+    up_got, down_got = shard_swap(up_parts[1]), across_swap(down_parts[1])
     grad_scaled, grad_keys, grad_values = attend_back(
-        queries, keys, values, key_docs, query_docs, grad_mixed, logs, reach
-    )
-    grad_keys, grad_values, up_got, down_got = tie(grad_keys, grad_values, up_got, down_got)
-    up_parts = low_sum(up_parts[0], up_got)
-    down_parts = low_sum(down_parts[0], down_got)
-    up_got = shard_swap(up_parts[1])
-    down_got = across_swap(down_parts[1])
-    own_sum, onward, give = span_grads(
+        *attention, split, width // PAIR - split, back
+    )
+    grad_keys, up_got, down_got, out_pieces[2] = tie(grad_keys, up_got, down_got, out_pieces[2])
+    ffn_parts = jnp.concatenate(
+        [low_sum(up_parts[0], up_got), low_sum(down_parts[0], down_got)], axis=1
+    )
+    ffn_near = scatter_tp_start(ffn_parts)
+    own_sum, first, second, give = span_grads(
         place, grad_scaled, grad_keys, grad_values, weights_t, grad_one
     )
     got = core_swap(give)
-    got, *out_shifted = tie(got, *out_shifted)
     shared = reach - count
     to_own = lax.dynamic_slice_in_dim(got, (1 - core) * shared, count, 0)
     to_next = lax.dynamic_slice_in_dim(got, core * count, shared, 0)
-    next_at = (1 - core) * count
-    to_next = low_sum(lax.dynamic_slice_in_dim(onward, next_at, shared, 0), to_next)
-    onward = lax.dynamic_update_slice_in_dim(onward, to_next, next_at, 0)
-    arrived = lax.ppermute(onward, ("ctx", "tp"), chain_pairs())
+    no_rows = jnp.zeros((count - shared, width), bf16)
+    first = low_sum(
+        first,
+        jnp.where(
+            core == 0,
+            jnp.concatenate([no_rows, to_next], axis=0),
+            jnp.concatenate([to_next, no_rows], axis=0),
+        ),
+    )
+    first_got = lax.ppermute(first, ("ctx", "tp"), chain_pairs(1))
+    second_got = lax.ppermute(second, ("ctx", "tp"), chain_pairs(0))
     head_sums = jnp.concatenate(
         [
             jnp.sum(grad_scaled, axis=0, dtype=f32).reshape(4, 1, heads),
@@ -1175,7 +1425,7 @@
         ]
     )
     sums = sums.reshape(2, 4, 2, 8, depth).transpose(0, 2, 1, 3, 4)
-    grad_keys, onward = tie(grad_keys, onward)
+    grad_keys, first_now = tie(grad_keys, first)
     attn_parts = attn_grads(
         place,
         grad_scaled,
@@ -1187,58 +1437,75 @@
         in_window,
         sums,
     )
-    arrived, up_got, down_got, attn_parts = tie(arrived, up_got, down_got, attn_parts)
-    ffn_parts = jnp.concatenate(
-        [low_sum(up_parts[0], up_got), low_sum(down_parts[0], down_got)], axis=1
-    )
-    ffn_near = scatter_tp_start(ffn_parts)
-    attn_parts = low_sum(attn_parts[0], core_swap(attn_parts[1]))
-    passed = core_swap(lax.dynamic_slice_in_dim(arrived, next_at, shared, 0)).astype(f32)
-    own_sum += to_own.astype(f32)
-    own_sum += lax.dynamic_slice_in_dim(arrived, core * shared, count, 0).astype(f32)
-    rest_rows = jnp.zeros((count - shared, width), f32)
+    first_got, second_got, attn_keep, attn_give, ffn_near[1] = tie(
+        first_got, second_got, *attn_parts, ffn_near[1]
+    )
+    attn_core = core_swap(attn_give)
+    own_sum += to_own.astype(f32) + first_got.astype(f32)
     own_sum += jnp.where(
         core == 0,
-        jnp.concatenate([rest_rows, passed], axis=0),
-        jnp.concatenate([passed, rest_rows], axis=0),
-    )
-    own_sum, attn_parts = tie(own_sum, attn_parts)
-    attn_got = across_swap(attn_parts[1])
-    in_packed, in_moved = deliver_start(own_sum.astype(bf16))
-    attn_got, ffn_near = tie(attn_got, ffn_near)
-    attn_mid = low_sum(attn_parts[0], attn_got)
-    attn_got = shard_swap(attn_mid[1])
+        jnp.concatenate([no_rows, second_got], axis=0),
+        jnp.concatenate([second_got, no_rows], axis=0),
+    ).astype(f32)
+    own_low = own_sum.astype(bf16)
+    in_moves = deliver_start(own_low)
+    *in_moves, attn_core, ffn_near[3] = tie(*in_moves, attn_core, ffn_near[3])
+    in_packed = deliver_pack(own_low, *in_moves)
+    in_pieces = [in_packed] + tp_shifts(in_packed)
+    attn_parts = low_sum(attn_keep, attn_core)
+    attn_got = shard_swap(attn_parts[1])
+    parity = (tp + 1 + across + core) & 1
+    out_sent = [
+        jnp.where(
+            core == 0,
+            jnp.where(parity == 0, even[:block], odd_one[:block]),
+            jnp.where(parity == 0, even[-block:], odd_one[-block:]),
+        )
+        for even, odd_one in (out_pieces[:2], out_pieces[2:])
+    ]
+    out_foreign = lax.ppermute(jnp.stack(out_sent), "ctx", [(i, 3 - i) for i in range(4)])
+    out_middle = core_swap(
+        jnp.stack(
+            [
+                jnp.where(((across + tp + k) & 1) == 0, piece[block:], piece[:half_block])
+                for k, piece in enumerate(out_pieces)
+            ]
+        )
+    )
+    attn_got, in_pieces[1], ffn_near[2] = tie(attn_got, in_pieces[1], ffn_near[2])
     ffn_low = scatter_tp_end(ffn_near)
     ffn_got = across_swap(ffn_low)
-    in_moved, attn_got, ffn_got = tie(in_moved, attn_got, ffn_got)
+    attn_mid = low_sum(attn_parts[0], attn_got)
+    attn_got = across_swap(attn_mid[1])
+    attn_got, in_pieces[3], ffn_got, out_middle, out_foreign = tie(
+        attn_got, in_pieces[3], ffn_got, out_middle, out_foreign
+    )
     attn_near = scatter_tp_start(low_sum(attn_mid[0], attn_got))
-    layer_output = deliver_end(out_packed, out_shifted)
-    input_grad = deliver_end(in_packed, in_moved).astype(f32)
-
-
-    def spread(low, got):
-        mine = jnp.stack(in_order(across, low, got))
-        return in_order(core, mine, core_swap(mine))
-
-    ffn_lo, ffn_hi = spread(ffn_low, ffn_got)
+    layer_output = assemble(
+        assemble_late_kernel, place, out_pieces, (out_middle, out_foreign), seqs, bf16
+    )
+    layer_output, in_pieces[2] = tie(layer_output, in_pieces[2])
+    in_halves = core_swap(jnp.stack([piece[block:] for piece in in_pieces]))
+    input_grad = assemble(assemble_kernel, place, in_pieces, (in_halves,), seqs, f32)
+    up_grad, down_grad = finish(
+        finish_ffn_kernel,
+        place,
+        (ffn_low, ffn_got, core_swap(ffn_low), core_swap(ffn_got)),
+        ((cut, 2 * cut), (2 * cut, cut)),
+        "finish_ffn",
+    )
     attn_low = scatter_tp_end(attn_near)
-    attn_lo, attn_hi = spread(attn_low, across_swap(attn_low))
-    quarter = cut // 2
-    up_grad, down_grad = (
-        [part[:, at : at + quarter].reshape(cut, cut) for part in (ffn_lo, ffn_hi)]
-        for at in (0, quarter)
-    )
-    up_grad = jnp.concatenate(up_grad, axis=1).astype(f32)
-    down_grad = jnp.concatenate(down_grad, axis=0).astype(f32)
-    weight_grads = [
-        jnp.concatenate(
-            [part[m // 2, (m % 2) * half : (m % 2 + 1) * half] for part in (attn_lo, attn_hi)], axis=0
-        ).astype(f32)
-        for m in range(4)
-    ]
-    sums = attn_lo[:, 2 * half :].astype(f32).reshape(16, depth)
+    attn_got, input_grad = tie(across_swap(attn_low), input_grad)
+    *weight_grads, sums = finish(
+        finish_attn_kernel,
+        place,
+        (attn_low, attn_got, core_swap(attn_low), core_swap(attn_got)),
+        ((heads, depth),) * 4 + ((2, 2, 8, depth),),
+        "finish_attn",
+    )
+    up_bias_grad = sums[:, 1, 5].reshape(-1)
+    sums = sums[0].reshape(16, depth)
     row_sums = sums[1:13].reshape(6, width)
-    up_bias_grad = jnp.concatenate([sums[13], attn_hi[1, 2 * half + 5].astype(f32)])
     return (
         layer_output,
         input_grad,

time: 436 us -> 392 us (0.90)
  starting transfers between devices: 89.6 us -> 63.6 us
  local copies, waits for them, and re-layouts: 67.4 us -> 48.2 us
  Pallas kernels: 105 us -> 117 us
  other arithmetic: 39.5 us -> 33.2 us
    ppermute x6, waiting for transfers between devices: 3.73 us -> 37 us  [scatter_tp_start(): lax.ppermute(sent, 'tp', [(i, (i + shift) % 4) for i in range(4)])]
    ppermute x25 -> x23, waiting for transfers between devices: 37.9 us -> 10.9 us  [ctx_swap(): return lax.ppermute(array, 'ctx', [(i, i ^ bit) for i in range(4)])]
    ppermute x6, starting transfers between devices: 21.8 us -> 4.1 us  [scatter_tp_start(): lax.ppermute(sent, 'tp', [(i, (i + shift) % 4) for i in range(4)])]
    unnamed x195 -> x148, local copies, waits for them, and re-layouts: 43.3 us -> 26.3 us
    ppermute x13 -> x18, starting transfers between devices: 37.2 us -> 23.3 us  [the longest x13 11.8 us: tp_shifts(): lax.ppermute(array[cut], 'tp', [(i, (i + shift) % 4) for i in range(4)])]
    pallas_call x0 -> x4, Pallas kernels: none -> 10.6 us  [the longest x2 6.86 us: assemble(): pl.pallas_call(kernel, in_specs=[pl.BlockSpec(memory_space=pltpu.SMEM)] +...]
    another operation x1 -> x19, local copies, waits for them, and re-layouts: 0.01 us -> 7.45 us  [the longest x8 2.48 us: span_shards(): jnp.stack([one[-out_half:], two[-out_half:]])]
    squeeze x9 -> x4, local copies, waits for them, and re-layouts: 8.03 us -> 1.19 us  [the longest x1 0.95 us: span_shards(): attn_got = across_swap(attn_mid[1])]
  transfers between devices with their start and end apart: 53 -> 57, of which waited for: 16 -> 21; matrix products, arithmetic and copies ran while one was open for 14% -> 11% of each run, Pallas kernels for 24% -> 28%
where the time goes in v3:
time: 392 us; the launch traced here: 385 us
  waiting for transfers between devices  121 us (31%)
  Pallas kernels  117 us (30%)
  starting transfers between devices  63.6 us (16%)
  local copies, waits for them, and re-layouts  48.2 us (12%)
  other arithmetic  33.2 us (8%)
    ppermute x13, waiting for transfers between devices, tp_shifts(): lax.ppermute(array[cut], 'tp', [(i, (i + shift) % 4) for i in range(4)])  55.2 us
    ppermute x6, waiting for transfers between devices, scatter_tp_start(): lax.ppermute(sent, 'tp', [(i, (i + shift) % 4) for i in range(4)])  37 us
    pallas_call x2, Pallas kernels, attend_back(): pl.pallas_call(partial(attend_back_kernel, span), grid=(pairs, blocks), i...  26.9 us
    unnamed x148, local copies, waits for them, and re-layouts  26.3 us
    ppermute x23, starting transfers between devices, ctx_swap(): return lax.ppermute(array, 'ctx', [(i, i ^ bit) for i in range(4)])  25 us
    pallas_call x2, Pallas kernels, attend(): pl.pallas_call(partial(attend_kernel, span), grid=(pairs, blocks), in_spe...  21.2 us
    pallas_call x1, Pallas kernels, ffn_back(): pl.pallas_call(ffn_back_kernel, grid_spec=pltpu.PrefetchScalarGridSpec(nu...  19 us
    ppermute x9, waiting for transfers between devices, shard_swap(): return lax.ppermute(array, 'shard', [(0, 1), (1, 0)])  14.1 us
  transfers between devices with their start and end apart: 57, of which 21 were waited for; matrix products, arithmetic and copies ran while one was open for 11% of the time, Pallas kernels for 28%

profile of v3, /device:TPU:1, one launch (start us, length us, event | category | flops | bytes accessed | tf_op | source)
XLA Modules:
  0.0 384.7 jit_solution(14412981459722844678)
XLA Ops:
  16.1 7.8 %collective-permute-done.1 = bf16[304,384]{1,0:T(8,128)(2,1)} collective-permute-done((bf16[304,384]{1,0:T(8,128)(2,1)S(1)}, bf16[304,384]{1,0:T(8,128)(2,1)}, u32[]{:S(2)}, u32[]{:S(2)}) %collective-permute-start.1) | collective-permute-done | bytes 233504 | tf_op jit(solution)/shard_map/ppermute | solution.py:1122
  23.9 3.7 collective-permute-done.4
  36.7 2.9 collective-permute-start.8
  41.9 7.6 %collective-permute-done.6 = bf16[864,384]{1,0:T(8,128)(2,1)} collective-permute-done((bf16[864,384]{1,0:T(8,128)(2,1)S(1)}, bf16[864,384]{1,0:T(8,128)(2,1)}, u32[]{:S(2)}, u32[]{:S(2)}) %collective-permute-start.6) | collective-permute-done | bytes 663584 | tf_op jit(solution)/shard_map/ppermute | solution.py:1122
  49.6 3.0 collective-permute-done.5
  54.0 3.3 collective-permute-start.7
  66.6 7.7 %project.1 = (bf16[384,768]{1,0:T(8,128)(2,1)S(1)}, bf16[1408,768]{1,0:T(8,128)(2,1)S(1)}, bf16[1408,768]{1,0:T(8,128)(2,1)S(1)}, bf16[1408,768]{1,0:T(8,128)(2,1)S(1)}, bf16[3,768,768]{2,1,0:T(8,128)(2,1)S(1)}) custom-call(s32[5]{0:T(128)S(1)} %stack.262.place_ref, bf16[2,4,304,384]{3,2,1,0:T(8,128)(2,1)S(1)} %pad_maximum_fusion.1.w_mine, ...), custom_call_target="tpu_custom_call" | custom-call | flops 3321888768 | bytes 16777216 | tf_op jit(solution)/shard_map/project/pallas_call | solution.py:695
  75.7 10.6 %attend.2 = (bf16[384,768]{1,0:T(8,128)(2,1)S(1)}, f32[6,3,1,256]{3,2,1,0:T(1,128)S(1)}) custom-call(bf16[384,768]{1,0:T(8,128)(2,1)S(1)} %get-tuple-element.150.q_ref, bf16[1408,768]{1,0:T(8,128)(2,1)S(1)} %get-tuple-element.151.k_ref, bf16[1408,768]{1,0:T(8,128)(2,1)S(1)} %get-tuple-element.152.v_ref, s32[1408,128]{1,0:T(8,128)S(1)} %broadcast_in_dim.18.kd_ref, ...), custom_call_target="tpu_custom_call" | custom-call | flops 2717908992 | bytes 4194304 | tf_op jit(solution)/shard_map/attend/pallas_call | solution.py:390
  86.3 13.5 %collective-permute-done.11 = bf16[480,384]{1,0:T(8,128)(2,1)S(1)} collective-permute-done((bf16[480,384]{1,0:T(8,128)(2,1)S(1)}, bf16[480,384]{1,0:T(8,128)(2,1)S(1)}, u32[]{:S(2)}, u32[]{:S(2)}) %collective-permute-start.11) | collective-permute-done | bytes 368672 | tf_op jit(solution)/shard_map/ppermute | solution.py:1122
  102.7 3.2 collective-permute-start.19
  106.0 10.6 %attend.3 = (bf16[384,768]{1,0:T(8,128)(2,1)S(1)}, f32[6,3,1,256]{3,2,1,0:T(1,128)S(1)}) custom-call(bf16[384,768]{1,0:T(8,128)(2,1)S(1)} %get-tuple-element.150.q_ref, bf16[1408,768]{1,0:T(8,128)(2,1)S(1)} %get-tuple-element.151.k_ref, bf16[1408,768]{1,0:T(8,128)(2,1)S(1)} %get-tuple-element.152.v_ref, ...), custom_call_target="tpu_custom_call", output_to_operand_aliasing={{0}: (5, {}), {1}: (6, {})} | custom-call | flops 2717908992 | bytes 4194304 | tf_op jit(solution)/shard_map/attend/pallas_call | solution.py:390
  116.7 5.5 %collective-permute-done.13 = bf16[480,384]{1,0:T(8,128)(2,1)S(1)} collective-permute-done((bf16[480,384]{1,0:T(8,128)(2,1)S(1)}, bf16[480,384]{1,0:T(8,128)(2,1)S(1)}, u32[]{:S(2)}, u32[]{:S(2)}) %collective-permute-start.13) | collective-permute-done | bytes 368672 | tf_op jit(solution)/shard_map/ppermute | solution.py:1135
  122.4 2.8 collective-permute-start.15
  132.8 8.5 %ffn.2 = (bf16[768,1536]{1,0:T(8,128)(2,1)S(1)}, bf16[768,1536]{1,0:T(8,128)(2,1)S(1)}, f32[768,768]{1,0:T(8,128)S(1)}) custom-call(s32[5]{0:T(128)S(1)} %stack.262.place_ref, bf16[768,768]{1,0:T(8,128)(2,1)S(1)} %constant_dynamic-update-slice_fusion.hb_ref, bf16[4,2,768,384]{3,2,1,0:T(8,128)(2,1)S(1)} %pad_maximum_fusion.up_ref.down_ref, ...), custom_call_target="tpu_custom_call" | custom-call | flops 8153726976 | bytes 9437184 | tf_op jit(solution)/shard_map/ffn/pallas_call | solution.py:576
  150.7 19.0 %ffn_back.1 = (f32[384,768]{1,0:T(8,128)S(1)}, bf16[384,768]{1,0:T(8,128)(2,1)}, bf16[2,4,192,384]{3,2,1,0:T(8,128)(2,1)S(1)}, bf16[2,4,192,384]{3,2,1,0:T(8,128...) custom-call(s32[5]{0:T(128)S(1)} %stack.262.place_ref, ...), custom_call_target="tpu_custom_call" | custom-call | flops 10871635968 | bytes 20971520 | tf_op jit(solution)/shard_map/ffn_back/pallas_call | solution.py:613
  187.2 13.5 %attend_back.2 = (bf16[384,768]{1,0:T(8,128)(2,1)S(1)}, bf16[1408,768]{1,0:T(8,128)(2,1)S(1)}, bf16[1408,768]{1,0:T(8,128)(2,1)S(1)}) custom-call(bf16[384,768]{1,0:T(8,128)(2,1)S(1)} %copy-done.43, bf16[1408,768]{1,0:T(8,128)(2,1)S(1)} %copy-done.39, bf16[1408,768]{1,0:T(8,128)(2,1)S(1)} %copy-done.41, s32[1408,128]{1,0:T(8,128)S(1)} %copy-done.23, ...), custom_call_target="tpu_custom_call" | custom-call | flops 6794772480 | bytes 6291456 | tf_op jit(solution)/shard_map/attend_back/pallas_call | solution.py:416
  208.1 13.5 %attend_back.3 = (bf16[384,768]{1,0:T(8,128)(2,1)S(1)}, bf16[1408,768]{1,0:T(8,128)(2,1)S(1)}, bf16[1408,768]{1,0:T(8,128)(2,1)S(1)}) custom-call(bf16[384,768]{1,0:T(8,128)(2,1)S(1)} %copy-done.43, bf16[1408,768]{1,0:T(8,128)(2,1)S(1)} %copy-done.39, bf16[1408,768]{1,0:T(8,128)(2,1)S(1)} %copy-done.41, ...), custom_call_target="tpu_custom_call", output_to_operand_aliasing={{0}: (7, {}), {1}: (8, {}), {2}: (9, {})} | custom-call | flops 6794772480 | bytes 6291456 | tf_op jit(solution)/shard_map/attend_back/pallas_call | solution.py:416
  222.5 6.3 %span_grads.1 = (f32[384,768]{1,0:T(8,128)S(1)}, bf16[384,768]{1,0:T(8,128)(2,1)S(1)}, bf16[128,768]{1,0:T(8,128)(2,1)S(1)}, bf16[512,768]{1,0:T(8,128)(2,1)}) custom-call(s32[5]{0:T(128)S(1)} %stack.262.place_ref, bf16[384,768]{1,0:T(8,128)(2,1)S(1)} %get-tuple-element.206.dq_ref, bf16[1408,768]{1,0:T(8,128)(2,1)S(1)} %get-tuple-element.214.dk_ref, ...), custom_call_target="tpu_custom_call" | custom-call | flops 3321888768 | bytes 12582912 | tf_op jit(solution)/shard_map/span_grads/pallas_call | solution.py:947
  240.9 3.7 collective-permute-start.31
  249.5 8.1 %attn_grads.1 = (bf16[2,2,4,200,384]{4,3,2,1,0:T(8,128)(2,1)S(1)}, bf16[2,2,4,200,384]{4,3,2,1,0:T(8,128)(2,1)}) custom-call(s32[5]{0:T(128)S(1)} %stack.262.place_ref, bf16[384,768]{1,0:T(8,128)(2,1)S(1)} %copy-done.27, bf16[1408,768]{1,0:T(8,128)(2,1)S(1)} %copy-done.37, bf16[1408,768]{1,0:T(8,128)(2,1)S(1)} %copy-done.5, bf16[384,768]{1,0:T(8,128)(2,1)S(1)} %copy-done.29, ...), custom_call_target="tpu_custom_call" | custom-call | flops 4227858432 | bytes 16777216 | tf_op jit(solution)/shard_map/attn_grads/pallas_call | solution.py:884
  259.9 2.9 collective-permute-start.37
  265.9 2.8 collective-permute-start.35
  272.4 3.3 collective-permute-done.36
  283.9 22.9 %collective-permute-done.41 = bf16[384,384]{1,0:T(8,128)(2,1)S(1)} collective-permute-done((bf16[384,384]{1,0:T(8,128)(2,1)S(1)}, bf16[384,384]{1,0:T(8,128)(2,1)S(1)}, u32[]{:S(2)}, u32[]{:S(2)}) %collective-permute-start.41) | collective-permute-done | bytes 294944 | tf_op jit(solution)/shard_map/ppermute | solution.py:1147
  312.2 12.4 %collective-permute-done.43.four = bf16[384,768]{1,0:T(8,128)(2,1)} collective-permute-done((bf16[384,768]{1,0:T(8,128)(2,1)S(1)}, bf16[384,768]{1,0:T(8,128)(2,1)}, u32[]{:S(2)}, u32[]{:S(2)}) %collective-permute-start.43) | collective-permute-done | bytes 589856 | tf_op jit(solution)/shard_map/ppermute | solution.py:1122
  324.6 6.6 %collective-permute-done.44.across_got = bf16[384,384]{1,0:T(8,128)(2,1)S(1)} collective-permute-done((bf16[384,384]{1,0:T(8,128)(2,1)S(1)}, bf16[384,384]{1,0:T(8,128)(2,1)S(1)}, u32[]{:S(2)}, u32[]{:S(2)}) %collective-permute-start.44) | collective-permute-done | bytes 294944 | tf_op jit(solution)/shard_map/ppermute | solution.py:1088
  331.2 3.1 assemble.2
  334.2 13.8 %collective-permute-done.47.three = bf16[384,768]{1,0:T(8,128)(2,1)} collective-permute-done((bf16[384,768]{1,0:T(8,128)(2,1)S(1)}, bf16[384,768]{1,0:T(8,128)(2,1)}, u32[]{:S(2)}, u32[]{:S(2)}) %collective-permute-start.47) | collective-permute-done | bytes 589856 | tf_op jit(solution)/shard_map/ppermute | solution.py:1122
  352.9 3.3 collective-permute-start.50
  356.6 3.1 collective-permute-done.50
  359.7 9.3 %collective-permute-done.49 = bf16[200,384]{1,0:T(8,128)(2,1)S(1)} collective-permute-done((bf16[200,384]{1,0:T(8,128)(2,1)S(1)}, bf16[200,384]{1,0:T(8,128)(2,1)S(1)}, u32[]{:S(2)}, u32[]{:S(2)}) %collective-permute-start.49) | collective-permute-done | bytes 153632 | tf_op jit(solution)/shard_map/ppermute | solution.py:1147
  371.7 3.8 assemble.3
  (390 shorter events, 139.8 us)
Async XLA Ops:
  5.6 18.3 %collective-permute-start.1 = (bf16[304,384]{1,0:T(8,128)(2,1)S(1)}, bf16[304,384]{1,0:T(8,128)(2,1)}, u32[]{:S(2)}, u32[]{:S(2)}) collective-permute-start(bf16[304,384]{1,0:T(8,128)(2,1)S(1)} %maximum_maximum_fusion), channel_id=1, source_target_pairs={{0,2},{1,3},{2,0},{3,1},{4,6},{5,7},{6,4},{7,5},{8,10},{9,11},{10,... | collective-permute-start | bytes 700424 | tf_op jit(solution)/shard_map/ppermute | solution.py:1122
  7.9 16.0 %collective-permute-start.2 = (bf16[304,384]{1,0:T(8,128)(2,1)S(1)}, bf16[304,384]{1,0:T(8,128)(2,1)}, u32[]{:S(2)}, u32[]{:S(2)}) collective-permute-start(bf16[304,384]{1,0:T(8,128)(2,1)S(1)} %maximum_maximum_fusion), channel_id=1, source_target_pairs={{0,3},{1,0},{2,1},{3,2},{4,7},{5,4},{6,5},{7,6},{8,11},{9,8},{10,9... | collective-permute-start | bytes 700424 | tf_op jit(solution)/shard_map/ppermute | solution.py:1122
  11.4 17.8 %collective-permute-start.3 = (bf16[2,256,768]{2,1,0:T(8,128)(2,1)}, bf16[2,256,768]{2,1,0:T(8,128)(2,1)S(1)}, u32[]{:S(2)}, u32[]{:S(2)}) collective-permute-start(bf16[2,256,768]{2,1,0:T(8,128)(2,1)} %get-tuple-element.256), channel_id=1, source_target_pairs={{0,8},{4,12},{8,0},{12,4},{1,9},{5,13},{9,1},{13,5},{2,10},{6,14},... | collective-permute-start | bytes 2359304 | tf_op jit(solution)/shard_map/ppermute | solution.py:1088
  32.4 20.2 %collective-permute-start.5 = (bf16[4,304,384]{2,1,0:T(8,128)(2,1)}, bf16[4,304,384]{2,1,0:T(8,128)(2,1)}, u32[]{:S(2)}, u32[]{:S(2)}) collective-permute-start(bf16[4,304,384]{2,1,0:T(8,128)(2,1)} %get-tuple-element.267), channel_id=1, source_target_pairs={{0,16},{16,0},{1,17},{17,1},{2,18},{18,2},{3,19},{19,3},{4,20},{20... | collective-permute-start | bytes 2801672 | tf_op jit(solution)/shard_map/ppermute | solution.py:1135
  36.7 29.0 %collective-permute-start.8 = (bf16[2,2,256,768]{3,2,1,0:T(8,128)(2,1)}, bf16[2,2,256,768]{3,2,1,0:T(8,128)(2,1)}, u32[]{:S(2)}, u32[]{:S(2)}) collective-permute-start(bf16[2,2,256,768]{3,2,1,0:T(8,128)(2,1)} %pad_maximum_fusion.2.x_mine), channel_id=1, source_target_pairs={{0,4},{4,0},{8,12},{12,8},{1,5},{5,1},{9,13},{13,9},{2,6},{6,2},{1... | collective-permute-start | bytes 4718600 | tf_op jit(solution)/shard_map/ppermute | solution.py:1088
  58.6 16.8 %collective-permute-start.9 = (bf16[864,384]{1,0:T(8,128)(2,1)}, bf16[864,384]{1,0:T(8,128)(2,1)S(1)}, u32[]{:S(2)}, u32[]{:S(2)}) collective-permute-start(bf16[864,384]{1,0:T(8,128)(2,1)} %collective-permute-done.6), channel_id=1, source_target_pairs={{0,16},{16,0},{1,17},{17,1},{2,18},{18,2},{3,19},{19,3},{4,20},{20... | collective-permute-start | bytes 1990664 | tf_op jit(solution)/shard_map/ppermute | solution.py:1135
  61.1 38.7 %collective-permute-start.10 = (bf16[864,384]{1,0:T(8,128)(2,1)}, bf16[864,384]{1,0:T(8,128)(2,1)S(1)}, u32[]{:S(2)}, u32[]{:S(2)}) collective-permute-start(bf16[864,384]{1,0:T(8,128)(2,1)} %copy-done.51), channel_id=1, source_target_pairs={{0,3},{1,0},{2,1},{3,2},{4,7},{5,4},{6,5},{7,6},{8,11},{9,8},{10,9... | collective-permute-start | bytes 1990664 | tf_op jit(solution)/shard_map/ppermute | solution.py:1122
  64.2 35.6 %collective-permute-start.11 = (bf16[480,384]{1,0:T(8,128)(2,1)S(1)}, bf16[480,384]{1,0:T(8,128)(2,1)S(1)}, u32[]{:S(2)}, u32[]{:S(2)}) collective-permute-start(bf16[480,384]{1,0:T(8,128)(2,1)S(1)} %slice.314), channel_id=1, source_target_pairs={{0,2},{1,3},{2,0},{3,1},{4,6},{5,7},{6,4},{7,5},{8,10},{9,11},{10,... | collective-permute-start | bytes 1105928 | tf_op jit(solution)/shard_map/ppermute | solution.py:1122
  65.7 51.0 %collective-permute-start.14 = (bf16[384,384]{1,0:T(8,128)(2,1)S(1)}, bf16[384,384]{1,0:T(8,128)(2,1)S(1)}, u32[]{:S(2)}, u32[]{:S(2)}) collective-permute-start(bf16[384,384]{1,0:T(8,128)(2,1)S(1)} %slice.315), channel_id=1, source_target_pairs={{0,2},{1,3},{2,0},{3,1},{4,6},{5,7},{6,4},{7,5},{8,10},{9,11},{10,... | collective-permute-start | bytes 884744 | tf_op jit(solution)/shard_map/ppermute | solution.py:1122
  99.8 22.5 %collective-permute-start.12 = (bf16[864,384]{1,0:T(8,128)(2,1)S(1)}, bf16[864,384]{1,0:T(8,128)(2,1)S(1)}, u32[]{:S(2)}, u32[]{:S(2)}) collective-permute-start(bf16[864,384]{1,0:T(8,128)(2,1)S(1)} %collective-permute-done.10), channel_id=1, source_target_pairs={{0,16},{16,0},{1,17},{17,1},{2,18},{18,2},{3,19},{19,3},{4,20},{20... | collective-permute-start | bytes 1990664 | tf_op jit(solution)/shard_map/ppermute | solution.py:1135
  100.0 22.2 %collective-permute-start.13 = (bf16[480,384]{1,0:T(8,128)(2,1)S(1)}, bf16[480,384]{1,0:T(8,128)(2,1)S(1)}, u32[]{:S(2)}, u32[]{:S(2)}) collective-permute-start(bf16[480,384]{1,0:T(8,128)(2,1)S(1)} %collective-permute-done.11), channel_id=1, source_target_pairs={{0,16},{16,0},{1,17},{17,1},{2,18},{18,2},{3,19},{19,3},{4,20},{20... | collective-permute-start | bytes 1105928 | tf_op jit(solution)/shard_map/ppermute | solution.py:1135
  102.7 22.7 %collective-permute-start.19 = (bf16[256,768]{1,0:T(8,128)(2,1)S(1)}, bf16[256,768]{1,0:T(8,128)(2,1)S(1)}, u32[]{:S(2)}, u32[]{:S(2)}) collective-permute-start(bf16[256,768]{1,0:T(8,128)(2,1)S(1)} %get-tuple-element.254), channel_id=1, source_target_pairs={{8,0},{4,12},{13,5},{1,9},{10,2},{6,14},{15,7},{3,11},{24,16},{20,... | collective-permute-start | bytes 1179656 | tf_op jit(solution)/shard_map/ppermute | solution.py:1344
  125.5 19.3 %collective-permute-start.20 = (bf16[2,256,768]{2,1,0:T(8,128)(2,1)S(1)}, bf16[2,256,768]{2,1,0:T(8,128)(2,1)S(1)}, u32[]{:S(2)}, u32[]{:S(2)}) collective-permute-start(bf16[2,256,768]{2,1,0:T(8,128)(2,1)S(1)} %pad_maximum_fusion.6), channel_id=1, source_target_pairs={{0,4},{4,0},{8,12},{12,8},{1,5},{5,1},{9,13},{13,9},{2,6},{6,2},{1... | collective-permute-start | bytes 2359304 | tf_op jit(solution)/shard_map/ppermute | solution.py:1088
  125.6 15.7 %collective-permute-start.17 = (bf16[384,384]{1,0:T(8,128)(2,1)S(1)}, bf16[384,384]{1,0:T(8,128)(2,1)S(1)}, u32[]{:S(2)}, u32[]{:S(2)}) collective-permute-start(bf16[384,384]{1,0:T(8,128)(2,1)S(1)} %collective-permute-done.14), channel_id=1, source_target_pairs={{0,16},{16,0},{1,17},{17,1},{2,18},{18,2},{3,19},{19,3},{4,20},{20... | collective-permute-start | bytes 884744 | tf_op jit(solution)/shard_map/ppermute | solution.py:1135
  149.0 28.6 %collective-permute-start.22 = (bf16[384,768]{1,0:T(8,128)(2,1)S(1)}, bf16[384,768]{1,0:T(8,128)(2,1)S(1)}, u32[]{:S(2)}, u32[]{:S(2)}) collective-permute-start(bf16[384,768]{1,0:T(8,128)(2,1)S(1)} %get-tuple-element.177.one), channel_id=1, source_target_pairs={{0,1},{1,2},{2,3},{3,0},{4,5},{5,6},{6,7},{7,4},{8,9},{9,10},{10,1... | collective-permute-start | bytes 1769480 | tf_op jit(solution)/shard_map/ppermute | solution.py:1122
  173.2 27.7 %collective-permute-start.24 = (bf16[2,4,192,384]{3,2,1,0:T(8,128)(2,1)}, bf16[2,4,192,384]{3,2,1,0:T(8,128)(2,1)}, u32[]{:S(2)}, u32[]{:S(2)}) collective-permute-start(bf16[2,4,192,384]{3,2,1,0:T(8,128)(2,1)} %get-tuple-element.194), channel_id=1, source_target_pairs={{0,8},{4,12},{8,0},{12,4},{1,9},{5,13},{9,1},{13,5},{2,10},{6,14},... | collective-permute-start | bytes 3538952 | tf_op jit(solution)/shard_map/ppermute | solution.py:1088
  174.2 27.4 %collective-permute-start.25 = (bf16[2,4,192,384]{3,2,1,0:T(8,128)(2,1)}, bf16[2,4,192,384]{3,2,1,0:T(8,128)(2,1)}, u32[]{:S(2)}, u32[]{:S(2)}) collective-permute-start(bf16[2,4,192,384]{3,2,1,0:T(8,128)(2,1)} %get-tuple-element.195), channel_id=1, source_target_pairs={{0,16},{16,0},{1,17},{17,1},{2,18},{18,2},{3,19},{19,3},{4,20},{20... | collective-permute-start | bytes 3538952 | tf_op jit(solution)/shard_map/ppermute | solution.py:1135
  175.0 25.7 %collective-permute-start.26 = (bf16[384,768]{1,0:T(8,128)(2,1)S(1)}, bf16[384,768]{1,0:T(8,128)(2,1)S(1)}, u32[]{:S(2)}, u32[]{:S(2)}) collective-permute-start(bf16[384,768]{1,0:T(8,128)(2,1)S(1)} %get-tuple-element.177.one), channel_id=1, source_target_pairs={{0,3},{1,0},{2,1},{3,2},{4,7},{5,4},{6,5},{7,6},{8,11},{9,8},{10,9... | collective-permute-start | bytes 1769480 | tf_op jit(solution)/shard_map/ppermute | solution.py:1122
  177.6 44.0 %collective-permute-start.29 = (bf16[384,768]{1,0:T(8,128)(2,1)S(1)}, bf16[384,768]{1,0:T(8,128)(2,1)S(1)}, u32[]{:S(2)}, u32[]{:S(2)}) collective-permute-start(bf16[384,768]{1,0:T(8,128)(2,1)S(1)} %get-tuple-element.177.one), channel_id=1, source_target_pairs={{0,2},{1,3},{2,0},{3,1},{4,6},{5,7},{6,4},{7,5},{8,10},{9,11},{10,... | collective-permute-start | bytes 1769480 | tf_op jit(solution)/shard_map/ppermute | solution.py:1122
  203.3 18.2 %collective-permute-start.27 = (bf16[4,192,384]{2,1,0:T(8,128)(2,1)S(1)}, bf16[4,192,384]{2,1,0:T(8,128)(2,1)S(1)}, u32[]{:S(2)}, u32[]{:S(2)}) collective-permute-start(bf16[4,192,384]{2,1,0:T(8,128)(2,1)S(1)} %slice_bitcast_fusion.7), channel_id=1, source_target_pairs={{0,16},{16,0},{1,17},{17,1},{2,18},{18,2},{3,19},{19,3},{4,20},{20... | collective-permute-start | bytes 1769480 | tf_op jit(solution)/shard_map/ppermute | solution.py:1135
  236.2 22.8 %collective-permute-start.32 = (bf16[128,768]{1,0:T(8,128)(2,1)S(1)}, bf16[128,768]{1,0:T(8,128)(2,1)S(1)}, u32[]{:S(2)}, u32[]{:S(2)}) collective-permute-start(bf16[128,768]{1,0:T(8,128)(2,1)S(1)} %get-tuple-element.213), channel_id=1, source_target_pairs={{4,5},{1,0},{5,13},{9,1},{13,12},{8,9},{6,7},{3,2},{7,15},{11,3},{... | collective-permute-start | bytes 589832 | tf_op jit(solution)/shard_map/ppermute | solution.py:1407
  240.9 18.1 %collective-permute-start.31 = (bf16[384,768]{1,0:T(8,128)(2,1)S(1)}, bf16[384,768]{1,0:T(8,128)(2,1)S(1)}, u32[]{:S(2)}, u32[]{:S(2)}) collective-permute-start(bf16[384,768]{1,0:T(8,128)(2,1)S(1)} %add_convert_fusion.4), channel_id=1, source_target_pairs={{4,1},{1,4},{5,9},{9,5},{13,8},{8,13},{6,3},{3,6},{7,11},{11,7},{1... | collective-permute-start | bytes 1769480 | tf_op jit(solution)/shard_map/ppermute | solution.py:1406
  259.9 15.8 %collective-permute-start.37 = (bf16[2,2,4,200,384]{4,3,2,1,0:T(8,128)(2,1)}, bf16[2,2,4,200,384]{4,3,2,1,0:T(8,128)(2,1)}, u32[]{:S(2)}, u32[]{:S(2)}) collective-permute-start(bf16[2,2,4,200,384]{4,3,2,1,0:T(8,128)(2,1)} %get-tuple-element.227), channel_id=1, source_target_pairs={{0,4},{4,0},{8,12},{12,8},{1,5},{5,1},{9,13},{13,9},{2,6},{6,2},{1... | collective-permute-start | bytes 7372808 | tf_op jit(solution)/shard_map/ppermute | solution.py:1088
  278.2 29.5 %collective-permute-start.39 = (bf16[2,4,200,384]{3,2,1,0:T(8,128)(2,1)S(1)}, bf16[2,4,200,384]{3,2,1,0:T(8,128)(2,1)S(1)}, u32[]{:S(2)}, u32[]{:S(2)}) collective-permute-start(bf16[2,4,200,384]{3,2,1,0:T(8,128)(2,1)S(1)} %slice_bitcast_fusion), channel_id=1, source_target_pairs={{0,16},{16,0},{1,17},{17,1},{2,18},{18,2},{3,19},{19,3},{4,20},{20... | collective-permute-start | bytes 3686408 | tf_op jit(solution)/shard_map/ppermute | solution.py:1135
  279.1 27.8 %collective-permute-start.41 = (bf16[384,384]{1,0:T(8,128)(2,1)S(1)}, bf16[384,384]{1,0:T(8,128)(2,1)S(1)}, u32[]{:S(2)}, u32[]{:S(2)}) collective-permute-start(bf16[384,384]{1,0:T(8,128)(2,1)S(1)} %copy-done.63), channel_id=1, source_target_pairs={{0,2},{1,3},{2,0},{3,1},{4,6},{5,7},{6,4},{7,5},{8,10},{9,11},{10,... | collective-permute-start | bytes 884744 | tf_op jit(solution)/shard_map/ppermute | solution.py:1147
  279.5 27.3 %collective-permute-start.40 = (bf16[384,768]{1,0:T(8,128)(2,1)S(1)}, bf16[384,768]{1,0:T(8,128)(2,1)S(1)}, u32[]{:S(2)}, u32[]{:S(2)}) collective-permute-start(bf16[384,768]{1,0:T(8,128)(2,1)S(1)} %pad_maximum_fusion.12.one), channel_id=1, source_target_pairs={{0,1},{1,2},{2,3},{3,0},{4,5},{5,6},{6,7},{7,4},{8,9},{9,10},{10,1... | collective-permute-start | bytes 1769480 | tf_op jit(solution)/shard_map/ppermute | solution.py:1122
  280.6 30.8 %collective-permute-start.45 = (bf16[4,128,768]{2,1,0:T(8,128)(2,1)}, bf16[4,128,768]{2,1,0:T(8,128)(2,1)}, u32[]{:S(2)}, u32[]{:S(2)}) collective-permute-start(bf16[4,128,768]{2,1,0:T(8,128)(2,1)} %pad_maximum_fusion.7), channel_id=1, source_target_pairs={{0,4},{4,0},{8,12},{12,8},{1,5},{5,1},{9,13},{13,9},{2,6},{6,2},{1... | collective-permute-start | bytes 2359304 | tf_op jit(solution)/shard_map/ppermute | solution.py:1088
  282.7 29.4 %collective-permute-start.46 = (bf16[2,256,768]{2,1,0:T(8,128)(2,1)}, bf16[2,256,768]{2,1,0:T(8,128)(2,1)}, u32[]{:S(2)}, u32[]{:S(2)}) collective-permute-start(bf16[2,256,768]{2,1,0:T(8,128)(2,1)} %pad_maximum_fusion.8), channel_id=1, source_target_pairs={{0,12},{4,8},{8,4},{12,0},{1,13},{5,9},{9,5},{13,1},{2,14},{6,10},... | collective-permute-start | bytes 2359304 | tf_op jit(solution)/shard_map/ppermute | solution.py:1466
  309.0 22.2 %collective-permute-start.42 = (bf16[4,200,384]{2,1,0:T(8,128)(2,1)}, bf16[4,200,384]{2,1,0:T(8,128)(2,1)}, u32[]{:S(2)}, u32[]{:S(2)}) collective-permute-start(bf16[4,200,384]{2,1,0:T(8,128)(2,1)} %slice_bitcast_fusion.3), channel_id=1, source_target_pairs={{0,8},{4,12},{8,0},{12,4},{1,9},{5,13},{9,1},{13,5},{2,10},{6,14},... | collective-permute-start | bytes 1843208 | tf_op jit(solution)/shard_map/ppermute | solution.py:1088
  309.9 38.1 %collective-permute-start.47 = (bf16[384,768]{1,0:T(8,128)(2,1)S(1)}, bf16[384,768]{1,0:T(8,128)(2,1)}, u32[]{:S(2)}, u32[]{:S(2)}) collective-permute-start(bf16[384,768]{1,0:T(8,128)(2,1)S(1)} %pad_maximum_fusion.12.one), channel_id=1, source_target_pairs={{0,2},{1,3},{2,0},{3,1},{4,6},{5,7},{6,4},{7,5},{8,10},{9,11},{10,... | collective-permute-start | bytes 1769480 | tf_op jit(solution)/shard_map/ppermute | solution.py:1122
  311.4 19.8 %collective-permute-start.44 = (bf16[384,384]{1,0:T(8,128)(2,1)S(1)}, bf16[384,384]{1,0:T(8,128)(2,1)S(1)}, u32[]{:S(2)}, u32[]{:S(2)}) collective-permute-start(bf16[384,384]{1,0:T(8,128)(2,1)S(1)} %fusion.12.mine), channel_id=1, source_target_pairs={{0,8},{4,12},{8,0},{12,4},{1,9},{5,13},{9,1},{13,5},{2,10},{6,14},... | collective-permute-start | bytes 884744 | tf_op jit(solution)/shard_map/ppermute | solution.py:1088
  350.0 21.6 %collective-permute-start.52 = (bf16[4,128,768]{2,1,0:T(8,128)(2,1)S(1)}, bf16[4,128,768]{2,1,0:T(8,128)(2,1)S(1)}, u32[]{:S(2)}, u32[]{:S(2)}) collective-permute-start(bf16[4,128,768]{2,1,0:T(8,128)(2,1)S(1)} %pad_maximum_fusion.9), channel_id=1, source_target_pairs={{0,4},{4,0},{8,12},{12,8},{1,5},{5,1},{9,13},{13,9},{2,6},{6,2},{1... | collective-permute-start | bytes 2359304 | tf_op jit(solution)/shard_map/ppermute | solution.py:1088
  (99 other events, 647.1 us)
